TPU v7x, 256 devices: a whole 4x4x8 slice. The times are simulated.
256 devices in a mesh: dom: 32 (over z, x), head: 8 (over y, core).
Axes of the slice: x: 4, y: 4, z: 8, core: 2. Of those that a mesh axis runs over, the one named last changes fastest.
Arguments:
- node_feats: float32 [32768, 512], P('dom')
- order: int32 [32768], P('dom'), may hold values from 0 to 32767, as said below
- node_count: int32 [256], replicated, may hold values from 32 to 128
- local_blocks: int32 [256, 3], P('dom'), may hold values from 0 to 255, as said below
- exp_blocks: int32 [256, 6], P('dom'), may hold values from 0 to 255, as said below
- virt_blocks: int32 [256], P('dom'), may hold values from 0 to 3
- virt_feats: float32 [512, 512], replicated, may hold values from -6 to 6
- w_query: float32 [512, 512], P(None, 'head'), may hold values from -0.25 to 0.25
- w_key: float32 [512, 512], P(None, 'head'), may hold values from -0.25 to 0.25
- w_value: float32 [512, 512], P(None, 'head'), may hold values from -0.25 to 0.25
- w_out: float32 [512, 512], P(None, 'head'), may hold values from -2 to 2
- w_up: float32 [512, 1024], P(None, 'head'), may hold values from -0.25 to 0.25
- w_down: float32 [1024, 512], P('head'), may hold values from -0.1875 to 0.1875
Outputs:
- refined: float32 [32768, 512], P('dom', 'head')
Inputs may be any that keep to these rules, and one draw needn't show every extreme that they name: `order`: each device's 8 * 128 entries are a permutation of that device's own node numbers (the rows it holds). `local_blocks`: every entry lies within 2 clusters of its own cluster; column 1 is exactly 2 away unless that leaves the grid, where it is clipped to the end. `exp_blocks`: call id // 8 the owner of a cluster id. Among the 48 entries of one device's clusters, at most 3 have any one owner, and for every device some owner has exactly 3.
All inputs are finite; a program needn't handle non-finite values.
Results may differ from a plain program's by a relative error of at most 0.0003.
Values sent between devices are 32-bit elements; how exact they have to be, the bound alone decides.
No kernel may reach another device: no remote copies, remote signals or barrier semaphores. Data moves between devices by JAX's collectives and lax.ppermute only.
A program may use at most 128 MiB of HBM per device.

v0:
```python
import math

import jax
import jax.numpy as jnp
from jax import lax
from jax.experimental import pallas as pl
from jax.experimental.pallas import tpu as pltpu
from jax.sharding import Mesh, PartitionSpec as P

D = 512
HD = 64
FF = 1024
CL = 128
CD = 8
NE = 6
NL = 3
CAP = 3
NZ, NX, NY, NC = 8, 4, 4, 2
PR = CL // (NY * NC)
EK = NE * CL
LK = (NL + 1) * CL
NEG = -1e30
VMEM_BYTES = 67043328
BF = jnp.bfloat16
F32 = jnp.float32
NT = (((1,), (1,)), ((), ()))
NN = (((1,), (0,)), ((), ()))

GROUPS = ((0, 1, 7, 2, 6), (3, 5, 4))


def split2(v):
    hi = v.astype(BF)
    return hi, (v - hi.astype(F32)).astype(BF)


def mm(a, b, dims):
    return lax.dot_general(a, b, dims, preferred_element_type=F32)


def dot3(ah, al, bh, bl, dims):
    return mm(ah, bh, dims) + (mm(ah, bl, dims) + mm(al, bh, dims))


def vspec():
    return pl.BlockSpec(memory_space=pltpu.VMEM)


def hspec():
    return pl.BlockSpec(memory_space=pltpu.HBM)


def sspec():
    return pl.BlockSpec(memory_space=pltpu.SMEM)


def params(mb):
    return pltpu.CompilerParams(vmem_limit_bytes=mb << 20)


def cost(flops, bytes_accessed, transcendentals=0):
    return pl.CostEstimate(flops=flops, bytes_accessed=bytes_accessed, transcendentals=transcendentals)


def sds(*shape, dtype=F32):
    return jax.ShapeDtypeStruct(shape, dtype)


def columns(row):
    return jnp.broadcast_to(row, (CL, CL)).T


def one_hot(cols):
    lanes = lax.broadcasted_iota(jnp.int32, cols.shape, 1).astype(F32)
    parts = [jnp.where(cols == lanes + float(j * CL), 1.0, 0.0).astype(BF) for j in range(CD)]
    return jnp.concatenate(parts, 1)


def first_kernel(pos, order_hbm, nodes_hbm, piece_out, edge_out, order_ref, nodes, sems):
    base, head, c = pos[0], pos[1], pos[2]
    step = 2 * CL
    parts = CD * CL // step
    fetch = [pltpu.make_async_copy(order_hbm, order_ref, sems.at[0])] + [
        pltpu.make_async_copy(nodes_hbm.at[i * step:(i + 1) * step, :], nodes.at[i * step:(i + 1) * step, :],
                              sems.at[i + 1]) for i in range(parts)]
    for copy in fetch:
        copy.start()
    fetch[0].wait()
    order = (order_ref[...] - base).astype(F32)
    mine = pltpu.roll(order, lax.rem(CL - head * PR, CL), 1)
    col = jnp.concatenate([mine] + [jnp.zeros((CL - CD, CL), F32)], 0).T
    pieces = [jnp.broadcast_to(col[:PR, k:k + 1], (PR, CL)) for k in range(CD)]
    edge = jnp.where(head < NY, CD - NC + c, c)
    edge_row = (order_ref[pl.ds(edge, 1), :] - base).astype(F32)
    pick = one_hot(jnp.concatenate(pieces + [columns(edge_row)], 0))
    rows = jnp.zeros((2 * CL, D), F32)
    for i in range(parts):
        fetch[i + 1].wait()
        hi, lo = split2(nodes[i * step:(i + 1) * step, :])
        some = pick[:, i * step:(i + 1) * step]
        rows = rows + (mm(some, hi, NN) + mm(some, lo, NN))
    piece_out[...] = rows[:CL]
    edge_out[...] = rows[CL:]


def first_call(pos, order, nodes):
    return pl.pallas_call(
        first_kernel,
        out_shape=[sds(CL, D), sds(CL, D)],
        in_specs=[sspec(), hspec(), hspec()],
        out_specs=[vspec()] * 2,
        scratch_shapes=[pltpu.VMEM((CD, CL), jnp.int32), pltpu.VMEM((CD * CL, D), F32),
                        pltpu.SemaphoreType.DMA((5,))],
        compiler_params=params(60),
        cost_estimate=cost(10**9, 3 << 20),
        name="first",
    )(pos, order, nodes)


def index_kernel(pos, exp_ref, table, row, seen, starts, widths):
    z, x = pos[0], pos[1]
    start = 0
    for group in GROUPS:
        for p, s in enumerate(group):
            starts[s] = start + p * CAP
            widths[s] = len(group) * CAP
        start += NX * len(group) * CAP

    def clear(i, carry):
        table[i] = 0
        seen[lax.bitwise_and(i, NZ * NX - 1)] = 0
        return carry

    lax.fori_loop(0, NX * NZ * CAP, clear, 0)

    def place(i, carry):
        for e in range(NE):
            block = exp_ref[i, e]
            owner = lax.shift_right_logical(block, 3)
            rank = seen[owner]
            seen[owner] = rank + 1
            oz = lax.shift_right_logical(owner, 2)
            back = lax.bitwise_and(x - lax.bitwise_and(owner, NX - 1), NX - 1)
            table[back * (NZ * CAP) + oz * CAP + rank] = lax.bitwise_and(block, CD - 1)
            off = lax.bitwise_and(oz - z, NZ - 1)
            row[i * NE + e] = (starts[off] + back * widths[off] + rank) * PR
        return carry

    lax.fori_loop(0, CD, place, 0)


def index_call(pos, exp_blocks):
    return pl.pallas_call(
        index_kernel,
        out_shape=[sds(NX * NZ * CAP, dtype=jnp.int32), sds(CD * NE, dtype=jnp.int32)],
        in_specs=[sspec()] * 2,
        out_specs=[sspec()] * 2,
        scratch_shapes=[pltpu.SMEM((NZ * NX,), jnp.int32), pltpu.SMEM((NZ,), jnp.int32), pltpu.SMEM((NZ,), jnp.int32)],
        compiler_params=params(2),
        cost_estimate=cost(1000, 4096),
        name="index",
    )(pos, exp_blocks)


def pack_kernel(q, k, v, o, up, down, att, ffw, sems):
    pairs = [(w, att.at[i * HD:(i + 1) * HD, :]) for i, w in enumerate((q, k, v, o))]
    pairs.append((down, ffw.at[:CL, :]))
    pairs += [(up.at[j * CL:(j + 1) * CL, :], ffw.at[CL:, j * CL:(j + 1) * CL]) for j in range(4)]
    copies = [pltpu.make_async_copy(src, dst, sems.at[i]) for i, (src, dst) in enumerate(pairs)]
    for copy in copies:
        copy.start()
    for copy in copies:
        copy.wait()


def pack_call(*w):
    return pl.pallas_call(
        pack_kernel,
        out_shape=[sds(2 * CL, D), sds(2 * CL, D)],
        in_specs=[hspec()] * 6,
        out_specs=[vspec()] * 2,
        scratch_shapes=[pltpu.SemaphoreType.DMA((9,))],
        compiler_params=params(60),
        cost_estimate=cost(0, 2 << 20),
        name="pack",
    )(*w)


def near_kernel(pos, local_ref, virt_ref, count_ref, order_ref, nodes_ref, e_in, e_other, virtual_ref, *rest):
    w = rest[:8]
    x_out, q_out, v_out, o_out, state, kh, kl = rest[8:]
    base, head, c, y = pos[0], pos[1], pos[2], pos[3]
    first = lax.shift_right_logical(base, 7)

    def order_row(r):
        return columns((order_ref[pl.ds(r, 1), :] - base).astype(F32))

    rel = [local_ref[head, j] - first for j in range(NL)]
    rows = [order_row(jnp.clip(r, 0, CD - 1)) for r in rel] + [order_row(head)]
    pick = one_hot(jnp.concatenate(rows, 0))
    nodes = nodes_ref[...]
    hi, lo = split2(nodes)
    got = mm(pick, hi, NN) + mm(pick, lo, NN)
    last = (nodes - hi.astype(F32) - lo.astype(F32)).astype(BF)
    x = got[NL * CL:] + mm(pick[NL * CL:], last, NN)
    x_out[...] = x
    lane = lax.broadcasted_iota(jnp.int32, (1, CL), 1)
    bias = []
    for j in range(NL):
        r = rel[j]
        at = jnp.where(r < 0, r + NC, r - CD)
        edge = jnp.where(at == c, e_in[...], e_other[...])
        keys = jnp.where((r >= 0) & (r < CD), got[j * CL:(j + 1) * CL], edge)
        kh[j * CL:(j + 1) * CL, :], kl[j * CL:(j + 1) * CL, :] = split2(keys)
        bias.append(jnp.where(lane < count_ref[local_ref[head, j]], 0.0, NEG))
    vat = pl.multiple_of(virt_ref[head] * CL, CL)
    kh[NL * CL:, :], kl[NL * CL:, :] = split2(virtual_ref[pl.ds(vat, CL), :])
    bias = jnp.concatenate(bias + [jnp.zeros((1, CL), F32)], 1)

    lanes = lax.broadcasted_iota(jnp.int32, (CL, 2 * HD), 1)
    lowq = lanes < HD
    xh, xl = split2(x)
    for dy in range(NY):
        a, b = w[2 * dy][...], w[2 * dy + 1][...]
        at = lax.rem(y - dy + NY, NY)
        left = jnp.where(c == 0, a, b)
        right = jnp.where(c == 0, b, a)
        wq, wk, wv, wo = (
            split2(jnp.concatenate([left[i * HD:(i + 1) * HD], right[i * HD:(i + 1) * HD]], 0))
            for i in range(4))
        q = dot3(xh, xl, *wq, NT) * (1.0 / math.sqrt(HD))
        both = jnp.concatenate([jnp.where(lowq, q, 0.0), jnp.where(lowq, 0.0, q)], 0)
        q_out[0, at], q_out[1, at] = split2(dot3(*split2(both), *wk, NN))
        v_out[0, at], v_out[1, at] = wv
        rows = pl.ds(pl.multiple_of(at * CL, CL), CL)
        o_out[0, rows, :], o_out[1, rows, :] = wo

    def body(p, carry):
        s = dot3(q_out[0, p], q_out[1, p], kh[...], kl[...], NT) + bias
        m = jnp.max(s, axis=1, keepdims=True)
        e = jnp.exp(s - m)
        l = jnp.sum(e, axis=1, keepdims=True)
        a = dot3(*split2(e), kh[...], kl[...], NN)
        o = dot3(*split2(a), v_out[0, p], v_out[1, p], NT)
        state[p, :CL, :] = jnp.where(lowq, o[:CL], jnp.where(lanes < HD + HD // 2, m[:CL], l[:CL]))
        state[p, CL:, :] = jnp.where(lowq, jnp.where(lanes < HD // 2, m[CL:], l[CL:]), o[CL:])
        return carry

    lax.fori_loop(0, NY, body, 0)


def near_call(scalars, arrays, weights):
    shapes = [
        sds(CL, D), sds(2, NY, 2 * CL, D, dtype=BF), sds(2, NY, 2 * HD, D, dtype=BF),
        sds(2, D, D, dtype=BF), sds(NY, 2 * CL, 2 * HD),
    ]
    return pl.pallas_call(
        near_kernel,
        out_shape=shapes,
        in_specs=[sspec()] * len(scalars) + [vspec()] * len(arrays)
        + [vspec()] * len(weights),
        out_specs=[vspec()] * len(shapes),
        scratch_shapes=[pltpu.VMEM((LK, D), BF), pltpu.VMEM((LK, D), BF)],
        compiler_params=params(60),
        cost_estimate=cost(6 * 10**9, 16 << 20, 1 << 20),
        name="near",
    )(*scalars, *arrays, *weights)


def prep_kernel(*refs):
    w = refs[:8]
    u_out, d_out = refs[8:]
    for i in range(8):
        rows = slice(i * CL, (i + 1) * CL)
        d_out[0, rows, :], d_out[1, rows, :] = split2(w[i][:CL, :])
        hi, lo = split2(w[i][CL:, :])
        for j in range(4):
            cols = slice(j * CL, (j + 1) * CL)
            u_out[0, cols, rows] = hi[:, cols]
            u_out[1, cols, rows] = lo[:, cols]


def prep_call(weights):
    return pl.pallas_call(
        prep_kernel,
        out_shape=[sds(2, D, FF, dtype=BF), sds(2, FF, D, dtype=BF)],
        in_specs=[vspec()] * len(weights),
        out_specs=[vspec()] * 2,
        compiler_params=params(60),
        cost_estimate=cost(10**7, 8 << 20),
        name="prep",
    )(*weights)


def far_kernel(pos, exp_ref, count_ref, xe_ref, q_hbm, s_hbm, v_hbm, x_hbm, o_hbm, u_hbm, d_hbm,
               out_ref, kh, kl, att, q, st, v, x, wo, u, d, sems):
    copies = [pltpu.make_async_copy(src, dst, sems.at[i]) for i, (src, dst) in enumerate(zip(
        (q_hbm, s_hbm, v_hbm, x_hbm, o_hbm, u_hbm, d_hbm), (q, st, v, x, wo, u, d)))]
    for copy in copies[:3]:
        copy.start()
    head = pos[1]
    hi, lo = split2(xe_ref[...])
    kh[...] = hi
    kl[...] = lo
    lowq = lax.broadcasted_iota(jnp.int32, (CL, 2 * HD), 1) < HD
    n = lax.broadcasted_iota(jnp.int32, (1, EK), 1)

    def steps(v, width, count):
        return sum(jnp.where(v >= width * k, 1, 0) for k in range(1, count))

    piece = steps(n, NE * PR, CD)
    r = n - piece * (NE * PR)
    entry = steps(r, PR, NE)
    slot = piece * PR + r - entry * PR
    bias = jnp.zeros((1, EK), F32)
    for e in range(NE):
        bad = (entry == e) & (slot >= count_ref[exp_ref[head, e]])
        bias = jnp.where(bad, NEG, bias)

    def scores(p):
        return dot3(q[0, p], q[1, p], kh[...], kl[...], NT) + bias

    def attend(p, s):
        m_near = jnp.concatenate([st[p, :CL, HD:HD + 1], st[p, CL:, :1]], 0)
        half = HD // 2
        l_near = jnp.concatenate([st[p, :CL, HD + half:HD + half + 1], st[p, CL:, half:half + 1]], 0)
        m = jnp.maximum(m_near, jnp.max(s, axis=1, keepdims=True))
        e = jnp.exp(s - m)
        scale = jnp.exp(m_near - m)
        total = jnp.sum(e, axis=1, keepdims=True) + l_near * scale
        a = dot3(*split2(e), kh[...], kl[...], NN)
        o = (dot3(*split2(a), v[0, p], v[1, p], NT) + st[p] * scale) / total
        att[p] = jnp.where(lowq, o[:CL], o[CL:])

    for copy in copies[:3]:
        copy.wait()
    for copy in copies[3:]:
        copy.start()

    def body(i, carry):
        one, two = scores(2 * i), scores(2 * i + 1)
        attend(2 * i, one)
        attend(2 * i + 1, two)
        return carry

    lax.fori_loop(0, NY // 2, body, 0)
    ah, al = split2(jnp.concatenate([att[p] for p in range(NY)], 1))
    for copy in copies[3:]:
        copy.wait()
    r = x[...] + dot3(ah, al, wo[0], wo[1], NT)
    mean = jnp.sum(r, axis=1, keepdims=True) * (1.0 / D)
    square = jnp.sum(r * r, axis=1, keepdims=True) * (1.0 / D)
    normed = (r - mean) * lax.rsqrt(square - mean * mean + 1e-05)
    hid = dot3(*split2(normed), u[0], u[1], NN)
    act = 0.5 * hid * (1.0 + lax.erf(hid * math.sqrt(0.5)))
    y = r + dot3(*split2(act), d[0], d[1], NN)
    out_ref[...] = y.T


def far_call(scalars, arrays):
    return pl.pallas_call(
        far_kernel,
        out_shape=sds(D, CL),
        in_specs=[sspec()] * len(scalars) + [vspec()] + [hspec()] * (len(arrays) - 1),
        out_specs=vspec(),
        scratch_shapes=[pltpu.VMEM((EK, D), BF), pltpu.VMEM((EK, D), BF), pltpu.VMEM((NY, CL, 2 * HD), F32)]
        + [pltpu.VMEM(a.shape, a.dtype) for a in arrays[1:]] + [pltpu.SemaphoreType.DMA((len(arrays) - 1,))],
        compiler_params=params(60),
        cost_estimate=cost(6 * 10**9, 16 << 20, 1 << 20),
        name="far",
    )(*scalars, *arrays)


def place_kernel(pos, r_ref, order_ref, out_ref):
    full = jnp.concatenate([r_ref[i * HD:(i + 1) * HD, :] for i in range(CD)], 1)
    order = jnp.concatenate([order_ref[i:i + 1, :] for i in range(CD)], 1) - pos[0]
    hi = full.astype(BF)
    rest = full - hi.astype(F32)
    mid = rest.astype(BF)
    low = (rest - mid.astype(F32)).astype(BF)
    parts = jnp.concatenate([hi, mid, low], 0)
    step = 256
    for j in range(CD * CL // step):
        nodes = lax.broadcasted_iota(jnp.int32, (step, CD * CL), 0) + j * step
        pick = jnp.where(nodes == order, 1.0, 0.0).astype(BF)
        t = mm(parts, pick, NT)
        out_ref[:, j * step:(j + 1) * step] = t[:HD] + (t[HD:2 * HD] + t[2 * HD:])


def place_call(pos, received, order):
    return pl.pallas_call(
        place_kernel,
        out_shape=sds(HD, CD * CL),
        in_specs=[sspec(), vspec(), vspec()],
        out_specs=vspec(),
        compiler_params=params(12),
        cost_estimate=cost(4 * 10**8, 1 << 20),
        name="place",
    )(pos, received, order)


def pick_kernel(group, pos, *refs):
    tables, srcs, outs, sem = refs[:NX], refs[NX:-NX - 1], refs[-NX - 1:-1], refs[-1]
    z = pos[0]
    parts, at = [], 0
    for s in group:
        size = 2 if s == NZ // 2 else 1
        parts.append(srcs[at:at + size])
        at += size

    def send(src, at, out, to):
        pltpu.make_async_copy(src.at[pl.ds(pl.multiple_of(at, PR), PR), :], out.at[to:to + PR, :], sem).start()

    for k, out in enumerate(outs):
        for i, s in enumerate(group):
            src = parts[i]
            for j in range(CAP):
                b = tables[k][(k * NZ + lax.bitwise_and(z + s, NZ - 1)) * CAP + j]
                to = (i * CAP + j) * PR
                if len(src) == 1:
                    send(src[0], b * PR, out, to)
                else:
                    at = lax.bitwise_and(b, CD // 2 - 1) * PR

                    @pl.when(b < CD // 2)
                    def _(at=at, to=to, src=src, out=out):
                        send(src[0], at, out, to)

                    @pl.when(b >= CD // 2)
                    def _(at=at, to=to, src=src, out=out):
                        send(src[1], at, out, to)

    for out in outs:
        pltpu.make_async_copy(out, out, sem).wait()


def pick_call(group, pos, tables, srcs):
    rows = len(group) * CAP * PR
    return pl.pallas_call(
        lambda *refs: pick_kernel(group, *refs),
        out_shape=[sds(rows, D)] * NX,
        in_specs=[sspec()] * (1 + NX) + [vspec()] * len(srcs),
        out_specs=[vspec()] * NX,
        scratch_shapes=[pltpu.SemaphoreType.DMA],
        compiler_params=params(8),
        cost_estimate=cost(0, NX * rows * D * 8),
        name="pick",
    )(pos, *tables, *srcs)


def send_kernel(row, *refs):
    srcs, out, held = refs[:-2], refs[-2], refs[-1]
    at = 0
    for src in srcs:
        held[at:at + src.shape[0], :] = src[...]
        at += src.shape[0]
    for i in range(CD * NE):
        out[i * PR:(i + 1) * PR, :] = held[pl.ds(pl.multiple_of(row[i], PR), PR), :]


def send_call(row, srcs):
    return pl.pallas_call(
        send_kernel,
        out_shape=sds(CD * NE * PR, D),
        in_specs=[sspec()] + [vspec()] * len(srcs),
        out_specs=vspec(),
        scratch_shapes=[pltpu.VMEM((NZ * NX * CAP * PR, D), F32)],
        compiler_params=params(12),
        cost_estimate=cost(0, 6 << 20),
        name="send",
    )(row, *srcs)


def ring(size, step):
    return [(i, (i + step) % size) for i in range(size)]


SWAP = [(0, 1), (1, 0)]


def shards(node_feats, order, node_count, local_blocks, exp_blocks, virt_blocks, virt_feats,
           w_query, w_key, w_value, w_out, w_up, w_down):
    z, x, y, c = (lax.axis_index(a) for a in ("z", "x", "y", "c"))
    head = y * NC + c
    pos = jnp.stack([(z * NX + x) * (CD * CL), head, c, y]).astype(jnp.int32)
    zx = jnp.stack([z, x]).astype(jnp.int32)
    order = order.reshape(CD, CL)

    piece, edge = first_call(pos, order, node_feats)

    half = CL // 2
    tie = lax.optimization_barrier

    def both_z(a, b):
        return lax.ppermute(a, "z", ring(NZ, 1)), lax.ppermute(b, "z", ring(NZ, -1))

    def both_y(a):
        return lax.ppermute(a, "y", ring(NY, 1)), lax.ppermute(a, "y", ring(NY, -1))

    def swap(*arrays):
        return [lax.ppermute(t, "c", SWAP) for t in arrays]

    up, down = both_z(piece, piece)
    table, row = index_call(zx, exp_blocks)
    tables = [table] + [lax.ppermute(table, "x", ring(NX, -k)) for k in range(1, NX)]
    wa, wb = pack_call(w_query.T, w_key.T, w_value.T, w_out.T, w_up, w_down)
    held = {0: (piece,), 7: (up,), 1: (down,)}
    wa, wb, *tables = tie((wa, wb, *tables))
    a_up, a_down = both_y(wa)
    up, down, edge, *tables = tie((up, down, edge, *tables))

    e_in = lax.ppermute(edge, ("z", "x", "y", "c"), [
        (i * CD + h, (i + s) * CD + h)
        for s, hs in ((1, (0, 1)), (-1, (6, 7)))
        for i in range(NZ * NX) if 0 <= i + s < NZ * NX for h in hs])
    up, down = both_z(up, down)
    held[6], held[2] = (up,), (down,)
    up, down, a_up, a_down, wa, wb, e_in, *tables = tie((up, down, a_up, a_down, wa, wb, e_in, *tables))

    def exchange(group):
        blocks = pick_call(group, zx, tables, [t for s in group for t in held[s]])
        return [blocks[0]] + [lax.ppermute(blocks[k], "x", ring(NX, k)) for k in (1, 2, 3)]

    near_x = exchange(GROUPS[0])
    up, down = both_z(up, down)
    held[5], held[3] = (up,), (down,)
    first4, second4 = both_z(up[:half], down[half:])
    first4, second4, e_in, wa, wb, a_up, a_down = tie((first4, second4, e_in, wa, wb, a_up, a_down))
    held[4] = (first4, second4)
    b_up, b_down = both_y(wb)
    e_other, wa_o, wb_o, a_up_o, a_down_o = swap(e_in, wa, wb, a_up, a_down)
    a_up, first4, second4, *near_x = tie((a_up, first4, second4, *near_x))
    held[4] = (first4, second4)
    far_x = exchange(GROUPS[1])

    a_far = lax.ppermute(a_up, "y", ring(NY, 1))
    b_far = lax.ppermute(b_down, "y", ring(NY, -1))
    e_other, wa_o, wb_o, a_up_o, a_down_o, *far_x = tie((e_other, wa_o, wb_o, a_up_o, a_down_o, *far_x))

    sending = send_call(row, near_x + far_x)
    xe = lax.all_to_all(sending, ("y", "c"), 0, 0, tiled=True)
    _, a_far_s, b_far_s, b_up_s, b_down_s = tie((row, a_far, b_far, b_up, b_down))
    a_far_o, b_up_o, b_down_o, b_far_o = swap(a_far_s, b_up_s, b_down_s, b_far_s)
    wa = [wa, wa_o, a_up, a_up_o, a_far, a_far_o, a_down, a_down_o]
    wb = [wb, wb_o, b_up, b_up_o, b_far, b_far_o, b_down, b_down_o]

    x_own, q, wv, wo, state = near_call(
        (pos, local_blocks, virt_blocks, node_count), (order, node_feats, e_in, e_other, virt_feats), wa)
    wu, wd = prep_call(wb)
    result = far_call((pos, exp_blocks, node_count), (xe, q, state, wv, x_own, wo, wu, wd))
    received = lax.all_to_all(result, ("y", "c"), 0, 0, tiled=True)
    return place_call(pos, received, order).T


def solution(mesh):
    grid = Mesh(mesh.devices.reshape(NZ, NX, NY, NC), ("z", "x", "y", "c"))
    dom, head = ("z", "x"), ("y", "c")
    return jax.shard_map(
        shards,
        mesh=grid,
        in_specs=(P(dom, None), P(dom), P(), P(dom, None), P(dom, None), P(dom), P(),
                  P(None, head), P(None, head), P(None, head), P(None, head), P(None, head),
                  P(head, None)),
        out_specs=P(dom, head),
        check_vma=False,
    )
```

profile of v0, /device:TPU:1, one launch (start us, length us, event | category | flops | bytes accessed | tf_op | source)
XLA Modules:
  0.0 164.0 jit_solution(11284565206017283496)
XLA Ops:
  0.7 3.5 %first.1 = (f32[128,512]{1,0:T(8,128)}, f32[128,512]{1,0:T(8,128)}) custom-call(s32[4]{0:T(128)} %pad_add_fusion.pos, s32[8,128]{1,0:T(8,128)} %bitcast.17, f32[1024,512]{1,0:T(8,128)} %nodes_ref.1), custom_call_target="tpu_custom_call" | custom-call | flops 1000000000 | bytes 3145728 | tf_op jit(solution)/shard_map/first/pallas_call | solution.py:107
  4.2 2.5 %collective-permute-start = (f32[128,512]{1,0:T(8,128)}, f32[128,512]{1,0:T(8,128)S(1)}, u32[]{:S(2)}, u32[]{:S(2)}) collective-permute-start(f32[128,512]{1,0:T(8,128)} %get-tuple-element.78.refs_5_), channel_id=1, source_target_pairs={{0,32},{32,64},{64,96},{96,128},{128,160},{160,192},{192,224},{224... | collective-permute-start | bytes 786440 | tf_op jit(solution)/shard_map/ppermute | solution.py:495
  6.7 4.0 %collective-permute-start.1 = (f32[128,512]{1,0:T(8,128)}, f32[128,512]{1,0:T(8,128)S(1)}, u32[]{:S(2)}, u32[]{:S(2)}) collective-permute-start(f32[128,512]{1,0:T(8,128)} %get-tuple-element.78.refs_5_), channel_id=1, source_target_pairs={{0,224},{32,0},{64,32},{96,64},{128,96},{160,128},{192,160},{224,1... | collective-permute-start | bytes 786440 | tf_op jit(solution)/shard_map/ppermute | solution.py:495
  10.8 2.3 %index.1 = (s32[96]{0:T(128)S(1)}, s32[48]{0:T(128)S(1)}) custom-call(s32[2]{0:T(128)S(1)} %pad_add_fusion.1.pos.refs_0_, s32[8,6]{1,0:T(8,128)S(1)} %copy-done.1), custom_call_target="tpu_custom_call" | custom-call | flops 1000 | bytes 4096 | tf_op jit(solution)/shard_map/index/pallas_call | solution.py:153
  13.1 2.6 %collective-permute-start.2 = (s32[96]{0:T(128)S(1)}, s32[96]{0:T(128)S(1)}, u32[]{:S(2)}, u32[]{:S(2)}) collective-permute-start(s32[96]{0:T(128)S(1)} %get-tuple-element.106.refs_1_), channel_id=1, source_target_pairs={{0,24},{8,0},{16,8},{24,16},{1,25},{9,1},{17,9},{25,17},{2,26},{10... | collective-permute-start | bytes 1160 | tf_op jit(solution)/shard_map/ppermute | solution.py:505
  16.8 2.3 %pack.1 = (f32[256,512]{1,0:T(8,128)}, f32[256,512]{1,0:T(8,128)}) custom-call(f32[64,512]{1,0:T(8,128)} %bitcast.22, f32[64,512]{1,0:T(8,128)} %bitcast.23, f32[64,512]{1,0:T(8,128)} %bitcast.24, f32[64,512]{1,0:T(8,128)} %bitcast.25, f32[512,128]{1,0:T(8,128)} %up.1, f32[128,512]{1,0:T(8,128)} %down.1), custom_call_target="tpu_custom_call" | custom-call | bytes 2097152 | tf_op jit(solution)/shard_map/pack/pallas_call | solution.py:177
  19.8 1.3 collective-permute-start.7
  21.1 1.4 collective-permute-start.8
  22.5 2.7 %collective-permute-start.6 = (f32[128,512]{1,0:T(8,128)S(1)}, f32[128,512]{1,0:T(8,128)S(1)}, u32[]{:S(2)}, u32[]{:S(2)}) collective-permute-start(f32[128,512]{1,0:T(8,128)S(1)} %collective-permute-done.1.refs_6_), channel_id=1, source_target_pairs={{0,224},{32,0},{64,32},{96,64},{128,96},{160,128},{192,160},{224,1... | collective-permute-start | bytes 786440 | tf_op jit(solution)/shard_map/ppermute | solution.py:495
  25.2 2.9 %collective-permute-start.9 = (f32[128,512]{1,0:T(8,128)}, f32[128,512]{1,0:T(8,128)S(1)}, u32[]{:S(2)}, u32[]{:S(2)}) collective-permute-start(f32[128,512]{1,0:T(8,128)} %get-tuple-element.91), channel_id=1, source_target_pairs={{0,8},{1,9},{8,16},{9,17},{16,24},{17,25},{24,32},{25,33},{32,40},... | collective-permute-start | bytes 786440 | tf_op jit(solution)/shard_map/ppermute | solution.py:512
  28.1 1.2 collective-permute-done.5.refs_9_
  29.3 2.4 %collective-permute-done.9.e_in = f32[128,512]{1,0:T(8,128)S(1)} collective-permute-done((f32[128,512]{1,0:T(8,128)}, f32[128,512]{1,0:T(8,128)S(1)}, u32[]{:S(2)}, u32[]{:S(2)}) %collective-permute-start.9) | collective-permute-done | bytes 262176 | tf_op jit(solution)/shard_map/ppermute | solution.py:512
  32.2 0.9 copy-done
  33.1 3.4 %pick.2 = (f32[240,512]{1,0:T(8,128)S(1)}, f32[240,512]{1,0:T(8,128)S(1)}, f32[240,512]{1,0:T(8,128)S(1)}, f32[240,512]{1,0:T(8,128)S(1)}) custom-call(s32[2]{0:T(128)S(1)} %pad_add_fusion.1.pos.refs_0_, s32[96]{0:T(128)S(1)} %get-tuple-element.106.refs_1_, s32[96]{0:T(128)S(1)} %collective-permute-done.2.refs_2_, s32[96]{0:T(128)S(1)} %collective-permute-done.3.refs_3_, ...), custom_call_target="tpu_custom_call" | custom-call | bytes 3932160 | tf_op jit(solution)/shard_map/pick/pallas_call | solution.py:439
  36.6 2.0 %collective-permute-start.14 = (f32[240,512]{1,0:T(8,128)S(1)}, f32[240,512]{1,0:T(8,128)S(1)}, u32[]{:S(2)}, u32[]{:S(2)}) collective-permute-start(f32[240,512]{1,0:T(8,128)S(1)} %get-tuple-element.111), channel_id=1, source_target_pairs={{0,8},{8,16},{16,24},{24,0},{1,9},{9,17},{17,25},{25,1},{2,10},{10... | collective-permute-start | bytes 1474568 | tf_op jit(solution)/shard_map/ppermute | solution.py:522
  38.5 1.7 %collective-permute-start.15 = (f32[240,512]{1,0:T(8,128)S(1)}, f32[240,512]{1,0:T(8,128)S(1)}, u32[]{:S(2)}, u32[]{:S(2)}) collective-permute-start(f32[240,512]{1,0:T(8,128)S(1)} %get-tuple-element.112), channel_id=1, source_target_pairs={{0,16},{8,24},{16,0},{24,8},{1,17},{9,25},{17,1},{25,9},{2,18},{10... | collective-permute-start | bytes 1474568 | tf_op jit(solution)/shard_map/ppermute | solution.py:522
  41.0 0.9 collective-permute-start.10
  41.9 1.8 %collective-permute-start.12 = (f32[128,512]{1,0:T(8,128)S(1)}, f32[128,512]{1,0:T(8,128)S(1)}, u32[]{:S(2)}, u32[]{:S(2)}) collective-permute-start(f32[128,512]{1,0:T(8,128)S(1)} %collective-permute-done.6.refs_8_), channel_id=1, source_target_pairs={{0,224},{32,0},{64,32},{96,64},{128,96},{160,128},{192,160},{224,1... | collective-permute-start | bytes 786440 | tf_op jit(solution)/shard_map/ppermute | solution.py:495
  43.7 4.1 %collective-permute-done.10.refs_6_ = f32[128,512]{1,0:T(8,128)S(1)} collective-permute-done((f32[128,512]{1,0:T(8,128)S(1)}, f32[128,512]{1,0:T(8,128)S(1)}, u32[]{:S(2)}, u32[]{:S(2)}) %collective-permute-start.10) | collective-permute-done | bytes 262176 | tf_op jit(solution)/shard_map/ppermute | solution.py:495
  48.1 2.7 %collective-permute-start.13 = (f32[64,512]{1,0:T(8,128)S(1)}, f32[64,512]{1,0:T(8,128)S(1)}, u32[]{:S(2)}, u32[]{:S(2)}) collective-permute-start(f32[64,512]{1,0:T(8,128)S(1)} %slice.9), channel_id=1, source_target_pairs={{0,224},{32,0},{64,32},{96,64},{128,96},{160,128},{192,160},{224,1... | collective-permute-start | bytes 393224 | tf_op jit(solution)/shard_map/ppermute | solution.py:495
  50.8 3.8 %collective-permute-done.11.refs_7_ = f32[64,512]{1,0:T(8,128)S(1)} collective-permute-done((f32[64,512]{1,0:T(8,128)S(1)}, f32[64,512]{1,0:T(8,128)S(1)}, u32[]{:S(2)}, u32[]{:S(2)}) %collective-permute-start.11) | collective-permute-done | bytes 131104 | tf_op jit(solution)/shard_map/ppermute | solution.py:495
  54.6 3.9 %collective-permute-done.15.refs_2_ = f32[240,512]{1,0:T(8,128)S(1)} collective-permute-done((f32[240,512]{1,0:T(8,128)S(1)}, f32[240,512]{1,0:T(8,128)S(1)}, u32[]{:S(2)}, u32[]{:S(2)}) %collective-permute-start.15) | collective-permute-done | bytes 491552 | tf_op jit(solution)/shard_map/ppermute | solution.py:522
  58.5 2.4 %collective-permute-done.16.refs_3_ = f32[240,512]{1,0:T(8,128)S(1)} collective-permute-done((f32[240,512]{1,0:T(8,128)S(1)}, f32[240,512]{1,0:T(8,128)S(1)}, u32[]{:S(2)}, u32[]{:S(2)}) %collective-permute-start.16) | collective-permute-done | bytes 491552 | tf_op jit(solution)/shard_map/ppermute | solution.py:522
  61.0 2.4 %pick.3 = (f32[144,512]{1,0:T(8,128)S(1)}, f32[144,512]{1,0:T(8,128)S(1)}, f32[144,512]{1,0:T(8,128)S(1)}, f32[144,512]{1,0:T(8,128)S(1)}) custom-call(s32[2]{0:T(128)S(1)} %pad_add_fusion.1.pos.refs_0_, s32[96]{0:T(128)S(1)} %get-tuple-element.106.refs_1_, s32[96]{0:T(128)S(1)} %collective-permute-done.2.refs_2_, s32[96]{0:T(128)S(1)} %collective-permute-done.3.refs_3_, ...), custom_call_target="tpu_custom_call" | custom-call | bytes 2359296 | tf_op jit(solution)/shard_map/pick/pallas_call | solution.py:439
  63.4 2.5 %collective-permute-start.22 = (f32[144,512]{1,0:T(8,128)S(1)}, f32[144,512]{1,0:T(8,128)S(1)}, u32[]{:S(2)}, u32[]{:S(2)}) collective-permute-start(f32[144,512]{1,0:T(8,128)S(1)} %get-tuple-element.125), channel_id=1, source_target_pairs={{0,8},{8,16},{16,24},{24,0},{1,9},{9,17},{17,25},{25,1},{2,10},{10... | collective-permute-start | bytes 884744 | tf_op jit(solution)/shard_map/ppermute | solution.py:522
  65.8 1.0 collective-permute-start.17
  66.8 2.1 %collective-permute-start.23 = (f32[144,512]{1,0:T(8,128)S(1)}, f32[144,512]{1,0:T(8,128)S(1)}, u32[]{:S(2)}, u32[]{:S(2)}) collective-permute-start(f32[144,512]{1,0:T(8,128)S(1)} %get-tuple-element.126), channel_id=1, source_target_pairs={{0,16},{8,24},{16,0},{24,8},{1,17},{9,25},{17,1},{25,9},{2,18},{10... | collective-permute-start | bytes 884744 | tf_op jit(solution)/shard_map/ppermute | solution.py:522
  68.9 0.8 collective-permute-start.24
  70.5 2.1 %collective-permute-done.22.refs_5_ = f32[144,512]{1,0:T(8,128)S(1)} collective-permute-done((f32[144,512]{1,0:T(8,128)S(1)}, f32[144,512]{1,0:T(8,128)S(1)}, u32[]{:S(2)}, u32[]{:S(2)}) %collective-permute-start.22) | collective-permute-done | bytes 294944 | tf_op jit(solution)/shard_map/ppermute | solution.py:522
  72.6 3.7 %collective-permute-start.26 = (f32[256,512]{1,0:T(8,128)S(1)}, f32[256,512]{1,0:T(8,128)S(1)}, u32[]{:S(2)}, u32[]{:S(2)}) collective-permute-start(f32[256,512]{1,0:T(8,128)S(1)} %copy-done.5), channel_id=1, source_target_pairs={{0,6},{2,0},{4,2},{6,4},{1,7},{3,1},{5,3},{7,5},{8,14},{10,8},{12,... | collective-permute-start | bytes 1572872 | tf_op jit(solution)/shard_map/ppermute | solution.py:498
  76.3 4.5 %collective-permute-done.23.refs_6_ = f32[144,512]{1,0:T(8,128)S(1)} collective-permute-done((f32[144,512]{1,0:T(8,128)S(1)}, f32[144,512]{1,0:T(8,128)S(1)}, u32[]{:S(2)}, u32[]{:S(2)}) %collective-permute-start.23) | collective-permute-done | bytes 294944 | tf_op jit(solution)/shard_map/ppermute | solution.py:522
  80.8 1.5 collective-permute-start.20
  83.3 0.9 collective-permute-start.28
  84.2 1.0 collective-permute-start.25
  85.3 3.4 %collective-permute-start.27 = (f32[256,512]{1,0:T(8,128)S(1)}, f32[256,512]{1,0:T(8,128)}, u32[]{:S(2)}, u32[]{:S(2)}) collective-permute-start(f32[256,512]{1,0:T(8,128)S(1)} %collective-permute-done.26.refs_6_), channel_id=1, source_target_pairs={{0,6},{2,0},{4,2},{6,4},{1,7},{3,1},{5,3},{7,5},{8,14},{10,8},{12,... | collective-permute-start | bytes 1572872 | tf_op jit(solution)/shard_map/ppermute | solution.py:537
  88.7 0.8 copy-done.15
  89.6 2.1 %send.1 = f32[768,512]{1,0:T(8,128)} custom-call(s32[48]{0:T(128)S(1)} %get-tuple-element.77.row, f32[240,512]{1,0:T(8,128)S(1)} %get-tuple-element.114.refs_0_, f32[240,512]{1,0:T(8,128)S(1)} %collective-permute-done.14.refs_1_, f32[240,512]{1,0:T(8,128)S(1)} %collective-permute-done.15.refs_2_, f32[240,512]{1,0:T(8,128)S(1)} %collective-permute-done.16.refs_3_, ...), custom_call_target="tpu_custom_call" | custom-call | bytes 6291456 | tf_op jit(solution)/shard_map/send/pallas_call | solution.py:462
  91.7 6.9 %all-to-all-start = ((f32[8,96,512]{2,1,0:T(8,128)}), f32[8,96,512]{2,1,0:T(8,128)S(1)}, u32[]{:S(2)}, u32[]{:S(2)}) async-start(f32[8,96,512]{2,1,0:T(8,128)} %bitcast.11), calls=%async_computation | async-start | bytes 3145728 | tf_op jit(solution)/shard_map/all_to_all | solution.py:541
  99.3 11.2 %collective-permute-done.25.rest_4_ = f32[256,512]{1,0:T(8,128)} collective-permute-done((f32[256,512]{1,0:T(8,128)}, f32[256,512]{1,0:T(8,128)}, u32[]{:S(2)}, u32[]{:S(2)}) %collective-permute-start.25) | collective-permute-done | bytes 524320 | tf_op jit(solution)/shard_map/ppermute | solution.py:536
  110.5 0.9 collective-permute-start.30
  113.2 2.2 %collective-permute-done.31.refs_5_ = f32[256,512]{1,0:T(8,128)S(1)} collective-permute-done((f32[256,512]{1,0:T(8,128)}, f32[256,512]{1,0:T(8,128)S(1)}, u32[]{:S(2)}, u32[]{:S(2)}) %collective-permute-start.31) | collective-permute-done | bytes 524320 | tf_op jit(solution)/shard_map/ppermute | solution.py:501
  115.5 0.8 copy-done.9
  116.3 5.0 %prep.1 = (bf16[2,512,1024]{2,1,0:T(8,128)(2,1)}, bf16[2,1024,512]{2,1,0:T(8,128)(2,1)}) custom-call(f32[256,512]{1,0:T(8,128)} %get-tuple-element.120.refs_0_, f32[256,512]{1,0:T(8,128)} %copy-done.6, f32[256,512]{1,0:T(8,128)} %collective-permute-done.28.refs_2_, f32[256,512]{1,0:T(8,128)} %copy-done.8, f32[256,512]{1,0:T(8,128)} %collective-permute-done.27.refs_4_, ...), custom_call_target="tpu_custom_call" | custom-call | flops 10000000 | bytes 8388608 | tf_op jit(solution)/shard_map/prep/pallas_call | solution.py:284
  121.3 15.4 %near.1 = (f32[128,512]{1,0:T(8,128)}, bf16[2,4,256,512]{3,2,1,0:T(8,128)(2,1)}, bf16[2,4,128,512]{3,2,1,0:T(8,128)(2,1)}, bf16[2,512,512]{2,1,0:T(8,128)(2,1)}, f32[4,256,128]{2,1,0:T(8,128)}) custom-call(s32[4]{0:T(128)} %pad_add_fusion.pos, s32[8,3]{1,0:T(8,128)} %copy.14.local_ref, s32[8]{0:T(128)} %virt_ref.1, s32[256]{0:T(256)} %count_ref.3, ...), custom_call_target="tpu_custom_call" | custom-call | flops 6000000000 | bytes 16777216 | tf_op jit(solution)/shard_map/near/pallas_call | solution.py:257
  136.7 1.2 copy-done.4
  137.9 13.8 %far.1 = f32[512,128]{1,0:T(8,128)} custom-call(s32[4]{0:T(128)} %pad_add_fusion.pos, s32[8,6]{1,0:T(8,128)} %exp_ref.3, s32[256]{0:T(256)} %count_ref.3, f32[768,512]{1,0:T(8,128)} %bitcast.20, bf16[2,4,256,512]{3,2,1,0:T(8,128)(2,1)} %get-tuple-element.138.q_hbm, f32[4,256,128]{2,1,0:T(8,128)} %get-tuple-element.139.s_hbm, ...), custom_call_target="tpu_custom_call" | custom-call | flops 6000000000 | bytes 16777216 | tf_op jit(solution)/shard_map/far/pallas_call | solution.py:361
  151.7 10.2 %all_to_all.22 = f32[8,64,128]{2,1,0:T(8,128)S(1)} all-to-all(f32[8,64,128]{2,1,0:T(8,128)} %bitcast.21), channel_id=1, replica_groups=mesh['z'=8,'x'=4,'y'=4,'c'=2] {'y','c'}, dimensions={0} | all-to-all | bytes 524288 | tf_op jit(solution)/shard_map/all_to_all | solution.py:551
  161.9 2.1 %place.1 = f32[64,1024]{1,0:T(8,128)} custom-call(s32[4]{0:T(128)S(1)} %copy-done.2, f32[512,128]{1,0:T(8,128)S(1)} %bitcast.16, s32[8,128]{1,0:T(8,128)S(1)} %bitcast.19), custom_call_target="tpu_custom_call" | custom-call | flops 400000000 | bytes 1048576 | tf_op jit(solution)/shard_map/place/pallas_call | solution.py:391
  (72 shorter events, 8.3 us)
Async XLA Ops:
  0.0 10.8 %copy-start.1 = (s32[8,6]{1,0:T(8,128)S(1)}, s32[8,6]{1,0:T(8,128)}, u32[]{:S(2)}) copy-start(s32[8,6]{1,0:T(8,128)} %exp_ref.3) | copy-start | bytes 580
  4.2 18.3 %collective-permute-start = (f32[128,512]{1,0:T(8,128)}, f32[128,512]{1,0:T(8,128)S(1)}, u32[]{:S(2)}, u32[]{:S(2)}) collective-permute-start(f32[128,512]{1,0:T(8,128)} %get-tuple-element.78.refs_5_), channel_id=1, source_target_pairs={{0,32},{32,64},{64,96},{96,128},{128,160},{160,192},{192,224},{224... | collective-permute-start | bytes 786440 | tf_op jit(solution)/shard_map/ppermute | solution.py:495
  6.7 15.8 %collective-permute-start.1 = (f32[128,512]{1,0:T(8,128)}, f32[128,512]{1,0:T(8,128)S(1)}, u32[]{:S(2)}, u32[]{:S(2)}) collective-permute-start(f32[128,512]{1,0:T(8,128)} %get-tuple-element.78.refs_5_), channel_id=1, source_target_pairs={{0,224},{32,0},{64,32},{96,64},{128,96},{160,128},{192,160},{224,1... | collective-permute-start | bytes 786440 | tf_op jit(solution)/shard_map/ppermute | solution.py:495
  13.1 6.0 %collective-permute-start.2 = (s32[96]{0:T(128)S(1)}, s32[96]{0:T(128)S(1)}, u32[]{:S(2)}, u32[]{:S(2)}) collective-permute-start(s32[96]{0:T(128)S(1)} %get-tuple-element.106.refs_1_), channel_id=1, source_target_pairs={{0,24},{8,0},{16,8},{24,16},{1,25},{9,1},{17,9},{25,17},{2,26},{10... | collective-permute-start | bytes 1160 | tf_op jit(solution)/shard_map/ppermute | solution.py:505
  15.6 3.9 %collective-permute-start.3 = (s32[96]{0:T(128)S(1)}, s32[96]{0:T(128)S(1)}, u32[]{:S(2)}, u32[]{:S(2)}) collective-permute-start(s32[96]{0:T(128)S(1)} %get-tuple-element.106.refs_1_), channel_id=1, source_target_pairs={{0,16},{8,24},{16,0},{24,8},{1,17},{9,25},{17,1},{25,9},{2,18},{10... | collective-permute-start | bytes 1160 | tf_op jit(solution)/shard_map/ppermute | solution.py:505
  16.2 3.6 %collective-permute-start.4 = (s32[96]{0:T(128)S(1)}, s32[96]{0:T(128)S(1)}, u32[]{:S(2)}, u32[]{:S(2)}) collective-permute-start(s32[96]{0:T(128)S(1)} %get-tuple-element.106.refs_1_), channel_id=1, source_target_pairs={{0,8},{8,16},{16,24},{24,0},{1,9},{9,17},{17,25},{25,1},{2,10},{10... | collective-permute-start | bytes 1160 | tf_op jit(solution)/shard_map/ppermute | solution.py:505
  19.8 12.4 %collective-permute-start.7 = (f32[256,512]{1,0:T(8,128)}, f32[256,512]{1,0:T(8,128)}, u32[]{:S(2)}, u32[]{:S(2)}) collective-permute-start(f32[256,512]{1,0:T(8,128)} %get-tuple-element.119.rest_0_), channel_id=1, source_target_pairs={{0,2},{2,4},{4,6},{6,0},{1,3},{3,5},{5,7},{7,1},{8,10},{10,12},{12... | collective-permute-start | bytes 1572872 | tf_op jit(solution)/shard_map/ppermute | solution.py:498
  21.1 11.1 %collective-permute-start.8 = (f32[256,512]{1,0:T(8,128)}, f32[256,512]{1,0:T(8,128)S(1)}, u32[]{:S(2)}, u32[]{:S(2)}) collective-permute-start(f32[256,512]{1,0:T(8,128)} %get-tuple-element.119.rest_0_), channel_id=1, source_target_pairs={{0,6},{2,0},{4,2},{6,4},{1,7},{3,1},{5,3},{7,5},{8,14},{10,8},{12,... | collective-permute-start | bytes 1572872 | tf_op jit(solution)/shard_map/ppermute | solution.py:498
  22.5 6.8 %collective-permute-start.5 = (f32[128,512]{1,0:T(8,128)S(1)}, f32[128,512]{1,0:T(8,128)S(1)}, u32[]{:S(2)}, u32[]{:S(2)}) collective-permute-start(f32[128,512]{1,0:T(8,128)S(1)} %collective-permute-done.refs_7_), channel_id=1, source_target_pairs={{0,32},{32,64},{64,96},{96,128},{128,160},{160,192},{192,224},{224... | collective-permute-start | bytes 786440 | tf_op jit(solution)/shard_map/ppermute | solution.py:495
  22.5 6.8 %collective-permute-start.6 = (f32[128,512]{1,0:T(8,128)S(1)}, f32[128,512]{1,0:T(8,128)S(1)}, u32[]{:S(2)}, u32[]{:S(2)}) collective-permute-start(f32[128,512]{1,0:T(8,128)S(1)} %collective-permute-done.1.refs_6_), channel_id=1, source_target_pairs={{0,224},{32,0},{64,32},{96,64},{128,96},{160,128},{192,160},{224,1... | collective-permute-start | bytes 786440 | tf_op jit(solution)/shard_map/ppermute | solution.py:495
  25.2 6.5 %collective-permute-start.9 = (f32[128,512]{1,0:T(8,128)}, f32[128,512]{1,0:T(8,128)S(1)}, u32[]{:S(2)}, u32[]{:S(2)}) collective-permute-start(f32[128,512]{1,0:T(8,128)} %get-tuple-element.91), channel_id=1, source_target_pairs={{0,8},{1,9},{8,16},{9,17},{16,24},{17,25},{24,32},{25,33},{32,40},... | collective-permute-start | bytes 786440 | tf_op jit(solution)/shard_map/ppermute | solution.py:512
  31.7 59.9 %copy-start.16 = (f32[128,512]{1,0:T(8,128)}, f32[128,512]{1,0:T(8,128)S(1)}, u32[]{:S(2)}) copy-start(f32[128,512]{1,0:T(8,128)S(1)} %collective-permute-done.9.e_in) | copy-start | bytes 786436
  33.1 58.5 %copy-start.12 = (f32[256,512]{1,0:T(8,128)}, f32[256,512]{1,0:T(8,128)S(1)}, u32[]{:S(2)}) copy-start(f32[256,512]{1,0:T(8,128)S(1)} %collective-permute-done.8.rest_6_) | copy-start | bytes 1572868
  33.1 36.7 %copy-start.11 = (f32[256,512]{1,0:T(8,128)S(1)}, f32[256,512]{1,0:T(8,128)}, u32[]{:S(2)}) copy-start(f32[256,512]{1,0:T(8,128)} %get-tuple-element.119.rest_0_) | copy-start | bytes 1572868
  33.1 37.2 %copy-start.5 = (f32[256,512]{1,0:T(8,128)S(1)}, f32[256,512]{1,0:T(8,128)}, u32[]{:S(2)}) copy-start(f32[256,512]{1,0:T(8,128)} %get-tuple-element.120.refs_0_) | copy-start | bytes 1572868
  36.6 18.0 %collective-permute-start.14 = (f32[240,512]{1,0:T(8,128)S(1)}, f32[240,512]{1,0:T(8,128)S(1)}, u32[]{:S(2)}, u32[]{:S(2)}) collective-permute-start(f32[240,512]{1,0:T(8,128)S(1)} %get-tuple-element.111), channel_id=1, source_target_pairs={{0,8},{8,16},{16,24},{24,0},{1,9},{9,17},{17,25},{25,1},{2,10},{10... | collective-permute-start | bytes 1474568 | tf_op jit(solution)/shard_map/ppermute | solution.py:522
  38.5 20.0 %collective-permute-start.15 = (f32[240,512]{1,0:T(8,128)S(1)}, f32[240,512]{1,0:T(8,128)S(1)}, u32[]{:S(2)}, u32[]{:S(2)}) collective-permute-start(f32[240,512]{1,0:T(8,128)S(1)} %get-tuple-element.112), channel_id=1, source_target_pairs={{0,16},{8,24},{16,0},{24,8},{1,17},{9,25},{17,1},{25,9},{2,18},{10... | collective-permute-start | bytes 1474568 | tf_op jit(solution)/shard_map/ppermute | solution.py:522
  40.3 20.7 %collective-permute-start.16 = (f32[240,512]{1,0:T(8,128)S(1)}, f32[240,512]{1,0:T(8,128)S(1)}, u32[]{:S(2)}, u32[]{:S(2)}) collective-permute-start(f32[240,512]{1,0:T(8,128)S(1)} %get-tuple-element.113), channel_id=1, source_target_pairs={{0,24},{8,0},{16,8},{24,16},{1,25},{9,1},{17,9},{25,17},{2,26},{10... | collective-permute-start | bytes 1474568 | tf_op jit(solution)/shard_map/ppermute | solution.py:522
  41.0 6.7 %collective-permute-start.10 = (f32[128,512]{1,0:T(8,128)S(1)}, f32[128,512]{1,0:T(8,128)S(1)}, u32[]{:S(2)}, u32[]{:S(2)}) collective-permute-start(f32[128,512]{1,0:T(8,128)S(1)} %collective-permute-done.5.refs_9_), channel_id=1, source_target_pairs={{0,32},{32,64},{64,96},{96,128},{128,160},{160,192},{192,224},{224... | collective-permute-start | bytes 786440 | tf_op jit(solution)/shard_map/ppermute | solution.py:495
  41.9 6.1 %collective-permute-start.12 = (f32[128,512]{1,0:T(8,128)S(1)}, f32[128,512]{1,0:T(8,128)S(1)}, u32[]{:S(2)}, u32[]{:S(2)}) collective-permute-start(f32[128,512]{1,0:T(8,128)S(1)} %collective-permute-done.6.refs_8_), channel_id=1, source_target_pairs={{0,224},{32,0},{64,32},{96,64},{128,96},{160,128},{192,160},{224,1... | collective-permute-start | bytes 786440 | tf_op jit(solution)/shard_map/ppermute | solution.py:495
  47.8 6.9 %collective-permute-start.11 = (f32[64,512]{1,0:T(8,128)S(1)}, f32[64,512]{1,0:T(8,128)S(1)}, u32[]{:S(2)}, u32[]{:S(2)}) collective-permute-start(f32[64,512]{1,0:T(8,128)S(1)} %slice.8), channel_id=1, source_target_pairs={{0,32},{32,64},{64,96},{96,128},{128,160},{160,192},{192,224},{224... | collective-permute-start | bytes 393224 | tf_op jit(solution)/shard_map/ppermute | solution.py:495
  48.1 6.6 %collective-permute-start.13 = (f32[64,512]{1,0:T(8,128)S(1)}, f32[64,512]{1,0:T(8,128)S(1)}, u32[]{:S(2)}, u32[]{:S(2)}) collective-permute-start(f32[64,512]{1,0:T(8,128)S(1)} %slice.9), channel_id=1, source_target_pairs={{0,224},{32,0},{64,32},{96,64},{128,96},{160,128},{192,160},{224,1... | collective-permute-start | bytes 393224 | tf_op jit(solution)/shard_map/ppermute | solution.py:495
  63.4 9.3 %collective-permute-start.22 = (f32[144,512]{1,0:T(8,128)S(1)}, f32[144,512]{1,0:T(8,128)S(1)}, u32[]{:S(2)}, u32[]{:S(2)}) collective-permute-start(f32[144,512]{1,0:T(8,128)S(1)} %get-tuple-element.125), channel_id=1, source_target_pairs={{0,8},{8,16},{16,24},{24,0},{1,9},{9,17},{17,25},{25,1},{2,10},{10... | collective-permute-start | bytes 884744 | tf_op jit(solution)/shard_map/ppermute | solution.py:522
  65.8 4.5 %collective-permute-start.17 = (f32[128,512]{1,0:T(8,128)S(1)}, f32[128,512]{1,0:T(8,128)S(1)}, u32[]{:S(2)}, u32[]{:S(2)}) collective-permute-start(f32[128,512]{1,0:T(8,128)S(1)} %collective-permute-done.9.e_in), channel_id=1, source_target_pairs={{0,1},{1,0},{2,3},{3,2},{4,5},{5,4},{6,7},{7,6},{8,9},{9,8},{10,11... | collective-permute-start | bytes 786440 | tf_op jit(solution)/shard_map/ppermute | solution.py:501
  66.8 14.0 %collective-permute-start.23 = (f32[144,512]{1,0:T(8,128)S(1)}, f32[144,512]{1,0:T(8,128)S(1)}, u32[]{:S(2)}, u32[]{:S(2)}) collective-permute-start(f32[144,512]{1,0:T(8,128)S(1)} %get-tuple-element.126), channel_id=1, source_target_pairs={{0,16},{8,24},{16,0},{24,8},{1,17},{9,25},{17,1},{25,9},{2,18},{10... | collective-permute-start | bytes 884744 | tf_op jit(solution)/shard_map/ppermute | solution.py:522
  68.9 13.6 %collective-permute-start.24 = (f32[144,512]{1,0:T(8,128)S(1)}, f32[144,512]{1,0:T(8,128)S(1)}, u32[]{:S(2)}, u32[]{:S(2)}) collective-permute-start(f32[144,512]{1,0:T(8,128)S(1)} %get-tuple-element.127), channel_id=1, source_target_pairs={{0,24},{8,0},{16,8},{24,16},{1,25},{9,1},{17,9},{25,17},{2,26},{10... | collective-permute-start | bytes 884744 | tf_op jit(solution)/shard_map/ppermute | solution.py:522
  69.8 13.5 %collective-permute-start.18 = (f32[256,512]{1,0:T(8,128)S(1)}, f32[256,512]{1,0:T(8,128)S(1)}, u32[]{:S(2)}, u32[]{:S(2)}) collective-permute-start(f32[256,512]{1,0:T(8,128)S(1)} %copy-done.11), channel_id=1, source_target_pairs={{0,1},{1,0},{2,3},{3,2},{4,5},{5,4},{6,7},{7,6},{8,9},{9,8},{10,11... | collective-permute-start | bytes 1572872 | tf_op jit(solution)/shard_map/ppermute | solution.py:501
  70.4 5.9 %copy-start.17 = (f32[128,512]{1,0:T(8,128)}, f32[128,512]{1,0:T(8,128)S(1)}, u32[]{:S(2)}) copy-start(f32[128,512]{1,0:T(8,128)S(1)} %collective-permute-done.17.e_other) | copy-start | bytes 786436
  70.4 13.9 %collective-permute-start.19 = (f32[256,512]{1,0:T(8,128)S(1)}, f32[256,512]{1,0:T(8,128)S(1)}, u32[]{:S(2)}, u32[]{:S(2)}) collective-permute-start(f32[256,512]{1,0:T(8,128)S(1)} %copy-done.5), channel_id=1, source_target_pairs={{0,1},{1,0},{2,3},{3,2},{4,5},{5,4},{6,7},{7,6},{8,9},{9,8},{10,11... | collective-permute-start | bytes 1572872 | tf_op jit(solution)/shard_map/ppermute | solution.py:501
  72.6 12.7 %collective-permute-start.26 = (f32[256,512]{1,0:T(8,128)S(1)}, f32[256,512]{1,0:T(8,128)S(1)}, u32[]{:S(2)}, u32[]{:S(2)}) collective-permute-start(f32[256,512]{1,0:T(8,128)S(1)} %copy-done.5), channel_id=1, source_target_pairs={{0,6},{2,0},{4,2},{6,4},{1,7},{3,1},{5,3},{7,5},{8,14},{10,8},{12,... | collective-permute-start | bytes 1572872 | tf_op jit(solution)/shard_map/ppermute | solution.py:498
  80.8 7.9 %collective-permute-start.20 = (f32[256,512]{1,0:T(8,128)}, f32[256,512]{1,0:T(8,128)S(1)}, u32[]{:S(2)}, u32[]{:S(2)}) collective-permute-start(f32[256,512]{1,0:T(8,128)} %collective-permute-done.7.rest_2_), channel_id=1, source_target_pairs={{0,1},{1,0},{2,3},{3,2},{4,5},{5,4},{6,7},{7,6},{8,9},{9,8},{10,11... | collective-permute-start | bytes 1572872 | tf_op jit(solution)/shard_map/ppermute | solution.py:501
  82.5 6.2 %collective-permute-start.21 = (f32[256,512]{1,0:T(8,128)S(1)}, f32[256,512]{1,0:T(8,128)S(1)}, u32[]{:S(2)}, u32[]{:S(2)}) collective-permute-start(f32[256,512]{1,0:T(8,128)S(1)} %collective-permute-done.8.rest_6_), channel_id=1, source_target_pairs={{0,1},{1,0},{2,3},{3,2},{4,5},{5,4},{6,7},{7,6},{8,9},{9,8},{10,11... | collective-permute-start | bytes 1572872 | tf_op jit(solution)/shard_map/ppermute | solution.py:501
  83.3 5.4 %copy-start.13 = (f32[256,512]{1,0:T(8,128)}, f32[256,512]{1,0:T(8,128)S(1)}, u32[]{:S(2)}) copy-start(f32[256,512]{1,0:T(8,128)S(1)} %collective-permute-done.18.rest_1_) | copy-start | bytes 1572868
  83.3 16.0 %collective-permute-start.28 = (f32[256,512]{1,0:T(8,128)S(1)}, f32[256,512]{1,0:T(8,128)}, u32[]{:S(2)}, u32[]{:S(2)}) collective-permute-start(f32[256,512]{1,0:T(8,128)S(1)} %copy-done.5), channel_id=1, source_target_pairs={{0,2},{2,4},{4,6},{6,0},{1,3},{3,5},{5,7},{7,1},{8,10},{10,12},{12... | collective-permute-start | bytes 1572872 | tf_op jit(solution)/shard_map/ppermute | solution.py:498
  84.2 7.4 %copy-start.6 = (f32[256,512]{1,0:T(8,128)}, f32[256,512]{1,0:T(8,128)S(1)}, u32[]{:S(2)}) copy-start(f32[256,512]{1,0:T(8,128)S(1)} %collective-permute-done.19.refs_1_) | copy-start | bytes 1572868
  84.2 26.3 %collective-permute-start.25 = (f32[256,512]{1,0:T(8,128)}, f32[256,512]{1,0:T(8,128)}, u32[]{:S(2)}, u32[]{:S(2)}) collective-permute-start(f32[256,512]{1,0:T(8,128)} %collective-permute-done.7.rest_2_), channel_id=1, source_target_pairs={{0,2},{2,4},{4,6},{6,0},{1,3},{3,5},{5,7},{7,1},{8,10},{10,12},{12... | collective-permute-start | bytes 1572872 | tf_op jit(solution)/shard_map/ppermute | solution.py:536
  85.3 26.2 %copy-start.7 = (f32[256,512]{1,0:T(8,128)}, f32[256,512]{1,0:T(8,128)S(1)}, u32[]{:S(2)}) copy-start(f32[256,512]{1,0:T(8,128)S(1)} %collective-permute-done.26.refs_6_) | copy-start | bytes 1572868
  85.3 25.3 %collective-permute-start.27 = (f32[256,512]{1,0:T(8,128)S(1)}, f32[256,512]{1,0:T(8,128)}, u32[]{:S(2)}, u32[]{:S(2)}) collective-permute-start(f32[256,512]{1,0:T(8,128)S(1)} %collective-permute-done.26.refs_6_), channel_id=1, source_target_pairs={{0,6},{2,0},{4,2},{6,4},{1,7},{3,1},{5,3},{7,5},{8,14},{10,8},{12,... | collective-permute-start | bytes 1572872 | tf_op jit(solution)/shard_map/ppermute | solution.py:537
  88.7 3.0 %copy-start.14 = (f32[256,512]{1,0:T(8,128)}, f32[256,512]{1,0:T(8,128)S(1)}, u32[]{:S(2)}) copy-start(f32[256,512]{1,0:T(8,128)S(1)} %collective-permute-done.20.rest_3_) | copy-start | bytes 1572868
  91.7 20.3 %copy-start.10 = (s32[8,3]{0,1:T(4,128)S(1)}, s32[8,3]{0,1:T(4,128)}, u32[]{:S(2)}) copy-start(s32[8,3]{0,1:T(4,128)} %param.16) | copy-start | bytes 292
  91.7 45.0 %all-to-all-start = ((f32[8,96,512]{2,1,0:T(8,128)}), f32[8,96,512]{2,1,0:T(8,128)S(1)}, u32[]{:S(2)}, u32[]{:S(2)}) async-start(f32[8,96,512]{2,1,0:T(8,128)} %bitcast.11), calls=%async_computation | async-start | bytes 3145728 | tf_op jit(solution)/shard_map/all_to_all | solution.py:541
  110.5 2.7 %collective-permute-start.30 = (f32[256,512]{1,0:T(8,128)}, f32[256,512]{1,0:T(8,128)S(1)}, u32[]{:S(2)}, u32[]{:S(2)}) collective-permute-start(f32[256,512]{1,0:T(8,128)} %collective-permute-done.28.refs_2_), channel_id=1, source_target_pairs={{0,1},{1,0},{2,3},{3,2},{4,5},{5,4},{6,7},{7,6},{8,9},{9,8},{10,11... | collective-permute-start | bytes 1572872 | tf_op jit(solution)/shard_map/ppermute | solution.py:501
  111.5 4.0 %collective-permute-start.31 = (f32[256,512]{1,0:T(8,128)}, f32[256,512]{1,0:T(8,128)S(1)}, u32[]{:S(2)}, u32[]{:S(2)}) collective-permute-start(f32[256,512]{1,0:T(8,128)} %collective-permute-done.27.refs_4_), channel_id=1, source_target_pairs={{0,1},{1,0},{2,3},{3,2},{4,5},{5,4},{6,7},{7,6},{8,9},{9,8},{10,11... | collective-permute-start | bytes 1572872 | tf_op jit(solution)/shard_map/ppermute | solution.py:501
  111.5 4.0 %collective-permute-start.32 = (f32[256,512]{1,0:T(8,128)S(1)}, f32[256,512]{1,0:T(8,128)}, u32[]{:S(2)}, u32[]{:S(2)}) collective-permute-start(f32[256,512]{1,0:T(8,128)S(1)} %collective-permute-done.26.refs_6_), channel_id=1, source_target_pairs={{0,1},{1,0},{2,3},{3,2},{4,5},{5,4},{6,7},{7,6},{8,9},{9,8},{10,11... | collective-permute-start | bytes 1572872 | tf_op jit(solution)/shard_map/ppermute | solution.py:501
  112.0 9.3 %collective-permute-start.29 = (f32[256,512]{1,0:T(8,128)}, f32[256,512]{1,0:T(8,128)}, u32[]{:S(2)}, u32[]{:S(2)}) collective-permute-start(f32[256,512]{1,0:T(8,128)} %collective-permute-done.25.rest_4_), channel_id=1, source_target_pairs={{0,1},{1,0},{2,3},{3,2},{4,5},{5,4},{6,7},{7,6},{8,9},{9,8},{10,11... | collective-permute-start | bytes 1572872 | tf_op jit(solution)/shard_map/ppermute | solution.py:501
  113.2 2.3 %copy-start.8 = (f32[256,512]{1,0:T(8,128)}, f32[256,512]{1,0:T(8,128)S(1)}, u32[]{:S(2)}) copy-start(f32[256,512]{1,0:T(8,128)S(1)} %collective-permute-done.30.refs_3_) | copy-start | bytes 1572868
  137.9 24.0 %copy-start.2 = (s32[4]{0:T(128)S(1)}, s32[4]{0:T(128)}, u32[]{:S(2)}) copy-start(s32[4]{0:T(128)} %pad_add_fusion.pos) | copy-start | bytes 52
  137.9 24.0 %copy-start.3 = (s32[1024]{0:T(1024)S(1)}, s32[1024]{0:T(1024)}, u32[]{:S(2)}) copy-start(s32[1024]{0:T(1024)} %param.14) | copy-start | bytes 12292
  (4 other events, 3.8 us)
where the time goes:
time: 167 us; the launch traced here: 164 us
  starting transfers between devices  55.4 us (33%)
  Pallas kernels  52.2 us (31%)
  waiting for transfers between devices  40.7 us (24%)
  blocking collectives  10.2 us (6%)
  local copies, waits for them, and re-layouts  4.56 us (3%)
    pallas_call x1, Pallas kernels, near_call(): pl.pallas_call(near_kernel, out_shape=shapes, in_specs=[sspec()] * len(sc...  15.4 us
    pallas_call x1, Pallas kernels, far_call(): pl.pallas_call(far_kernel, out_shape=sds(D, CL), in_specs=[sspec()] * len...  13.8 us
    ppermute x6, waiting for transfers between devices, exchange(): lax.ppermute(blocks[k], 'x', ring(NX, k))  13.2 us
    ppermute x1, waiting for transfers between devices, shards(): a_far = lax.ppermute(a_up, 'y', ring(NY, 1))  11.2 us
    ppermute x4, starting transfers between devices, both_z(): lax.ppermute(b, 'z', ring(NZ, -1))  11.2 us
    all_to_all x1, blocking collectives, shards(): received = lax.all_to_all(result, ('y', 'c'), 0, 0, tiled=True)  10.2 us
    ppermute x6, starting transfers between devices, exchange(): lax.ppermute(blocks[k], 'x', ring(NX, k))  9.87 us
    ppermute x4, waiting for transfers between devices, both_z(): lax.ppermute(a, 'z', ring(NZ, 1))  9.09 us
  transfers between devices with their start and end apart: 34, of which 17 were waited for; matrix products, arithmetic and copies ran while one was open for 0% of the time, Pallas kernels for 15%

commit v1 on v0

--- a/solution.py
+++ b/solution.py
@@ -186,10 +186,11 @@
     )(*w)
 
 
-def near_kernel(pos, local_ref, virt_ref, count_ref, order_ref, nodes_ref, e_in, e_other, virtual_ref, *rest):
-    w = rest[:8]
-    x_out, q_out, v_out, o_out, state, kh, kl = rest[8:]
-    base, head, c, y = pos[0], pos[1], pos[2], pos[3]
+def near_kernel(pos, local_ref, virt_ref, count_ref, order_ref, nodes_ref, e_in, e_other, virtual_ref, w_hbm,
+                x_out, q_out, v_out, o_out, state, kh, kl, w, sem):
+    fetch = pltpu.make_async_copy(w_hbm, w, sem)
+    fetch.start()
+    base, head, c = pos[0], pos[1], pos[2]
     first = lax.shift_right_logical(base, 7)
 
     def order_row(r):
@@ -220,11 +221,9 @@
     lanes = lax.broadcasted_iota(jnp.int32, (CL, 2 * HD), 1)
     lowq = lanes < HD
     xh, xl = split2(x)
-    for dy in range(NY):
-        a, b = w[2 * dy][...], w[2 * dy + 1][...]
-        at = lax.rem(y - dy + NY, NY)
-        left = jnp.where(c == 0, a, b)
-        right = jnp.where(c == 0, b, a)
+    fetch.wait()
+    for at in range(NY):
+        left, right = w[2 * at], w[2 * at + 1]
         wq, wk, wv, wo = (
             split2(jnp.concatenate([left[i * HD:(i + 1) * HD], right[i * HD:(i + 1) * HD]], 0))
             for i in range(4))
@@ -232,7 +231,7 @@
         both = jnp.concatenate([jnp.where(lowq, q, 0.0), jnp.where(lowq, 0.0, q)], 0)
         q_out[0, at], q_out[1, at] = split2(dot3(*split2(both), *wk, NN))
         v_out[0, at], v_out[1, at] = wv
-        rows = pl.ds(pl.multiple_of(at * CL, CL), CL)
+        rows = slice(at * CL, (at + 1) * CL)
         o_out[0, rows, :], o_out[1, rows, :] = wo
 
     def body(p, carry):
@@ -249,7 +248,7 @@
     lax.fori_loop(0, NY, body, 0)
 
 
-def near_call(scalars, arrays, weights):
+def near_call(scalars, arrays):
     shapes = [
         sds(CL, D), sds(2, NY, 2 * CL, D, dtype=BF), sds(2, NY, 2 * HD, D, dtype=BF),
         sds(2, D, D, dtype=BF), sds(NY, 2 * CL, 2 * HD),
@@ -257,23 +256,21 @@
     return pl.pallas_call(
         near_kernel,
         out_shape=shapes,
-        in_specs=[sspec()] * len(scalars) + [vspec()] * len(arrays)
-        + [vspec()] * len(weights),
+        in_specs=[sspec()] * len(scalars) + [vspec()] * (len(arrays) - 1) + [hspec()],
         out_specs=[vspec()] * len(shapes),
-        scratch_shapes=[pltpu.VMEM((LK, D), BF), pltpu.VMEM((LK, D), BF)],
+        scratch_shapes=[pltpu.VMEM((LK, D), BF), pltpu.VMEM((LK, D), BF), pltpu.VMEM(arrays[-1].shape, F32),
+                        pltpu.SemaphoreType.DMA],
         compiler_params=params(60),
         cost_estimate=cost(6 * 10**9, 16 << 20, 1 << 20),
         name="near",
-    )(*scalars, *arrays, *weights)
-
-
-def prep_kernel(*refs):
-    w = refs[:8]
-    u_out, d_out = refs[8:]
+    )(*scalars, *arrays)
+
+
+def prep_kernel(w, u_out, d_out):
     for i in range(8):
         rows = slice(i * CL, (i + 1) * CL)
-        d_out[0, rows, :], d_out[1, rows, :] = split2(w[i][:CL, :])
-        hi, lo = split2(w[i][CL:, :])
+        d_out[0, rows, :], d_out[1, rows, :] = split2(w[i, :CL, :])
+        hi, lo = split2(w[i, CL:, :])
         for j in range(4):
             cols = slice(j * CL, (j + 1) * CL)
             u_out[0, cols, rows] = hi[:, cols]
@@ -284,12 +281,12 @@
     return pl.pallas_call(
         prep_kernel,
         out_shape=[sds(2, D, FF, dtype=BF), sds(2, FF, D, dtype=BF)],
-        in_specs=[vspec()] * len(weights),
+        in_specs=[vspec()],
         out_specs=[vspec()] * 2,
         compiler_params=params(60),
         cost_estimate=cost(10**7, 8 << 20),
         name="prep",
-    )(*weights)
+    )(weights)
 
 
 def far_kernel(pos, exp_ref, count_ref, xe_ref, q_hbm, s_hbm, v_hbm, x_hbm, o_hbm, u_hbm, d_hbm,
@@ -482,7 +479,7 @@
            w_query, w_key, w_value, w_out, w_up, w_down):
     z, x, y, c = (lax.axis_index(a) for a in ("z", "x", "y", "c"))
     head = y * NC + c
-    pos = jnp.stack([(z * NX + x) * (CD * CL), head, c, y]).astype(jnp.int32)
+    pos = jnp.stack([(z * NX + x) * (CD * CL), head, c]).astype(jnp.int32)
     zx = jnp.stack([z, x]).astype(jnp.int32)
     order = order.reshape(CD, CL)
 
@@ -493,9 +490,6 @@
 
     def both_z(a, b):
         return lax.ppermute(a, "z", ring(NZ, 1)), lax.ppermute(b, "z", ring(NZ, -1))
-
-    def both_y(a):
-        return lax.ppermute(a, "y", ring(NY, 1)), lax.ppermute(a, "y", ring(NY, -1))
 
     def swap(*arrays):
         return [lax.ppermute(t, "c", SWAP) for t in arrays]
@@ -503,11 +497,11 @@
     up, down = both_z(piece, piece)
     table, row = index_call(zx, exp_blocks)
     tables = [table] + [lax.ppermute(table, "x", ring(NX, -k)) for k in range(1, NX)]
+    held = {0: (piece,), 7: (up,), 1: (down,)}
     wa, wb = pack_call(w_query.T, w_key.T, w_value.T, w_out.T, w_up, w_down)
-    held = {0: (piece,), 7: (up,), 1: (down,)}
-    wa, wb, *tables = tie((wa, wb, *tables))
-    a_up, a_down = both_y(wa)
-    up, down, edge, *tables = tie((up, down, edge, *tables))
+    up, down, edge, wa, wb, *tables = tie((up, down, edge, wa, wb, *tables))
+    wa = lax.all_gather(wa, ("y", "c"), axis=0, tiled=True).reshape(CD, 2 * CL, D)
+    wb = lax.all_gather(wb, ("y", "c"), axis=0, tiled=True).reshape(CD, 2 * CL, D)
 
     e_in = lax.ppermute(edge, ("z", "x", "y", "c"), [
         (i * CD + h, (i + s) * CD + h)
@@ -515,37 +509,25 @@
         for i in range(NZ * NX) if 0 <= i + s < NZ * NX for h in hs])
     up, down = both_z(up, down)
     held[6], held[2] = (up,), (down,)
-    up, down, a_up, a_down, wa, wb, e_in, *tables = tie((up, down, a_up, a_down, wa, wb, e_in, *tables))
+    up, down, e_in, *tables = tie((up, down, e_in, *tables))
 
     def exchange(group):
         blocks = pick_call(group, zx, tables, [t for s in group for t in held[s]])
         return [blocks[0]] + [lax.ppermute(blocks[k], "x", ring(NX, k)) for k in (1, 2, 3)]
 
+    up, down = both_z(up, down)
     near_x = exchange(GROUPS[0])
-    up, down = both_z(up, down)
     held[5], held[3] = (up,), (down,)
-    first4, second4 = both_z(up[:half], down[half:])
-    first4, second4, e_in, wa, wb, a_up, a_down = tie((first4, second4, e_in, wa, wb, a_up, a_down))
-    held[4] = (first4, second4)
-    b_up, b_down = both_y(wb)
-    e_other, wa_o, wb_o, a_up_o, a_down_o = swap(e_in, wa, wb, a_up, a_down)
-    a_up, first4, second4, *near_x = tie((a_up, first4, second4, *near_x))
-    held[4] = (first4, second4)
+    held[4] = both_z(up[:half], down[half:])
     far_x = exchange(GROUPS[1])
-
-    a_far = lax.ppermute(a_up, "y", ring(NY, 1))
-    b_far = lax.ppermute(b_down, "y", ring(NY, -1))
-    e_other, wa_o, wb_o, a_up_o, a_down_o, *far_x = tie((e_other, wa_o, wb_o, a_up_o, a_down_o, *far_x))
+    (e_other,) = swap(e_in)
 
     sending = send_call(row, near_x + far_x)
     xe = lax.all_to_all(sending, ("y", "c"), 0, 0, tiled=True)
-    _, a_far_s, b_far_s, b_up_s, b_down_s = tie((row, a_far, b_far, b_up, b_down))
-    a_far_o, b_up_o, b_down_o, b_far_o = swap(a_far_s, b_up_s, b_down_s, b_far_s)
-    wa = [wa, wa_o, a_up, a_up_o, a_far, a_far_o, a_down, a_down_o]
-    wb = [wb, wb_o, b_up, b_up_o, b_far, b_far_o, b_down, b_down_o]
+    _, wa, wb, pos_late = tie((sending, wa, wb, pos))
 
     x_own, q, wv, wo, state = near_call(
-        (pos, local_blocks, virt_blocks, node_count), (order, node_feats, e_in, e_other, virt_feats), wa)
+        (pos_late, local_blocks, virt_blocks, node_count), (order, node_feats, e_in, e_other, virt_feats, wa))
     wu, wd = prep_call(wb)
     result = far_call((pos, exp_blocks, node_count), (xe, q, state, wv, x_own, wo, wu, wd))
     received = lax.all_to_all(result, ("y", "c"), 0, 0, tiled=True)

time: 167 us -> 160 us (0.958)
  the two profiles are of different devices: /device:TPU:1 before, /device:TPU:36 now
where the time goes in v1:
time: 160 us; the launch traced here: 159 us
  Pallas kernels  51.5 us (32%)
  waiting for transfers between devices  44.6 us (28%)
  starting transfers between devices  35.4 us (22%)
  between operations  13.6 us (8%)
  blocking collectives  10.9 us (7%)
  local copies, waits for them, and re-layouts  2.59 us (2%)
    all_gather x1, waiting for transfers between devices, shards(): lax.all_gather(wb, ('y', 'c'), axis=0, tiled=True).reshape(CD, 2 * CL, D)  17.4 us
    pallas_call x1, Pallas kernels, near_call(): pl.pallas_call(near_kernel, out_shape=shapes, in_specs=[sspec()] * len(sc...  14.7 us
    pallas_call x1, Pallas kernels, far_call(): pl.pallas_call(far_kernel, out_shape=sds(D, CL), in_specs=[sspec()] * len...  13.8 us
    ppermute x6, waiting for transfers between devices, exchange(): lax.ppermute(blocks[k], 'x', ring(NX, k))  13.5 us
    ppermute x6, starting transfers between devices, exchange(): lax.ppermute(blocks[k], 'x', ring(NX, k))  11.5 us
    all_to_all x1, blocking collectives, shards(): received = lax.all_to_all(result, ('y', 'c'), 0, 0, tiled=True)  10.9 us
    ppermute x4, starting transfers between devices, both_z(): lax.ppermute(b, 'z', ring(NZ, -1))  9.07 us
    ppermute x4, waiting for transfers between devices, both_z(): lax.ppermute(a, 'z', ring(NZ, 1))  6.46 us
  transfers between devices with their start and end apart: 22, of which 12 were waited for; matrix products, arithmetic and copies ran while one was open for 0% of the time, Pallas kernels for 19%

profile of v1, /device:TPU:36, one launch (start us, length us, event | category | flops | bytes accessed | tf_op | source)
XLA Modules:
  0.0 159.1 jit_solution(1890656408476029997)
XLA Ops:
  6.5 0.6 pad_add_fusion.pos
  7.1 3.5 %first.1 = (f32[128,512]{1,0:T(8,128)}, f32[128,512]{1,0:T(8,128)}) custom-call(s32[3]{0:T(128)} %pad_add_fusion.pos, s32[8,128]{1,0:T(8,128)} %bitcast.18, f32[1024,512]{1,0:T(8,128)} %nodes_ref.1), custom_call_target="tpu_custom_call" | custom-call | flops 1000000000 | bytes 3145728 | tf_op jit(solution)/shard_map/first/pallas_call | solution.py:107
  10.6 0.2 collective-permute-start.1
  10.8 1.9 %collective-permute-start = (f32[128,512]{1,0:T(8,128)}, f32[128,512]{1,0:T(8,128)S(1)}, u32[]{:S(2)}, u32[]{:S(2)}) collective-permute-start(f32[128,512]{1,0:T(8,128)} %get-tuple-element.46.refs_5_), channel_id=1, source_target_pairs={{0,32},{32,64},{64,96},{96,128},{128,160},{160,192},{192,224},{224... | collective-permute-start | bytes 786440 | tf_op jit(solution)/shard_map/ppermute | solution.py:492
  12.7 0.1 pad_add_fusion.1.pos.refs_0_
  12.8 2.3 %index.1 = (s32[96]{0:T(128)S(1)}, s32[48]{0:T(128)S(1)}) custom-call(s32[2]{0:T(128)S(1)} %pad_add_fusion.1.pos.refs_0_, s32[8,6]{1,0:T(8,128)S(1)} %copy-done.1), custom_call_target="tpu_custom_call" | custom-call | flops 1000 | bytes 4096 | tf_op jit(solution)/shard_map/index/pallas_call | solution.py:153
  15.1 1.3 collective-permute-start.4
  16.4 0.8 collective-permute-start.3
  17.2 1.1 collective-permute-start.2
  18.3 2.3 %pack.1 = (f32[256,512]{1,0:T(8,128)}, f32[256,512]{1,0:T(8,128)}) custom-call(f32[64,512]{1,0:T(8,128)} %bitcast.24, f32[64,512]{1,0:T(8,128)} %bitcast.25, f32[64,512]{1,0:T(8,128)} %bitcast.26, f32[64,512]{1,0:T(8,128)} %bitcast.27, f32[512,128]{1,0:T(8,128)} %up.1, f32[128,512]{1,0:T(8,128)} %down.1), custom_call_target="tpu_custom_call" | custom-call | bytes 2097152 | tf_op jit(solution)/shard_map/pack/pallas_call | solution.py:177
  20.6 0.8 collective-permute-done.3.refs_3_
  21.4 1.5 collective-permute-done.refs_7_
  23.0 0.0 all-gather.5.cloned.1.call-start
  23.0 0.7 all-gather.5.cloned.1.call-update
  23.7 0.5 collective-permute-start.5
  24.2 2.6 %collective-permute-start.6 = (f32[128,512]{1,0:T(8,128)S(1)}, f32[128,512]{1,0:T(8,128)S(1)}, u32[]{:S(2)}, u32[]{:S(2)}) collective-permute-start(f32[128,512]{1,0:T(8,128)S(1)} %collective-permute-done.1.refs_6_), channel_id=1, source_target_pairs={{0,224},{32,0},{64,32},{96,64},{128,96},{160,128},{192,160},{224,1... | collective-permute-start | bytes 786440 | tf_op jit(solution)/shard_map/ppermute | solution.py:492
  26.8 4.0 %collective-permute-start.7 = (f32[128,512]{1,0:T(8,128)S(1)}, f32[128,512]{1,0:T(8,128)S(1)}, u32[]{:S(2)}, u32[]{:S(2)}) collective-permute-start(f32[128,512]{1,0:T(8,128)S(1)} %copy-done.7), channel_id=1, source_target_pairs={{0,8},{1,9},{8,16},{9,17},{16,24},{17,25},{24,32},{25,33},{32,40},... | collective-permute-start | bytes 786440 | tf_op jit(solution)/shard_map/ppermute | solution.py:506
  30.8 1.0 collective-permute-done.5.refs_9_
  31.8 3.4 %collective-permute-done.7.e_in = f32[128,512]{1,0:T(8,128)S(1)} collective-permute-done((f32[128,512]{1,0:T(8,128)S(1)}, f32[128,512]{1,0:T(8,128)S(1)}, u32[]{:S(2)}, u32[]{:S(2)}) %collective-permute-start.7) | collective-permute-done | bytes 262176 | tf_op jit(solution)/shard_map/ppermute | solution.py:506
  35.3 3.4 %pick.2 = (f32[240,512]{1,0:T(8,128)S(1)}, f32[240,512]{1,0:T(8,128)S(1)}, f32[240,512]{1,0:T(8,128)S(1)}, f32[240,512]{1,0:T(8,128)S(1)}) custom-call(s32[2]{0:T(128)S(1)} %pad_add_fusion.1.pos.refs_0_, s32[96]{0:T(128)S(1)} %get-tuple-element.58.refs_1_, s32[96]{0:T(128)S(1)} %collective-permute-done.2.refs_2_, s32[96]{0:T(128)S(1)} %collective-permute-done.3.refs_3_, ...), custom_call_target="tpu_custom_call" | custom-call | bytes 3932160 | tf_op jit(solution)/shard_map/pick/pallas_call | solution.py:436
  38.7 2.0 %collective-permute-start.8 = (f32[240,512]{1,0:T(8,128)S(1)}, f32[240,512]{1,0:T(8,128)S(1)}, u32[]{:S(2)}, u32[]{:S(2)}) collective-permute-start(f32[240,512]{1,0:T(8,128)S(1)} %get-tuple-element.63), channel_id=1, source_target_pairs={{0,8},{8,16},{16,24},{24,0},{1,9},{9,17},{17,25},{25,1},{2,10},{10... | collective-permute-start | bytes 1474568 | tf_op jit(solution)/shard_map/ppermute | solution.py:516
  40.7 3.2 %collective-permute-start.11 = (f32[128,512]{1,0:T(8,128)S(1)}, f32[128,512]{1,0:T(8,128)S(1)}, u32[]{:S(2)}, u32[]{:S(2)}) collective-permute-start(f32[128,512]{1,0:T(8,128)S(1)} %collective-permute-done.6.refs_8_), channel_id=1, source_target_pairs={{0,224},{32,0},{64,32},{96,64},{128,96},{160,128},{192,160},{224,1... | collective-permute-start | bytes 786440 | tf_op jit(solution)/shard_map/ppermute | solution.py:492
  44.0 2.3 %collective-permute-start.9 = (f32[240,512]{1,0:T(8,128)S(1)}, f32[240,512]{1,0:T(8,128)S(1)}, u32[]{:S(2)}, u32[]{:S(2)}) collective-permute-start(f32[240,512]{1,0:T(8,128)S(1)} %get-tuple-element.64), channel_id=1, source_target_pairs={{0,16},{8,24},{16,0},{24,8},{1,17},{9,25},{17,1},{25,9},{2,18},{10... | collective-permute-start | bytes 1474568 | tf_op jit(solution)/shard_map/ppermute | solution.py:516
  46.2 2.5 %collective-permute-start.10 = (f32[240,512]{1,0:T(8,128)S(1)}, f32[240,512]{1,0:T(8,128)S(1)}, u32[]{:S(2)}, u32[]{:S(2)}) collective-permute-start(f32[240,512]{1,0:T(8,128)S(1)} %get-tuple-element.65), channel_id=1, source_target_pairs={{0,24},{8,0},{16,8},{24,16},{1,25},{9,1},{17,9},{25,17},{2,26},{10... | collective-permute-start | bytes 1474568 | tf_op jit(solution)/shard_map/ppermute | solution.py:516
  48.8 3.0 %collective-permute-start.14 = (f32[64,512]{1,0:T(8,128)S(1)}, f32[64,512]{1,0:T(8,128)S(1)}, u32[]{:S(2)}, u32[]{:S(2)}) collective-permute-start(f32[64,512]{1,0:T(8,128)S(1)} %slice.9), channel_id=1, source_target_pairs={{0,224},{32,0},{64,32},{96,64},{128,96},{160,128},{192,160},{224,1... | collective-permute-start | bytes 393224 | tf_op jit(solution)/shard_map/ppermute | solution.py:492
  51.8 0.3 collective-permute-start.13
  52.1 2.2 %collective-permute-done.14.refs_8_ = f32[64,512]{1,0:T(8,128)S(1)} collective-permute-done((f32[64,512]{1,0:T(8,128)S(1)}, f32[64,512]{1,0:T(8,128)S(1)}, u32[]{:S(2)}, u32[]{:S(2)}) %collective-permute-start.14) | collective-permute-done | bytes 131104 | tf_op jit(solution)/shard_map/ppermute | solution.py:492
  54.4 3.9 %collective-permute-done.13.refs_7_ = f32[64,512]{1,0:T(8,128)S(1)} collective-permute-done((f32[64,512]{1,0:T(8,128)S(1)}, f32[64,512]{1,0:T(8,128)S(1)}, u32[]{:S(2)}, u32[]{:S(2)}) %collective-permute-start.13) | collective-permute-done | bytes 131104 | tf_op jit(solution)/shard_map/ppermute | solution.py:492
  58.3 2.4 %pick.3 = (f32[144,512]{1,0:T(8,128)S(1)}, f32[144,512]{1,0:T(8,128)S(1)}, f32[144,512]{1,0:T(8,128)S(1)}, f32[144,512]{1,0:T(8,128)S(1)}) custom-call(s32[2]{0:T(128)S(1)} %pad_add_fusion.1.pos.refs_0_, s32[96]{0:T(128)S(1)} %get-tuple-element.58.refs_1_, s32[96]{0:T(128)S(1)} %collective-permute-done.2.refs_2_, s32[96]{0:T(128)S(1)} %collective-permute-done.3.refs_3_, ...), custom_call_target="tpu_custom_call" | custom-call | bytes 2359296 | tf_op jit(solution)/shard_map/pick/pallas_call | solution.py:436
  60.7 3.0 %collective-permute-start.15 = (f32[144,512]{1,0:T(8,128)S(1)}, f32[144,512]{1,0:T(8,128)S(1)}, u32[]{:S(2)}, u32[]{:S(2)}) collective-permute-start(f32[144,512]{1,0:T(8,128)S(1)} %get-tuple-element.69), channel_id=1, source_target_pairs={{0,8},{8,16},{16,24},{24,0},{1,9},{9,17},{17,25},{25,1},{2,10},{10... | collective-permute-start | bytes 884744 | tf_op jit(solution)/shard_map/ppermute | solution.py:516
  63.6 1.8 %collective-permute-start.17 = (f32[144,512]{1,0:T(8,128)S(1)}, f32[144,512]{1,0:T(8,128)S(1)}, u32[]{:S(2)}, u32[]{:S(2)}) collective-permute-start(f32[144,512]{1,0:T(8,128)S(1)} %get-tuple-element.71), channel_id=1, source_target_pairs={{0,24},{8,0},{16,8},{24,16},{1,25},{9,1},{17,9},{25,17},{2,26},{10... | collective-permute-start | bytes 884744 | tf_op jit(solution)/shard_map/ppermute | solution.py:516
  65.4 1.3 collective-permute-done.9.refs_2_
  66.8 3.2 %collective-permute-done.10.refs_3_ = f32[240,512]{1,0:T(8,128)S(1)} collective-permute-done((f32[240,512]{1,0:T(8,128)S(1)}, f32[240,512]{1,0:T(8,128)S(1)}, u32[]{:S(2)}, u32[]{:S(2)}) %collective-permute-start.10) | collective-permute-done | bytes 491552 | tf_op jit(solution)/shard_map/ppermute | solution.py:516
  70.0 3.1 %collective-permute-done.15.refs_5_ = f32[144,512]{1,0:T(8,128)S(1)} collective-permute-done((f32[144,512]{1,0:T(8,128)S(1)}, f32[144,512]{1,0:T(8,128)S(1)}, u32[]{:S(2)}, u32[]{:S(2)}) %collective-permute-start.15) | collective-permute-done | bytes 294944 | tf_op jit(solution)/shard_map/ppermute | solution.py:516
  73.1 3.5 %collective-permute-done.16.refs_6_ = f32[144,512]{1,0:T(8,128)S(1)} collective-permute-done((f32[144,512]{1,0:T(8,128)S(1)}, f32[144,512]{1,0:T(8,128)S(1)}, u32[]{:S(2)}, u32[]{:S(2)}) %collective-permute-start.16) | collective-permute-done | bytes 294944 | tf_op jit(solution)/shard_map/ppermute | solution.py:516
  76.6 2.4 %collective-permute-done.17.refs_7_ = f32[144,512]{1,0:T(8,128)S(1)} collective-permute-done((f32[144,512]{1,0:T(8,128)S(1)}, f32[144,512]{1,0:T(8,128)S(1)}, u32[]{:S(2)}, u32[]{:S(2)}) %collective-permute-start.17) | collective-permute-done | bytes 294944 | tf_op jit(solution)/shard_map/ppermute | solution.py:516
  79.0 2.0 %send.1 = f32[768,512]{1,0:T(8,128)} custom-call(s32[48]{0:T(128)S(1)} %get-tuple-element.45.row, f32[240,512]{1,0:T(8,128)S(1)} %get-tuple-element.62.refs_0_, f32[240,512]{1,0:T(8,128)S(1)} %collective-permute-done.8.refs_1_, f32[240,512]{1,0:T(8,128)S(1)} %collective-permute-done.9.refs_2_, f32[240,512]{1,0:T(8,128)S(1)} %collective-permute-done.10.refs_3_, ...), custom_call_target="tpu_custom_call" | custom-call | bytes 6291456 | tf_op jit(solution)/shard_map/send/pallas_call | solution.py:459
  81.0 4.3 %all-to-all-start = ((f32[8,96,512]{2,1,0:T(8,128)}), f32[8,96,512]{2,1,0:T(8,128)S(1)}, u32[]{:S(2)}, u32[]{:S(2)}) async-start(f32[8,96,512]{2,1,0:T(8,128)} %bitcast.10), calls=%async_computation | async-start | bytes 3145728 | tf_op jit(solution)/shard_map/all_to_all | solution.py:526
  85.3 0.5 collective-permute-start.18
  85.8 0.7 copy.14.local_ref
  86.5 17.4 %all-gather.5.cloned.1.call-done = f32[2048,512]{1,0:T(8,128)} async-done(((f32[256,512]{1,0:T(8,128)}), f32[2048,512]{1,0:T(8,128)}) %all-gather.5.cloned.1.call-update) | async-done | bytes 4194320 | tf_op jit(solution)/shard_map/all_gather | solution.py:504
  103.9 5.0 %prep.1 = (bf16[2,512,1024]{2,1,0:T(8,128)(2,1)}, bf16[2,1024,512]{2,1,0:T(8,128)(2,1)}) custom-call(f32[8,256,512]{2,1,0:T(8,128)} %bitcast.21), custom_call_target="tpu_custom_call" | custom-call | flops 10000000 | bytes 8388608 | tf_op jit(solution)/shard_map/prep/pallas_call | solution.py:281
  108.9 0.7 copy-done.8
  109.6 14.7 %near.1 = (f32[128,512]{1,0:T(8,128)}, bf16[2,4,256,512]{3,2,1,0:T(8,128)(2,1)}, bf16[2,4,128,512]{3,2,1,0:T(8,128)(2,1)}, bf16[2,512,512]{2,1,0:T(8,128)(2,1)}, f32[4,256,128]{2,1,0:T(8,128)}) custom-call(s32[3]{0:T(128)} %pad_add_fusion.pos, s32[8,3]{1,0:T(8,128)} %copy.14.local_ref, s32[8]{0:T(128)} %virt_ref.1, s32[256]{0:T(256)} %count_ref.3, ...), custom_call_target="tpu_custom_call" | custom-call | flops 6000000000 | bytes 16777216 | tf_op jit(solution)/shard_map/near/pallas_call | solution.py:256
  124.4 1.2 copy-done.4
  125.5 13.8 %far.1 = f32[512,128]{1,0:T(8,128)} custom-call(s32[3]{0:T(128)} %pad_add_fusion.pos, s32[8,6]{1,0:T(8,128)} %exp_ref.3, s32[256]{0:T(256)} %count_ref.3, f32[768,512]{1,0:T(8,128)} %bitcast.22, bf16[2,4,256,512]{3,2,1,0:T(8,128)(2,1)} %get-tuple-element.77.q_hbm, f32[4,256,128]{2,1,0:T(8,128)} %get-tuple-element.78.s_hbm, ...), custom_call_target="tpu_custom_call" | custom-call | flops 6000000000 | bytes 16777216 | tf_op jit(solution)/shard_map/far/pallas_call | solution.py:358
  139.3 10.9 %all_to_all.22 = f32[8,64,128]{2,1,0:T(8,128)S(1)} all-to-all(f32[8,64,128]{2,1,0:T(8,128)} %bitcast.23), channel_id=1, replica_groups=mesh['z'=8,'x'=4,'y'=4,'c'=2] {'y','c'}, dimensions={0} | all-to-all | bytes 524288 | tf_op jit(solution)/shard_map/all_to_all | solution.py:533
  150.2 2.1 %place.1 = f32[64,1024]{1,0:T(8,128)} custom-call(s32[3]{0:T(128)S(1)} %copy-done.2, f32[512,128]{1,0:T(8,128)S(1)} %bitcast.17, s32[8,128]{1,0:T(8,128)S(1)} %bitcast.20), custom_call_target="tpu_custom_call" | custom-call | flops 400000000 | bytes 1048576 | tf_op jit(solution)/shard_map/place/pallas_call | solution.py:388
  (32 shorter events, 0.1 us)
Async XLA Ops:
  6.5 6.3 %copy-start.1 = (s32[8,6]{1,0:T(8,128)S(1)}, s32[8,6]{1,0:T(8,128)}, u32[]{:S(2)}) copy-start(s32[8,6]{1,0:T(8,128)} %exp_ref.3) | copy-start | bytes 580
  6.5 79.9 %all-gather.3.cloned.1.call-start = ((), (), s32[]{:S(2)}) async-start(), calls=%async_computation.2 | async-start | bytes 4718592 | tf_op jit(solution)/shard_map/all_gather | solution.py:503
  10.6 16.2 %copy-start.7 = (f32[128,512]{1,0:T(8,128)S(1)}, f32[128,512]{1,0:T(8,128)}, u32[]{:S(2)}) copy-start(f32[128,512]{1,0:T(8,128)} %get-tuple-element.53) | copy-start | bytes 786436
  10.6 24.7 %copy-start = (f32[128,512]{1,0:T(8,128)S(1)}, f32[128,512]{1,0:T(8,128)}, u32[]{:S(2)}) copy-start(f32[128,512]{1,0:T(8,128)} %get-tuple-element.46.refs_5_) | copy-start | bytes 786436
  10.6 10.8 %collective-permute-start.1 = (f32[128,512]{1,0:T(8,128)}, f32[128,512]{1,0:T(8,128)S(1)}, u32[]{:S(2)}, u32[]{:S(2)}) collective-permute-start(f32[128,512]{1,0:T(8,128)} %get-tuple-element.46.refs_5_), channel_id=1, source_target_pairs={{0,224},{32,0},{64,32},{96,64},{128,96},{160,128},{192,160},{224,1... | collective-permute-start | bytes 786440 | tf_op jit(solution)/shard_map/ppermute | solution.py:492
  10.8 12.1 %collective-permute-start = (f32[128,512]{1,0:T(8,128)}, f32[128,512]{1,0:T(8,128)S(1)}, u32[]{:S(2)}, u32[]{:S(2)}) collective-permute-start(f32[128,512]{1,0:T(8,128)} %get-tuple-element.46.refs_5_), channel_id=1, source_target_pairs={{0,32},{32,64},{64,96},{96,128},{128,160},{160,192},{192,224},{224... | collective-permute-start | bytes 786440 | tf_op jit(solution)/shard_map/ppermute | solution.py:492
  15.1 5.5 %collective-permute-start.4 = (s32[96]{0:T(128)S(1)}, s32[96]{0:T(128)S(1)}, u32[]{:S(2)}, u32[]{:S(2)}) collective-permute-start(s32[96]{0:T(128)S(1)} %get-tuple-element.58.refs_1_), channel_id=1, source_target_pairs={{0,8},{8,16},{16,24},{24,0},{1,9},{9,17},{17,25},{25,1},{2,10},{10... | collective-permute-start | bytes 1160 | tf_op jit(solution)/shard_map/ppermute | solution.py:499
  16.4 5.0 %collective-permute-start.3 = (s32[96]{0:T(128)S(1)}, s32[96]{0:T(128)S(1)}, u32[]{:S(2)}, u32[]{:S(2)}) collective-permute-start(s32[96]{0:T(128)S(1)} %get-tuple-element.58.refs_1_), channel_id=1, source_target_pairs={{0,16},{8,24},{16,0},{24,8},{1,17},{9,25},{17,1},{25,9},{2,18},{10... | collective-permute-start | bytes 1160 | tf_op jit(solution)/shard_map/ppermute | solution.py:499
  17.2 4.2 %collective-permute-start.2 = (s32[96]{0:T(128)S(1)}, s32[96]{0:T(128)S(1)}, u32[]{:S(2)}, u32[]{:S(2)}) collective-permute-start(s32[96]{0:T(128)S(1)} %get-tuple-element.58.refs_1_), channel_id=1, source_target_pairs={{0,24},{8,0},{16,8},{24,16},{1,25},{9,1},{17,9},{25,17},{2,26},{10... | collective-permute-start | bytes 1160 | tf_op jit(solution)/shard_map/ppermute | solution.py:499
  23.0 80.9 %all-gather.5.cloned.1.call-start = ((), (), s32[]{:S(2)}) async-start(), calls=%async_computation.3 | async-start | bytes 4718592 | tf_op jit(solution)/shard_map/all_gather | solution.py:504
  23.7 8.1 %collective-permute-start.5 = (f32[128,512]{1,0:T(8,128)S(1)}, f32[128,512]{1,0:T(8,128)S(1)}, u32[]{:S(2)}, u32[]{:S(2)}) collective-permute-start(f32[128,512]{1,0:T(8,128)S(1)} %collective-permute-done.refs_7_), channel_id=1, source_target_pairs={{0,32},{32,64},{64,96},{96,128},{128,160},{160,192},{192,224},{224... | collective-permute-start | bytes 786440 | tf_op jit(solution)/shard_map/ppermute | solution.py:492
  24.2 7.6 %collective-permute-start.6 = (f32[128,512]{1,0:T(8,128)S(1)}, f32[128,512]{1,0:T(8,128)S(1)}, u32[]{:S(2)}, u32[]{:S(2)}) collective-permute-start(f32[128,512]{1,0:T(8,128)S(1)} %collective-permute-done.1.refs_6_), channel_id=1, source_target_pairs={{0,224},{32,0},{64,32},{96,64},{128,96},{160,128},{192,160},{224,1... | collective-permute-start | bytes 786440 | tf_op jit(solution)/shard_map/ppermute | solution.py:492
  26.8 8.5 %collective-permute-start.7 = (f32[128,512]{1,0:T(8,128)S(1)}, f32[128,512]{1,0:T(8,128)S(1)}, u32[]{:S(2)}, u32[]{:S(2)}) collective-permute-start(f32[128,512]{1,0:T(8,128)S(1)} %copy-done.7), channel_id=1, source_target_pairs={{0,8},{1,9},{8,16},{9,17},{16,24},{17,25},{24,32},{25,33},{32,40},... | collective-permute-start | bytes 786440 | tf_op jit(solution)/shard_map/ppermute | solution.py:506
  35.3 50.0 %copy-start.6 = (f32[128,512]{1,0:T(8,128)}, f32[128,512]{1,0:T(8,128)S(1)}, u32[]{:S(2)}) copy-start(f32[128,512]{1,0:T(8,128)S(1)} %collective-permute-done.7.e_in) | copy-start | bytes 786436
  38.7 24.9 %collective-permute-start.8 = (f32[240,512]{1,0:T(8,128)S(1)}, f32[240,512]{1,0:T(8,128)S(1)}, u32[]{:S(2)}, u32[]{:S(2)}) collective-permute-start(f32[240,512]{1,0:T(8,128)S(1)} %get-tuple-element.63), channel_id=1, source_target_pairs={{0,8},{8,16},{16,24},{24,0},{1,9},{9,17},{17,25},{25,1},{2,10},{10... | collective-permute-start | bytes 1474568 | tf_op jit(solution)/shard_map/ppermute | solution.py:516
  40.7 8.0 %collective-permute-start.11 = (f32[128,512]{1,0:T(8,128)S(1)}, f32[128,512]{1,0:T(8,128)S(1)}, u32[]{:S(2)}, u32[]{:S(2)}) collective-permute-start(f32[128,512]{1,0:T(8,128)S(1)} %collective-permute-done.6.refs_8_), channel_id=1, source_target_pairs={{0,224},{32,0},{64,32},{96,64},{128,96},{160,128},{192,160},{224,1... | collective-permute-start | bytes 786440 | tf_op jit(solution)/shard_map/ppermute | solution.py:492
  44.0 7.9 %collective-permute-start.12 = (f32[128,512]{1,0:T(8,128)S(1)}, f32[128,512]{1,0:T(8,128)S(1)}, u32[]{:S(2)}, u32[]{:S(2)}) collective-permute-start(f32[128,512]{1,0:T(8,128)S(1)} %collective-permute-done.5.refs_9_), channel_id=1, source_target_pairs={{0,32},{32,64},{64,96},{96,128},{128,160},{160,192},{192,224},{224... | collective-permute-start | bytes 786440 | tf_op jit(solution)/shard_map/ppermute | solution.py:492
  44.0 22.8 %collective-permute-start.9 = (f32[240,512]{1,0:T(8,128)S(1)}, f32[240,512]{1,0:T(8,128)S(1)}, u32[]{:S(2)}, u32[]{:S(2)}) collective-permute-start(f32[240,512]{1,0:T(8,128)S(1)} %get-tuple-element.64), channel_id=1, source_target_pairs={{0,16},{8,24},{16,0},{24,8},{1,17},{9,25},{17,1},{25,9},{2,18},{10... | collective-permute-start | bytes 1474568 | tf_op jit(solution)/shard_map/ppermute | solution.py:516
  46.2 23.8 %collective-permute-start.10 = (f32[240,512]{1,0:T(8,128)S(1)}, f32[240,512]{1,0:T(8,128)S(1)}, u32[]{:S(2)}, u32[]{:S(2)}) collective-permute-start(f32[240,512]{1,0:T(8,128)S(1)} %get-tuple-element.65), channel_id=1, source_target_pairs={{0,24},{8,0},{16,8},{24,16},{1,25},{9,1},{17,9},{25,17},{2,26},{10... | collective-permute-start | bytes 1474568 | tf_op jit(solution)/shard_map/ppermute | solution.py:516
  48.8 5.6 %collective-permute-start.14 = (f32[64,512]{1,0:T(8,128)S(1)}, f32[64,512]{1,0:T(8,128)S(1)}, u32[]{:S(2)}, u32[]{:S(2)}) collective-permute-start(f32[64,512]{1,0:T(8,128)S(1)} %slice.9), channel_id=1, source_target_pairs={{0,224},{32,0},{64,32},{96,64},{128,96},{160,128},{192,160},{224,1... | collective-permute-start | bytes 393224 | tf_op jit(solution)/shard_map/ppermute | solution.py:492
  51.8 6.4 %collective-permute-start.13 = (f32[64,512]{1,0:T(8,128)S(1)}, f32[64,512]{1,0:T(8,128)S(1)}, u32[]{:S(2)}, u32[]{:S(2)}) collective-permute-start(f32[64,512]{1,0:T(8,128)S(1)} %slice.8), channel_id=1, source_target_pairs={{0,32},{32,64},{64,96},{96,128},{128,160},{160,192},{192,224},{224... | collective-permute-start | bytes 393224 | tf_op jit(solution)/shard_map/ppermute | solution.py:492
  60.7 12.4 %collective-permute-start.15 = (f32[144,512]{1,0:T(8,128)S(1)}, f32[144,512]{1,0:T(8,128)S(1)}, u32[]{:S(2)}, u32[]{:S(2)}) collective-permute-start(f32[144,512]{1,0:T(8,128)S(1)} %get-tuple-element.69), channel_id=1, source_target_pairs={{0,8},{8,16},{16,24},{24,0},{1,9},{9,17},{17,25},{25,1},{2,10},{10... | collective-permute-start | bytes 884744 | tf_op jit(solution)/shard_map/ppermute | solution.py:516
  63.6 12.9 %collective-permute-start.16 = (f32[144,512]{1,0:T(8,128)S(1)}, f32[144,512]{1,0:T(8,128)S(1)}, u32[]{:S(2)}, u32[]{:S(2)}) collective-permute-start(f32[144,512]{1,0:T(8,128)S(1)} %get-tuple-element.70), channel_id=1, source_target_pairs={{0,16},{8,24},{16,0},{24,8},{1,17},{9,25},{17,1},{25,9},{2,18},{10... | collective-permute-start | bytes 884744 | tf_op jit(solution)/shard_map/ppermute | solution.py:516
  63.6 15.3 %collective-permute-start.17 = (f32[144,512]{1,0:T(8,128)S(1)}, f32[144,512]{1,0:T(8,128)S(1)}, u32[]{:S(2)}, u32[]{:S(2)}) collective-permute-start(f32[144,512]{1,0:T(8,128)S(1)} %get-tuple-element.71), channel_id=1, source_target_pairs={{0,24},{8,0},{16,8},{24,16},{1,25},{9,1},{17,9},{25,17},{2,26},{10... | collective-permute-start | bytes 884744 | tf_op jit(solution)/shard_map/ppermute | solution.py:516
  81.0 4.8 %copy-start.5 = (s32[8,3]{0,1:T(4,128)S(1)}, s32[8,3]{0,1:T(4,128)}, u32[]{:S(2)}) copy-start(s32[8,3]{0,1:T(4,128)} %param.16) | copy-start | bytes 292
  81.0 43.4 %all-to-all-start = ((f32[8,96,512]{2,1,0:T(8,128)}), f32[8,96,512]{2,1,0:T(8,128)S(1)}, u32[]{:S(2)}, u32[]{:S(2)}) async-start(f32[8,96,512]{2,1,0:T(8,128)} %bitcast.10), calls=%async_computation | async-start | bytes 3145728 | tf_op jit(solution)/shard_map/all_to_all | solution.py:526
  85.3 23.6 %collective-permute-start.18 = (f32[128,512]{1,0:T(8,128)S(1)}, f32[128,512]{1,0:T(8,128)S(1)}, u32[]{:S(2)}, u32[]{:S(2)}) collective-permute-start(f32[128,512]{1,0:T(8,128)S(1)} %collective-permute-done.7.e_in), channel_id=1, source_target_pairs={{0,1},{1,0},{2,3},{3,2},{4,5},{5,4},{6,7},{7,6},{8,9},{9,8},{10,11... | collective-permute-start | bytes 786440 | tf_op jit(solution)/shard_map/ppermute | solution.py:495
  108.9 0.7 copy-start.8
  124.3 1.2 copy-start.4
  125.5 24.7 %copy-start.2 = (s32[3]{0:T(128)S(1)}, s32[3]{0:T(128)}, u32[]{:S(2)}) copy-start(s32[3]{0:T(128)} %pad_add_fusion.pos) | copy-start | bytes 40
  125.5 24.7 %copy-start.3 = (s32[1024]{0:T(1024)S(1)}, s32[1024]{0:T(1024)}, u32[]{:S(2)}) copy-start(s32[1024]{0:T(1024)} %param.14) | copy-start | bytes 12292
Sparse Core Ops, SparseCore 0:
  23.1 36.8 all-gather.2
  61.9 41.9 all-gather.4

commit v2 on v1

--- a/solution.py
+++ b/solution.py
@@ -26,7 +26,7 @@
 NT = (((1,), (1,)), ((), ()))
 NN = (((1,), (0,)), ((), ()))
 
-GROUPS = ((0, 1, 7, 2, 6), (3, 5, 4))
+GROUPS = ((0, 1, 7), (2, 6), (3, 5, 4))
 
 
 def split2(v):
@@ -117,7 +117,13 @@
     )(pos, order, nodes)
 
 
-def index_kernel(pos, exp_ref, table, row, seen, starts, widths):
+def setup_kernel(pos, exp_ref, q, k, v, o, up, down, table, row, att, ffw, seen, starts, widths, sems):
+    pairs = [(w, att.at[i * HD:(i + 1) * HD, :]) for i, w in enumerate((q, k, v, o))]
+    pairs.append((down, ffw.at[:CL, :]))
+    pairs += [(up.at[j * CL:(j + 1) * CL, :], ffw.at[CL:, j * CL:(j + 1) * CL]) for j in range(4)]
+    copies = [pltpu.make_async_copy(src, dst, sems.at[i]) for i, (src, dst) in enumerate(pairs)]
+    for copy in copies:
+        copy.start()
     z, x = pos[0], pos[1]
     start = 0
     for group in GROUPS:
@@ -125,13 +131,10 @@
             starts[s] = start + p * CAP
             widths[s] = len(group) * CAP
         start += NX * len(group) * CAP
-
-    def clear(i, carry):
+    for i in range(NX * NZ * CAP):
         table[i] = 0
-        seen[lax.bitwise_and(i, NZ * NX - 1)] = 0
-        return carry
-
-    lax.fori_loop(0, NX * NZ * CAP, clear, 0)
+    for i in range(NZ * NX):
+        seen[i] = 0
 
     def place(i, carry):
         for e in range(NE):
@@ -147,49 +150,30 @@
         return carry
 
     lax.fori_loop(0, CD, place, 0)
-
-
-def index_call(pos, exp_blocks):
-    return pl.pallas_call(
-        index_kernel,
-        out_shape=[sds(NX * NZ * CAP, dtype=jnp.int32), sds(CD * NE, dtype=jnp.int32)],
-        in_specs=[sspec()] * 2,
-        out_specs=[sspec()] * 2,
-        scratch_shapes=[pltpu.SMEM((NZ * NX,), jnp.int32), pltpu.SMEM((NZ,), jnp.int32), pltpu.SMEM((NZ,), jnp.int32)],
-        compiler_params=params(2),
-        cost_estimate=cost(1000, 4096),
-        name="index",
-    )(pos, exp_blocks)
-
-
-def pack_kernel(q, k, v, o, up, down, att, ffw, sems):
-    pairs = [(w, att.at[i * HD:(i + 1) * HD, :]) for i, w in enumerate((q, k, v, o))]
-    pairs.append((down, ffw.at[:CL, :]))
-    pairs += [(up.at[j * CL:(j + 1) * CL, :], ffw.at[CL:, j * CL:(j + 1) * CL]) for j in range(4)]
-    copies = [pltpu.make_async_copy(src, dst, sems.at[i]) for i, (src, dst) in enumerate(pairs)]
-    for copy in copies:
-        copy.start()
     for copy in copies:
         copy.wait()
 
 
-def pack_call(*w):
-    return pl.pallas_call(
-        pack_kernel,
-        out_shape=[sds(2 * CL, D), sds(2 * CL, D)],
-        in_specs=[hspec()] * 6,
-        out_specs=[vspec()] * 2,
-        scratch_shapes=[pltpu.SemaphoreType.DMA((9,))],
+def setup_call(pos, exp_blocks, *w):
+    return pl.pallas_call(
+        setup_kernel,
+        out_shape=[sds(NX * NZ * CAP, dtype=jnp.int32), sds(CD * NE, dtype=jnp.int32),
+                   sds(2 * CL, D), sds(2 * CL, D)],
+        in_specs=[sspec()] * 2 + [hspec()] * 6,
+        out_specs=[sspec()] * 2 + [vspec()] * 2,
+        scratch_shapes=[pltpu.SMEM((NZ * NX,), jnp.int32), pltpu.SMEM((NZ,), jnp.int32), pltpu.SMEM((NZ,), jnp.int32),
+                        pltpu.SemaphoreType.DMA((9,))],
         compiler_params=params(60),
-        cost_estimate=cost(0, 2 << 20),
-        name="pack",
-    )(*w)
-
-
-def near_kernel(pos, local_ref, virt_ref, count_ref, order_ref, nodes_ref, e_in, e_other, virtual_ref, w_hbm,
-                x_out, q_out, v_out, o_out, state, kh, kl, w, sem):
-    fetch = pltpu.make_async_copy(w_hbm, w, sem)
-    fetch.start()
+        cost_estimate=cost(1000, 2 << 20),
+        name="setup",
+    )(pos, exp_blocks, *w)
+
+
+def near_kernel(pos, local_ref, virt_ref, count_ref, order_ref, nodes_ref, e_in, e_other, virtual_ref, mine_hbm, other_hbm,
+                x_out, q_out, v_out, o_out, state, kh, kl, mine, other, sems):
+    fetch = [pltpu.make_async_copy(mine_hbm, mine, sems.at[0]), pltpu.make_async_copy(other_hbm, other, sems.at[1])]
+    for copy in fetch:
+        copy.start()
     base, head, c = pos[0], pos[1], pos[2]
     first = lax.shift_right_logical(base, 7)
 
@@ -221,9 +205,11 @@
     lanes = lax.broadcasted_iota(jnp.int32, (CL, 2 * HD), 1)
     lowq = lanes < HD
     xh, xl = split2(x)
-    fetch.wait()
+    for copy in fetch:
+        copy.wait()
     for at in range(NY):
-        left, right = w[2 * at], w[2 * at + 1]
+        a, b = mine[at * 2 * CL:(at + 1) * 2 * CL, :], other[at * 2 * CL:(at + 1) * 2 * CL, :]
+        left, right = jnp.where(c == 0, a, b), jnp.where(c == 0, b, a)
         wq, wk, wv, wo = (
             split2(jnp.concatenate([left[i * HD:(i + 1) * HD], right[i * HD:(i + 1) * HD]], 0))
             for i in range(4))
@@ -256,37 +242,38 @@
     return pl.pallas_call(
         near_kernel,
         out_shape=shapes,
-        in_specs=[sspec()] * len(scalars) + [vspec()] * (len(arrays) - 1) + [hspec()],
+        in_specs=[sspec()] * len(scalars) + [vspec()] * (len(arrays) - 2) + [hspec()] * 2,
         out_specs=[vspec()] * len(shapes),
         scratch_shapes=[pltpu.VMEM((LK, D), BF), pltpu.VMEM((LK, D), BF), pltpu.VMEM(arrays[-1].shape, F32),
-                        pltpu.SemaphoreType.DMA],
+                        pltpu.VMEM(arrays[-1].shape, F32), pltpu.SemaphoreType.DMA((2,))],
         compiler_params=params(60),
         cost_estimate=cost(6 * 10**9, 16 << 20, 1 << 20),
         name="near",
     )(*scalars, *arrays)
 
 
-def prep_kernel(w, u_out, d_out):
+def prep_kernel(mine, other, u_out, d_out):
     for i in range(8):
+        w, at = (mine, other)[i // NY], i % NY * 2 * CL
         rows = slice(i * CL, (i + 1) * CL)
-        d_out[0, rows, :], d_out[1, rows, :] = split2(w[i, :CL, :])
-        hi, lo = split2(w[i, CL:, :])
+        d_out[0, rows, :], d_out[1, rows, :] = split2(w[at:at + CL, :])
+        hi, lo = split2(w[at + CL:at + 2 * CL, :])
         for j in range(4):
             cols = slice(j * CL, (j + 1) * CL)
             u_out[0, cols, rows] = hi[:, cols]
             u_out[1, cols, rows] = lo[:, cols]
 
 
-def prep_call(weights):
+def prep_call(mine, other):
     return pl.pallas_call(
         prep_kernel,
         out_shape=[sds(2, D, FF, dtype=BF), sds(2, FF, D, dtype=BF)],
-        in_specs=[vspec()],
+        in_specs=[vspec()] * 2,
         out_specs=[vspec()] * 2,
         compiler_params=params(60),
         cost_estimate=cost(10**7, 8 << 20),
         name="prep",
-    )(weights)
+    )(mine, other)
 
 
 def far_kernel(pos, exp_ref, count_ref, xe_ref, q_hbm, s_hbm, v_hbm, x_hbm, o_hbm, u_hbm, d_hbm,
@@ -397,7 +384,7 @@
 
 
 def pick_kernel(group, pos, *refs):
-    tables, srcs, outs, sem = refs[:NX], refs[NX:-NX - 1], refs[-NX - 1:-1], refs[-1]
+    tables, srcs, outs = refs[:NX], refs[NX:-NX], refs[-NX:]
     z = pos[0]
     parts, at = [], 0
     for s in group:
@@ -405,30 +392,17 @@
         parts.append(srcs[at:at + size])
         at += size
 
-    def send(src, at, out, to):
-        pltpu.make_async_copy(src.at[pl.ds(pl.multiple_of(at, PR), PR), :], out.at[to:to + PR, :], sem).start()
-
     for k, out in enumerate(outs):
         for i, s in enumerate(group):
             src = parts[i]
             for j in range(CAP):
                 b = tables[k][(k * NZ + lax.bitwise_and(z + s, NZ - 1)) * CAP + j]
-                to = (i * CAP + j) * PR
                 if len(src) == 1:
-                    send(src[0], b * PR, out, to)
+                    block = src[0][pl.ds(pl.multiple_of(b * PR, PR), PR), :]
                 else:
-                    at = lax.bitwise_and(b, CD // 2 - 1) * PR
-
-                    @pl.when(b < CD // 2)
-                    def _(at=at, to=to, src=src, out=out):
-                        send(src[0], at, out, to)
-
-                    @pl.when(b >= CD // 2)
-                    def _(at=at, to=to, src=src, out=out):
-                        send(src[1], at, out, to)
-
-    for out in outs:
-        pltpu.make_async_copy(out, out, sem).wait()
+                    at = pl.multiple_of(lax.bitwise_and(b, CD // 2 - 1) * PR, PR)
+                    block = jnp.where(b < CD // 2, src[0][pl.ds(at, PR), :], src[1][pl.ds(at, PR), :])
+                out[(i * CAP + j) * PR:(i * CAP + j + 1) * PR, :] = block
 
 
 def pick_call(group, pos, tables, srcs):
@@ -438,7 +412,6 @@
         out_shape=[sds(rows, D)] * NX,
         in_specs=[sspec()] * (1 + NX) + [vspec()] * len(srcs),
         out_specs=[vspec()] * NX,
-        scratch_shapes=[pltpu.SemaphoreType.DMA],
         compiler_params=params(8),
         cost_estimate=cost(0, NX * rows * D * 8),
         name="pick",
@@ -495,40 +468,45 @@
         return [lax.ppermute(t, "c", SWAP) for t in arrays]
 
     up, down = both_z(piece, piece)
-    table, row = index_call(zx, exp_blocks)
+    table, row, wa, wb = setup_call(zx, exp_blocks, w_query.T, w_key.T, w_value.T, w_out.T, w_up, w_down)
     tables = [table] + [lax.ppermute(table, "x", ring(NX, -k)) for k in range(1, NX)]
     held = {0: (piece,), 7: (up,), 1: (down,)}
-    wa, wb = pack_call(w_query.T, w_key.T, w_value.T, w_out.T, w_up, w_down)
     up, down, edge, wa, wb, *tables = tie((up, down, edge, wa, wb, *tables))
-    wa = lax.all_gather(wa, ("y", "c"), axis=0, tiled=True).reshape(CD, 2 * CL, D)
-    wb = lax.all_gather(wb, ("y", "c"), axis=0, tiled=True).reshape(CD, 2 * CL, D)
-
+    wa = lax.all_gather(wa, "y", axis=0, tiled=True)
+    wb = lax.all_gather(wb, "y", axis=0, tiled=True)
+
+    def pick(group):
+        return pick_call(group, zx, tables, [t for s in group for t in held[s]])
+
+    def exchange(blocks):
+        return [blocks[0]] + [lax.ppermute(blocks[k], "x", ring(NX, k)) for k in (1, 2, 3)]
+
+    one = pick(GROUPS[0])
+    up, down = both_z(up, down)
+    held[6], held[2] = (up,), (down,)
+    up, down, *_ = tie((up, down, *one))
+    one = exchange(one)
+    two = pick(GROUPS[1])
+    up, down = both_z(up, down)
+    held[5], held[3] = (up,), (down,)
+    up, down, *_ = tie((up, down, *one, *two))
+    held[4] = both_z(up[:half], down[half:])
+    arrived = one + exchange(two) + exchange(pick(GROUPS[2]))
+
+    sending = send_call(row, arrived)
+    xe = lax.all_to_all(sending, ("y", "c"), 0, 0, tiled=True)
+
+    _, wa, wb, edge, pos_late = tie((sending, wa, wb, edge, pos))
     e_in = lax.ppermute(edge, ("z", "x", "y", "c"), [
         (i * CD + h, (i + s) * CD + h)
         for s, hs in ((1, (0, 1)), (-1, (6, 7)))
         for i in range(NZ * NX) if 0 <= i + s < NZ * NX for h in hs])
-    up, down = both_z(up, down)
-    held[6], held[2] = (up,), (down,)
-    up, down, e_in, *tables = tie((up, down, e_in, *tables))
-
-    def exchange(group):
-        blocks = pick_call(group, zx, tables, [t for s in group for t in held[s]])
-        return [blocks[0]] + [lax.ppermute(blocks[k], "x", ring(NX, k)) for k in (1, 2, 3)]
-
-    up, down = both_z(up, down)
-    near_x = exchange(GROUPS[0])
-    held[5], held[3] = (up,), (down,)
-    held[4] = both_z(up[:half], down[half:])
-    far_x = exchange(GROUPS[1])
-    (e_other,) = swap(e_in)
-
-    sending = send_call(row, near_x + far_x)
-    xe = lax.all_to_all(sending, ("y", "c"), 0, 0, tiled=True)
-    _, wa, wb, pos_late = tie((sending, wa, wb, pos))
-
+    e_other, wa_other, wb_other = swap(e_in, wa, wb)
     x_own, q, wv, wo, state = near_call(
-        (pos_late, local_blocks, virt_blocks, node_count), (order, node_feats, e_in, e_other, virt_feats, wa))
-    wu, wd = prep_call(wb)
+        (pos_late, local_blocks, virt_blocks, node_count),
+        (order, node_feats, e_in, e_other, virt_feats, wa, wa_other))
+    state, wb, wb_other = tie((state, wb, wb_other))
+    wu, wd = prep_call(wb, wb_other)
     result = far_call((pos, exp_blocks, node_count), (xe, q, state, wv, x_own, wo, wu, wd))
     received = lax.all_to_all(result, ("y", "c"), 0, 0, tiled=True)
     return place_call(pos, received, order).T

time: 160 us -> 172 us (1.075)
  the two profiles are of different devices: /device:TPU:36 before, /device:TPU:1 now
where the time goes in v2:
time: 172 us; the launch traced here: 170 us
  waiting for transfers between devices  51.2 us (30%)
  Pallas kernels  46.5 us (27%)
  starting transfers between devices  42 us (24%)
  between operations  13.6 us (8%)
  blocking collectives  12.1 us (7%)
  local copies, waits for them, and re-layouts  3.34 us (2%)
    ppermute x9, waiting for transfers between devices, exchange(): lax.ppermute(blocks[k], 'x', ring(NX, k))  22.9 us
    all_gather x1, waiting for transfers between devices, shards(): wb = lax.all_gather(wb, 'y', axis=0, tiled=True)  15.5 us
    pallas_call x1, Pallas kernels, near_call(): pl.pallas_call(near_kernel, out_shape=shapes, in_specs=[sspec()] * len(sc...  15 us
    ppermute x9, starting transfers between devices, exchange(): lax.ppermute(blocks[k], 'x', ring(NX, k))  14.6 us
    pallas_call x1, Pallas kernels, far_call(): pl.pallas_call(far_kernel, out_shape=sds(D, CL), in_specs=[sspec()] * len...  13.8 us
    ppermute x4, starting transfers between devices, both_z(): lax.ppermute(b, 'z', ring(NZ, -1))  12.8 us
    all_to_all x1, blocking collectives, shards(): received = lax.all_to_all(result, ('y', 'c'), 0, 0, tiled=True)  12.1 us
    ppermute x1, waiting for transfers between devices, shards(): lax.ppermute(edge, ('z', 'x', 'y', 'c'), [(i * CD + h, (i + s) * CD + h)...  5.52 us
  transfers between devices with their start and end apart: 27, of which 11 were waited for; matrix products, arithmetic and copies ran while one was open for 1% of the time, Pallas kernels for 15%

profile of v2, /device:TPU:1, one launch (start us, length us, event | category | flops | bytes accessed | tf_op | source)
XLA Modules:
  0.0 170.0 jit_solution(13143916034234626992)
XLA Ops:
  6.5 0.7 pad_add_fusion.pos
  7.2 3.5 %first.1 = (f32[128,512]{1,0:T(8,128)}, f32[128,512]{1,0:T(8,128)}) custom-call(s32[3]{0:T(128)} %pad_add_fusion.pos, s32[8,128]{1,0:T(8,128)} %bitcast.16, f32[1024,512]{1,0:T(8,128)} %nodes_ref.1), custom_call_target="tpu_custom_call" | custom-call | flops 1000000000 | bytes 3145728 | tf_op jit(solution)/shard_map/first/pallas_call | solution.py:107
  10.7 6.5 %collective-permute-start.1 = (f32[128,512]{1,0:T(8,128)}, f32[128,512]{1,0:T(8,128)S(1)}, u32[]{:S(2)}, u32[]{:S(2)}) collective-permute-start(f32[128,512]{1,0:T(8,128)} %get-tuple-element.51.refs_5_), channel_id=1, source_target_pairs={{0,224},{32,0},{64,32},{96,64},{128,96},{160,128},{192,160},{224,1... | collective-permute-start | bytes 786440 | tf_op jit(solution)/shard_map/ppermute | solution.py:465
  17.2 0.6 pad_add_fusion.1.pos.refs_0_
  17.8 3.0 %setup.1 = (s32[96]{0:T(128)}, s32[48]{0:T(128)}, f32[256,512]{1,0:T(8,128)}, f32[256,512]{1,0:T(8,128)}) custom-call(s32[2]{0:T(128)} %pad_add_fusion.1.pos.refs_0_, s32[8,6]{1,0:T(8,128)} %exp_ref.3, f32[64,512]{1,0:T(8,128)} %bitcast.20, f32[64,512]{1,0:T(8,128)} %bitcast.21, f32[64,512]{1,0:T(8,128)} %bitcast.22, f32[64,512]{1,0:T(8,128)} %bitcast.23, ...), custom_call_target="tpu_custom_call" | custom-call | flops 1000 | bytes 2097152 | tf_op jit(solution)/shard_map/setup/pallas_call | solution.py:158
  20.9 1.3 collective-permute-start.4
  22.2 2.5 %collective-permute-start.3 = (s32[96]{0:T(128)}, s32[96]{0:T(128)S(1)}, u32[]{:S(2)}, u32[]{:S(2)}) collective-permute-start(s32[96]{0:T(128)} %get-tuple-element.56.refs_1_), channel_id=1, source_target_pairs={{0,16},{8,24},{16,0},{24,8},{1,17},{9,25},{17,1},{25,9},{2,18},{10... | collective-permute-start | bytes 1160 | tf_op jit(solution)/shard_map/ppermute | solution.py:472
  24.6 1.2 collective-permute-start.2
  25.8 0.3 collective-permute-done.3.refs_3_
  26.1 0.9 collective-permute-done.2.refs_2_
  27.1 0.7 all-gather.5.cloned.1.call-update
  27.8 2.7 %collective-permute-start.8 = (f32[128,512]{1,0:T(8,128)S(1)}, f32[128,512]{1,0:T(8,128)S(1)}, u32[]{:S(2)}, u32[]{:S(2)}) collective-permute-start(f32[128,512]{1,0:T(8,128)S(1)} %collective-permute-done.1.refs_6_), channel_id=1, source_target_pairs={{0,224},{32,0},{64,32},{96,64},{128,96},{160,128},{192,160},{224,1... | collective-permute-start | bytes 786440 | tf_op jit(solution)/shard_map/ppermute | solution.py:465
  30.6 0.6 copy-done.2
  31.2 0.7 pick.3
  31.9 0.3 collective-permute-start.5
  32.2 3.3 %collective-permute-start.6 = (f32[144,512]{1,0:T(8,128)S(1)}, f32[144,512]{1,0:T(8,128)S(1)}, u32[]{:S(2)}, u32[]{:S(2)}) collective-permute-start(f32[144,512]{1,0:T(8,128)S(1)} %get-tuple-element.62), channel_id=1, source_target_pairs={{0,16},{8,24},{16,0},{24,8},{1,17},{9,25},{17,1},{25,9},{2,18},{10... | collective-permute-start | bytes 884744 | tf_op jit(solution)/shard_map/ppermute | solution.py:482
  35.5 1.5 collective-permute-done.9.refs_6_
  37.0 1.2 collective-permute-start.13
  38.3 0.2 collective-permute-start.14
  38.5 0.6 pick.4
  39.1 6.0 %collective-permute-done.6.refs_2_ = f32[144,512]{1,0:T(8,128)S(1)} collective-permute-done((f32[144,512]{1,0:T(8,128)S(1)}, f32[144,512]{1,0:T(8,128)S(1)}, u32[]{:S(2)}, u32[]{:S(2)}) %collective-permute-start.6) | collective-permute-done | bytes 294944 | tf_op jit(solution)/shard_map/ppermute | solution.py:482
  45.2 1.5 collective-permute-done.7.refs_3_
  46.7 2.3 %collective-permute-start.16 = (f32[64,512]{1,0:T(8,128)S(1)}, f32[64,512]{1,0:T(8,128)S(1)}, u32[]{:S(2)}, u32[]{:S(2)}) collective-permute-start(f32[64,512]{1,0:T(8,128)S(1)} %slice.7), channel_id=1, source_target_pairs={{0,224},{32,0},{64,32},{96,64},{128,96},{160,128},{192,160},{224,1... | collective-permute-start | bytes 393224 | tf_op jit(solution)/shard_map/ppermute | solution.py:465
  49.1 2.2 %collective-permute-start.10 = (f32[96,512]{1,0:T(8,128)S(1)}, f32[96,512]{1,0:T(8,128)S(1)}, u32[]{:S(2)}, u32[]{:S(2)}) collective-permute-start(f32[96,512]{1,0:T(8,128)S(1)} %get-tuple-element.67), channel_id=1, source_target_pairs={{0,8},{8,16},{16,24},{24,0},{1,9},{9,17},{17,25},{25,1},{2,10},{10... | collective-permute-start | bytes 589832 | tf_op jit(solution)/shard_map/ppermute | solution.py:482
  51.3 3.2 %collective-permute-done.15.refs_7_ = f32[64,512]{1,0:T(8,128)S(1)} collective-permute-done((f32[64,512]{1,0:T(8,128)S(1)}, f32[64,512]{1,0:T(8,128)S(1)}, u32[]{:S(2)}, u32[]{:S(2)}) %collective-permute-start.15) | collective-permute-done | bytes 131104 | tf_op jit(solution)/shard_map/ppermute | solution.py:465
  54.5 0.7 pick.5
  55.2 2.3 %collective-permute-start.17 = (f32[144,512]{1,0:T(8,128)S(1)}, f32[144,512]{1,0:T(8,128)S(1)}, u32[]{:S(2)}, u32[]{:S(2)}) collective-permute-start(f32[144,512]{1,0:T(8,128)S(1)} %get-tuple-element.75), channel_id=1, source_target_pairs={{0,8},{8,16},{16,24},{24,0},{1,9},{9,17},{17,25},{25,1},{2,10},{10... | collective-permute-start | bytes 884744 | tf_op jit(solution)/shard_map/ppermute | solution.py:482
  57.5 2.7 %collective-permute-start.18 = (f32[144,512]{1,0:T(8,128)S(1)}, f32[144,512]{1,0:T(8,128)S(1)}, u32[]{:S(2)}, u32[]{:S(2)}) collective-permute-start(f32[144,512]{1,0:T(8,128)S(1)} %get-tuple-element.76), channel_id=1, source_target_pairs={{0,16},{8,24},{16,0},{24,8},{1,17},{9,25},{17,1},{25,9},{2,18},{10... | collective-permute-start | bytes 884744 | tf_op jit(solution)/shard_map/ppermute | solution.py:482
  60.1 1.3 collective-permute-start.11
  61.4 2.6 %collective-permute-start.12 = (f32[96,512]{1,0:T(8,128)S(1)}, f32[96,512]{1,0:T(8,128)S(1)}, u32[]{:S(2)}, u32[]{:S(2)}) collective-permute-start(f32[96,512]{1,0:T(8,128)S(1)} %get-tuple-element.69), channel_id=1, source_target_pairs={{0,24},{8,0},{16,8},{24,16},{1,25},{9,1},{17,9},{25,17},{2,26},{10... | collective-permute-start | bytes 589832 | tf_op jit(solution)/shard_map/ppermute | solution.py:482
  64.0 10.7 %collective-permute-done.11.refs_6_ = f32[96,512]{1,0:T(8,128)S(1)} collective-permute-done((f32[96,512]{1,0:T(8,128)S(1)}, f32[96,512]{1,0:T(8,128)S(1)}, u32[]{:S(2)}, u32[]{:S(2)}) %collective-permute-start.11) | collective-permute-done | bytes 196640 | tf_op jit(solution)/shard_map/ppermute | solution.py:482
  74.7 4.6 %collective-permute-done.12.refs_7_ = f32[96,512]{1,0:T(8,128)S(1)} collective-permute-done((f32[96,512]{1,0:T(8,128)S(1)}, f32[96,512]{1,0:T(8,128)S(1)}, u32[]{:S(2)}, u32[]{:S(2)}) %collective-permute-start.12) | collective-permute-done | bytes 196640 | tf_op jit(solution)/shard_map/ppermute | solution.py:482
  79.3 2.0 %send.1 = f32[768,512]{1,0:T(8,128)} custom-call(s32[48]{0:T(128)S(1)} %copy-done.4, f32[144,512]{1,0:T(8,128)S(1)} %get-tuple-element.60.refs_0_, f32[144,512]{1,0:T(8,128)S(1)} %collective-permute-done.5.refs_1_, f32[144,512]{1,0:T(8,128)S(1)} %collective-permute-done.6.refs_2_, f32[144,512]{1,0:T(8,128)S(1)} %collective-permute-done.7.refs_3_, ...), custom_call_target="tpu_custom_call" | custom-call | bytes 6291456 | tf_op jit(solution)/shard_map/send/pallas_call | solution.py:432
  81.3 15.5 %all-gather.5.cloned.1.call-done.mine = f32[1024,512]{1,0:T(8,128)} async-done(((f32[256,512]{1,0:T(8,128)}), f32[1024,512]{1,0:T(8,128)}) %all-gather.5.cloned.1.call-update) | async-done | bytes 2097168 | tf_op jit(solution)/shard_map/all_gather | solution.py:476
  96.9 0.7 collective-permute-start.22
  97.5 4.7 %all-to-all-start = ((f32[8,96,512]{2,1,0:T(8,128)}), f32[8,96,512]{2,1,0:T(8,128)}, u32[]{:S(2)}, u32[]{:S(2)}) async-start(f32[8,96,512]{2,1,0:T(8,128)} %bitcast.10), calls=%async_computation | async-start | bytes 3145728 | tf_op jit(solution)/shard_map/all_to_all | solution.py:497
  102.2 3.1 %collective-permute-start.20 = (f32[128,512]{1,0:T(8,128)S(1)}, f32[128,512]{1,0:T(8,128)S(1)}, u32[]{:S(2)}, u32[]{:S(2)}) collective-permute-start(f32[128,512]{1,0:T(8,128)S(1)} %copy-done.9), channel_id=1, source_target_pairs={{0,8},{1,9},{8,16},{9,17},{16,24},{17,25},{24,32},{25,33},{32,40},... | collective-permute-start | bytes 786440 | tf_op jit(solution)/shard_map/ppermute | solution.py:500
  105.3 5.5 %collective-permute-done.20.e_in = f32[128,512]{1,0:T(8,128)S(1)} collective-permute-done((f32[128,512]{1,0:T(8,128)S(1)}, f32[128,512]{1,0:T(8,128)S(1)}, u32[]{:S(2)}, u32[]{:S(2)}) %collective-permute-start.20) | collective-permute-done | bytes 262176 | tf_op jit(solution)/shard_map/ppermute | solution.py:500
  110.9 1.0 collective-permute-start.21
  111.8 0.7 copy.14.local_ref
  112.5 0.5 collective-permute-done.21.e_other
  113.0 0.7 copy-done.11
  113.7 15.0 %near.1 = (f32[128,512]{1,0:T(8,128)}, bf16[2,4,256,512]{3,2,1,0:T(8,128)(2,1)}, bf16[2,4,128,512]{3,2,1,0:T(8,128)(2,1)}, bf16[2,512,512]{2,1,0:T(8,128)(2,1)}, f32[4,256,128]{2,1,0:T(8,128)}) custom-call(s32[3]{0:T(128)} %pad_add_fusion.pos, s32[8,3]{1,0:T(8,128)} %copy.14.local_ref, s32[8]{0:T(128)} %virt_ref.1, s32[256]{0:T(256)} %count_ref.3, ...), custom_call_target="tpu_custom_call" | custom-call | flops 6000000000 | bytes 16777216 | tf_op jit(solution)/shard_map/near/pallas_call | solution.py:242
  128.7 1.3 copy-done.7
  130.0 5.1 %prep.1 = (bf16[2,512,1024]{2,1,0:T(8,128)(2,1)}, bf16[2,1024,512]{2,1,0:T(8,128)(2,1)}) custom-call(f32[1024,512]{1,0:T(8,128)} %all-gather.5.cloned.1.call-done.mine, f32[1024,512]{1,0:T(8,128)} %copy-done.7), custom_call_target="tpu_custom_call" | custom-call | flops 10000000 | bytes 8388608 | tf_op jit(solution)/shard_map/prep/pallas_call | solution.py:268
  135.2 13.8 %far.1 = f32[512,128]{1,0:T(8,128)} custom-call(s32[3]{0:T(128)} %pad_add_fusion.pos, s32[8,6]{1,0:T(8,128)} %exp_ref.3, s32[256]{0:T(256)} %count_ref.3, f32[768,512]{1,0:T(8,128)} %bitcast.11.xe_ref, bf16[2,4,256,512]{3,2,1,0:T(8,128)(2,1)} %get-tuple-element.84.q_hbm, f32[4,256,128]{2,1,0:T(8,128)} %get-tuple-element.87.s_hbm, ...), custom_call_target="tpu_custom_call" | custom-call | flops 6000000000 | bytes 16777216 | tf_op jit(solution)/shard_map/far/pallas_call | solution.py:345
  149.0 12.1 %all_to_all.22 = f32[8,64,128]{2,1,0:T(8,128)S(1)} all-to-all(f32[8,64,128]{2,1,0:T(8,128)} %bitcast.19), channel_id=1, replica_groups=mesh['z'=8,'x'=4,'y'=4,'c'=2] {'y','c'}, dimensions={0} | all-to-all | bytes 524288 | tf_op jit(solution)/shard_map/all_to_all | solution.py:511
  161.0 2.1 %place.1 = f32[64,1024]{1,0:T(8,128)} custom-call(s32[3]{0:T(128)S(1)} %copy-done.5, f32[512,128]{1,0:T(8,128)S(1)} %bitcast.15, s32[8,128]{1,0:T(8,128)S(1)} %bitcast.18), custom_call_target="tpu_custom_call" | custom-call | flops 400000000 | bytes 1048576 | tf_op jit(solution)/shard_map/place/pallas_call | solution.py:375
  (48 shorter events, 0.2 us)
Async XLA Ops:
  6.5 74.8 %all-gather.3.cloned.1.call-start = ((), (), s32[]{:S(2)}) async-start(), calls=%async_computation.2 | async-start | bytes 2621440 | tf_op jit(solution)/shard_map/all_gather | solution.py:475
  10.7 19.9 %copy-start = (f32[128,512]{1,0:T(8,128)S(1)}, f32[128,512]{1,0:T(8,128)}, u32[]{:S(2)}) copy-start(f32[128,512]{1,0:T(8,128)} %get-tuple-element.51.refs_5_) | copy-start | bytes 786436
  10.7 16.4 %collective-permute-start.1 = (f32[128,512]{1,0:T(8,128)}, f32[128,512]{1,0:T(8,128)S(1)}, u32[]{:S(2)}, u32[]{:S(2)}) collective-permute-start(f32[128,512]{1,0:T(8,128)} %get-tuple-element.51.refs_5_), channel_id=1, source_target_pairs={{0,224},{32,0},{64,32},{96,64},{128,96},{160,128},{192,160},{224,1... | collective-permute-start | bytes 786440 | tf_op jit(solution)/shard_map/ppermute | solution.py:465
  17.2 9.9 %collective-permute-start = (f32[128,512]{1,0:T(8,128)}, f32[128,512]{1,0:T(8,128)S(1)}, u32[]{:S(2)}, u32[]{:S(2)}) collective-permute-start(f32[128,512]{1,0:T(8,128)} %get-tuple-element.51.refs_5_), channel_id=1, source_target_pairs={{0,32},{32,64},{64,96},{96,128},{128,160},{160,192},{192,224},{224... | collective-permute-start | bytes 786440 | tf_op jit(solution)/shard_map/ppermute | solution.py:465
  17.8 12.8 %copy-start.1 = (s32[2]{0:T(128)S(1)}, s32[2]{0:T(128)}, u32[]{:S(2)}) copy-start(s32[2]{0:T(128)} %pad_add_fusion.1.pos.refs_0_) | copy-start | bytes 28
  20.9 33.6 %copy-start.3 = (s32[96]{0:T(128)S(1)}, s32[96]{0:T(128)}, u32[]{:S(2)}) copy-start(s32[96]{0:T(128)} %get-tuple-element.56.refs_1_) | copy-start | bytes 1156
  20.9 58.4 %copy-start.4 = (s32[48]{0:T(128)S(1)}, s32[48]{0:T(128)}, u32[]{:S(2)}) copy-start(s32[48]{0:T(128)} %get-tuple-element.50.row) | copy-start | bytes 580
  20.9 4.9 %collective-permute-start.4 = (s32[96]{0:T(128)}, s32[96]{0:T(128)S(1)}, u32[]{:S(2)}, u32[]{:S(2)}) collective-permute-start(s32[96]{0:T(128)} %get-tuple-element.56.refs_1_), channel_id=1, source_target_pairs={{0,8},{8,16},{16,24},{24,0},{1,9},{9,17},{17,25},{25,1},{2,10},{10... | collective-permute-start | bytes 1160 | tf_op jit(solution)/shard_map/ppermute | solution.py:472
  22.2 4.0 %collective-permute-start.3 = (s32[96]{0:T(128)}, s32[96]{0:T(128)S(1)}, u32[]{:S(2)}, u32[]{:S(2)}) collective-permute-start(s32[96]{0:T(128)} %get-tuple-element.56.refs_1_), channel_id=1, source_target_pairs={{0,16},{8,24},{16,0},{24,8},{1,17},{9,25},{17,1},{25,9},{2,18},{10... | collective-permute-start | bytes 1160 | tf_op jit(solution)/shard_map/ppermute | solution.py:472
  24.6 2.4 %collective-permute-start.2 = (s32[96]{0:T(128)}, s32[96]{0:T(128)S(1)}, u32[]{:S(2)}, u32[]{:S(2)}) collective-permute-start(s32[96]{0:T(128)} %get-tuple-element.56.refs_1_), channel_id=1, source_target_pairs={{0,24},{8,0},{16,8},{24,16},{1,25},{9,1},{17,9},{25,17},{2,26},{10... | collective-permute-start | bytes 1160 | tf_op jit(solution)/shard_map/ppermute | solution.py:472
  27.1 69.8 %all-gather.5.cloned.1.call-start = ((), (), s32[]{:S(2)}) async-start(), calls=%async_computation.3 | async-start | bytes 2621440 | tf_op jit(solution)/shard_map/all_gather | solution.py:476
  27.8 7.7 %collective-permute-start.8 = (f32[128,512]{1,0:T(8,128)S(1)}, f32[128,512]{1,0:T(8,128)S(1)}, u32[]{:S(2)}, u32[]{:S(2)}) collective-permute-start(f32[128,512]{1,0:T(8,128)S(1)} %collective-permute-done.1.refs_6_), channel_id=1, source_target_pairs={{0,224},{32,0},{64,32},{96,64},{128,96},{160,128},{192,160},{224,1... | collective-permute-start | bytes 786440 | tf_op jit(solution)/shard_map/ppermute | solution.py:465
  30.6 6.4 %collective-permute-start.9 = (f32[128,512]{1,0:T(8,128)S(1)}, f32[128,512]{1,0:T(8,128)S(1)}, u32[]{:S(2)}, u32[]{:S(2)}) collective-permute-start(f32[128,512]{1,0:T(8,128)S(1)} %collective-permute-done.refs_7_), channel_id=1, source_target_pairs={{0,32},{32,64},{64,96},{96,128},{128,160},{160,192},{192,224},{224... | collective-permute-start | bytes 786440 | tf_op jit(solution)/shard_map/ppermute | solution.py:465
  30.6 0.6 copy-start.2
  31.9 7.3 %collective-permute-start.5 = (f32[144,512]{1,0:T(8,128)S(1)}, f32[144,512]{1,0:T(8,128)S(1)}, u32[]{:S(2)}, u32[]{:S(2)}) collective-permute-start(f32[144,512]{1,0:T(8,128)S(1)} %get-tuple-element.61), channel_id=1, source_target_pairs={{0,8},{8,16},{16,24},{24,0},{1,9},{9,17},{17,25},{25,1},{2,10},{10... | collective-permute-start | bytes 884744 | tf_op jit(solution)/shard_map/ppermute | solution.py:482
  32.2 13.0 %collective-permute-start.6 = (f32[144,512]{1,0:T(8,128)S(1)}, f32[144,512]{1,0:T(8,128)S(1)}, u32[]{:S(2)}, u32[]{:S(2)}) collective-permute-start(f32[144,512]{1,0:T(8,128)S(1)} %get-tuple-element.62), channel_id=1, source_target_pairs={{0,16},{8,24},{16,0},{24,8},{1,17},{9,25},{17,1},{25,9},{2,18},{10... | collective-permute-start | bytes 884744 | tf_op jit(solution)/shard_map/ppermute | solution.py:482
  35.5 11.2 %collective-permute-start.7 = (f32[144,512]{1,0:T(8,128)S(1)}, f32[144,512]{1,0:T(8,128)S(1)}, u32[]{:S(2)}, u32[]{:S(2)}) collective-permute-start(f32[144,512]{1,0:T(8,128)S(1)} %get-tuple-element.63), channel_id=1, source_target_pairs={{0,24},{8,0},{16,8},{24,16},{1,25},{9,1},{17,9},{25,17},{2,26},{10... | collective-permute-start | bytes 884744 | tf_op jit(solution)/shard_map/ppermute | solution.py:482
  37.0 9.7 %collective-permute-start.13 = (f32[128,512]{1,0:T(8,128)S(1)}, f32[128,512]{1,0:T(8,128)S(1)}, u32[]{:S(2)}, u32[]{:S(2)}) collective-permute-start(f32[128,512]{1,0:T(8,128)S(1)} %collective-permute-done.8.refs_5_), channel_id=1, source_target_pairs={{0,224},{32,0},{64,32},{96,64},{128,96},{160,128},{192,160},{224,1... | collective-permute-start | bytes 786440 | tf_op jit(solution)/shard_map/ppermute | solution.py:465
  38.3 8.5 %collective-permute-start.14 = (f32[128,512]{1,0:T(8,128)S(1)}, f32[128,512]{1,0:T(8,128)S(1)}, u32[]{:S(2)}, u32[]{:S(2)}) collective-permute-start(f32[128,512]{1,0:T(8,128)S(1)} %collective-permute-done.9.refs_6_), channel_id=1, source_target_pairs={{0,32},{32,64},{64,96},{96,128},{128,160},{160,192},{192,224},{224... | collective-permute-start | bytes 786440 | tf_op jit(solution)/shard_map/ppermute | solution.py:465
  46.7 4.5 %collective-permute-start.16 = (f32[64,512]{1,0:T(8,128)S(1)}, f32[64,512]{1,0:T(8,128)S(1)}, u32[]{:S(2)}, u32[]{:S(2)}) collective-permute-start(f32[64,512]{1,0:T(8,128)S(1)} %slice.7), channel_id=1, source_target_pairs={{0,224},{32,0},{64,32},{96,64},{128,96},{160,128},{192,160},{224,1... | collective-permute-start | bytes 393224 | tf_op jit(solution)/shard_map/ppermute | solution.py:465
  49.1 5.4 %collective-permute-start.15 = (f32[64,512]{1,0:T(8,128)S(1)}, f32[64,512]{1,0:T(8,128)S(1)}, u32[]{:S(2)}, u32[]{:S(2)}) collective-permute-start(f32[64,512]{1,0:T(8,128)S(1)} %slice.6), channel_id=1, source_target_pairs={{0,32},{32,64},{64,96},{96,128},{128,160},{160,192},{192,224},{224... | collective-permute-start | bytes 393224 | tf_op jit(solution)/shard_map/ppermute | solution.py:465
  49.1 12.3 %collective-permute-start.10 = (f32[96,512]{1,0:T(8,128)S(1)}, f32[96,512]{1,0:T(8,128)S(1)}, u32[]{:S(2)}, u32[]{:S(2)}) collective-permute-start(f32[96,512]{1,0:T(8,128)S(1)} %get-tuple-element.67), channel_id=1, source_target_pairs={{0,8},{8,16},{16,24},{24,0},{1,9},{9,17},{17,25},{25,1},{2,10},{10... | collective-permute-start | bytes 589832 | tf_op jit(solution)/shard_map/ppermute | solution.py:482
  55.2 24.1 %collective-permute-start.17 = (f32[144,512]{1,0:T(8,128)S(1)}, f32[144,512]{1,0:T(8,128)S(1)}, u32[]{:S(2)}, u32[]{:S(2)}) collective-permute-start(f32[144,512]{1,0:T(8,128)S(1)} %get-tuple-element.75), channel_id=1, source_target_pairs={{0,8},{8,16},{16,24},{24,0},{1,9},{9,17},{17,25},{25,1},{2,10},{10... | collective-permute-start | bytes 884744 | tf_op jit(solution)/shard_map/ppermute | solution.py:482
  57.5 21.8 %collective-permute-start.18 = (f32[144,512]{1,0:T(8,128)S(1)}, f32[144,512]{1,0:T(8,128)S(1)}, u32[]{:S(2)}, u32[]{:S(2)}) collective-permute-start(f32[144,512]{1,0:T(8,128)S(1)} %get-tuple-element.76), channel_id=1, source_target_pairs={{0,16},{8,24},{16,0},{24,8},{1,17},{9,25},{17,1},{25,9},{2,18},{10... | collective-permute-start | bytes 884744 | tf_op jit(solution)/shard_map/ppermute | solution.py:482
  60.1 19.2 %collective-permute-start.19 = (f32[144,512]{1,0:T(8,128)S(1)}, f32[144,512]{1,0:T(8,128)S(1)}, u32[]{:S(2)}, u32[]{:S(2)}) collective-permute-start(f32[144,512]{1,0:T(8,128)S(1)} %get-tuple-element.77), channel_id=1, source_target_pairs={{0,24},{8,0},{16,8},{24,16},{1,25},{9,1},{17,9},{25,17},{2,26},{10... | collective-permute-start | bytes 884744 | tf_op jit(solution)/shard_map/ppermute | solution.py:482
  60.1 14.6 %collective-permute-start.11 = (f32[96,512]{1,0:T(8,128)S(1)}, f32[96,512]{1,0:T(8,128)S(1)}, u32[]{:S(2)}, u32[]{:S(2)}) collective-permute-start(f32[96,512]{1,0:T(8,128)S(1)} %get-tuple-element.68), channel_id=1, source_target_pairs={{0,16},{8,24},{16,0},{24,8},{1,17},{9,25},{17,1},{25,9},{2,18},{10... | collective-permute-start | bytes 589832 | tf_op jit(solution)/shard_map/ppermute | solution.py:482
  61.4 17.9 %collective-permute-start.12 = (f32[96,512]{1,0:T(8,128)S(1)}, f32[96,512]{1,0:T(8,128)S(1)}, u32[]{:S(2)}, u32[]{:S(2)}) collective-permute-start(f32[96,512]{1,0:T(8,128)S(1)} %get-tuple-element.69), channel_id=1, source_target_pairs={{0,24},{8,0},{16,8},{24,16},{1,25},{9,1},{17,9},{25,17},{2,26},{10... | collective-permute-start | bytes 589832 | tf_op jit(solution)/shard_map/ppermute | solution.py:482
  81.3 20.9 %copy-start.9 = (f32[128,512]{1,0:T(8,128)S(1)}, f32[128,512]{1,0:T(8,128)}, u32[]{:S(2)}) copy-start(f32[128,512]{1,0:T(8,128)} %get-tuple-element.82) | copy-start | bytes 786436
  81.3 30.5 %copy-start.8 = (s32[8,3]{0,1:T(4,128)S(1)}, s32[8,3]{0,1:T(4,128)}, u32[]{:S(2)}) copy-start(s32[8,3]{0,1:T(4,128)} %param.16) | copy-start | bytes 292
  96.9 16.1 %collective-permute-start.22 = (f32[1024,512]{1,0:T(8,128)}, f32[1024,512]{1,0:T(8,128)}, u32[]{:S(2)}, u32[]{:S(2)}) collective-permute-start(f32[1024,512]{1,0:T(8,128)} %all-gather.3.cloned.1.call-done.mine_hbm), channel_id=1, source_target_pairs={{0,1},{1,0},{2,3},{3,2},{4,5},{5,4},{6,7},{7,6},{8,9},{9,8},{10,11... | collective-permute-start | bytes 6291464 | tf_op jit(solution)/shard_map/ppermute | solution.py:468
  97.5 31.2 %collective-permute-start.23 = (f32[1024,512]{1,0:T(8,128)}, f32[1024,512]{1,0:T(8,128)S(1)}, u32[]{:S(2)}, u32[]{:S(2)}) collective-permute-start(f32[1024,512]{1,0:T(8,128)} %all-gather.5.cloned.1.call-done.mine), channel_id=1, source_target_pairs={{0,1},{1,0},{2,3},{3,2},{4,5},{5,4},{6,7},{7,6},{8,9},{9,8},{10,11... | collective-permute-start | bytes 6291464 | tf_op jit(solution)/shard_map/ppermute | solution.py:468
  97.5 37.6 %all-to-all-start = ((f32[8,96,512]{2,1,0:T(8,128)}), f32[8,96,512]{2,1,0:T(8,128)}, u32[]{:S(2)}, u32[]{:S(2)}) async-start(f32[8,96,512]{2,1,0:T(8,128)} %bitcast.10), calls=%async_computation | async-start | bytes 3145728 | tf_op jit(solution)/shard_map/all_to_all | solution.py:497
  102.2 8.6 %collective-permute-start.20 = (f32[128,512]{1,0:T(8,128)S(1)}, f32[128,512]{1,0:T(8,128)S(1)}, u32[]{:S(2)}, u32[]{:S(2)}) collective-permute-start(f32[128,512]{1,0:T(8,128)S(1)} %copy-done.9), channel_id=1, source_target_pairs={{0,8},{1,9},{8,16},{9,17},{16,24},{17,25},{24,32},{25,33},{32,40},... | collective-permute-start | bytes 786440 | tf_op jit(solution)/shard_map/ppermute | solution.py:500
  110.9 2.1 %copy-start.10 = (f32[128,512]{1,0:T(8,128)}, f32[128,512]{1,0:T(8,128)S(1)}, u32[]{:S(2)}) copy-start(f32[128,512]{1,0:T(8,128)S(1)} %collective-permute-done.20.e_in) | copy-start | bytes 786436
  110.9 2.1 %collective-permute-start.21 = (f32[128,512]{1,0:T(8,128)S(1)}, f32[128,512]{1,0:T(8,128)S(1)}, u32[]{:S(2)}, u32[]{:S(2)}) collective-permute-start(f32[128,512]{1,0:T(8,128)S(1)} %collective-permute-done.20.e_in), channel_id=1, source_target_pairs={{0,1},{1,0},{2,3},{3,2},{4,5},{5,4},{6,7},{7,6},{8,9},{9,8},{10,11... | collective-permute-start | bytes 786440 | tf_op jit(solution)/shard_map/ppermute | solution.py:468
  113.0 0.7 copy-start.11
  128.7 1.3 copy-start.7
  135.1 25.9 %copy-start.5 = (s32[3]{0:T(128)S(1)}, s32[3]{0:T(128)}, u32[]{:S(2)}) copy-start(s32[3]{0:T(128)} %pad_add_fusion.pos) | copy-start | bytes 40
  135.1 25.9 %copy-start.6 = (s32[1024]{0:T(1024)S(1)}, s32[1024]{0:T(1024)}, u32[]{:S(2)}) copy-start(s32[1024]{0:T(1024)} %param.14) | copy-start | bytes 12292
Sparse Core Ops, SparseCore 0:
  27.2 34.3 all-gather.2
  63.4 33.4 all-gather.4

commit v3 on v2

--- a/solution.py
+++ b/solution.py
@@ -26,7 +26,7 @@
 NT = (((1,), (1,)), ((), ()))
 NN = (((1,), (0,)), ((), ()))
 
-GROUPS = ((0, 1, 7), (2, 6), (3, 5, 4))
+GROUPS = ((0, 1, 7), (2, 6, 3, 5, 4))
 
 
 def split2(v):
@@ -117,14 +117,14 @@
     )(pos, order, nodes)
 
 
-def setup_kernel(pos, exp_ref, q, k, v, o, up, down, table, row, att, ffw, seen, starts, widths, sems):
-    pairs = [(w, att.at[i * HD:(i + 1) * HD, :]) for i, w in enumerate((q, k, v, o))]
-    pairs.append((down, ffw.at[:CL, :]))
-    pairs += [(up.at[j * CL:(j + 1) * CL, :], ffw.at[CL:, j * CL:(j + 1) * CL]) for j in range(4)]
+def setup_kernel(pos, exp_ref, q, k, v, o, up, down, table, row, out, seen, starts, widths, sems):
+    pairs = [(w, out.at[i * HD:(i + 1) * HD, :]) for i, w in enumerate((q, k, v, o))]
+    pairs.append((down, out.at[2 * CL:3 * CL, :]))
+    pairs += [(up.at[j * CL:(j + 1) * CL, :], out.at[3 * CL:, j * CL:(j + 1) * CL]) for j in range(4)]
     copies = [pltpu.make_async_copy(src, dst, sems.at[i]) for i, (src, dst) in enumerate(pairs)]
     for copy in copies:
         copy.start()
-    z, x = pos[0], pos[1]
+    z, x = pos[3], pos[4]
     start = 0
     for group in GROUPS:
         for p, s in enumerate(group):
@@ -158,9 +158,9 @@
     return pl.pallas_call(
         setup_kernel,
         out_shape=[sds(NX * NZ * CAP, dtype=jnp.int32), sds(CD * NE, dtype=jnp.int32),
-                   sds(2 * CL, D), sds(2 * CL, D)],
+                   sds(D, D)],
         in_specs=[sspec()] * 2 + [hspec()] * 6,
-        out_specs=[sspec()] * 2 + [vspec()] * 2,
+        out_specs=[sspec()] * 2 + [vspec()],
         scratch_shapes=[pltpu.SMEM((NZ * NX,), jnp.int32), pltpu.SMEM((NZ,), jnp.int32), pltpu.SMEM((NZ,), jnp.int32),
                         pltpu.SemaphoreType.DMA((9,))],
         compiler_params=params(60),
@@ -169,11 +169,10 @@
     )(pos, exp_blocks, *w)
 
 
-def near_kernel(pos, local_ref, virt_ref, count_ref, order_ref, nodes_ref, e_in, e_other, virtual_ref, mine_hbm, other_hbm,
-                x_out, q_out, v_out, o_out, state, kh, kl, mine, other, sems):
-    fetch = [pltpu.make_async_copy(mine_hbm, mine, sems.at[0]), pltpu.make_async_copy(other_hbm, other, sems.at[1])]
-    for copy in fetch:
-        copy.start()
+def near_kernel(pos, local_ref, virt_ref, count_ref, order_ref, nodes_ref, e_in, e_other, virtual_ref, w_hbm,
+                x_out, q_out, v_out, o_out, state, kh, kl, w, sem):
+    fetch = pltpu.make_async_copy(w_hbm.at[:, :2 * CL, :], w, sem)
+    fetch.start()
     base, head, c = pos[0], pos[1], pos[2]
     first = lax.shift_right_logical(base, 7)
 
@@ -205,11 +204,9 @@
     lanes = lax.broadcasted_iota(jnp.int32, (CL, 2 * HD), 1)
     lowq = lanes < HD
     xh, xl = split2(x)
-    for copy in fetch:
-        copy.wait()
+    fetch.wait()
     for at in range(NY):
-        a, b = mine[at * 2 * CL:(at + 1) * 2 * CL, :], other[at * 2 * CL:(at + 1) * 2 * CL, :]
-        left, right = jnp.where(c == 0, a, b), jnp.where(c == 0, b, a)
+        left, right = w[2 * at], w[2 * at + 1]
         wq, wk, wv, wo = (
             split2(jnp.concatenate([left[i * HD:(i + 1) * HD], right[i * HD:(i + 1) * HD]], 0))
             for i in range(4))
@@ -242,38 +239,42 @@
     return pl.pallas_call(
         near_kernel,
         out_shape=shapes,
-        in_specs=[sspec()] * len(scalars) + [vspec()] * (len(arrays) - 2) + [hspec()] * 2,
+        in_specs=[sspec()] * len(scalars) + [vspec()] * (len(arrays) - 1) + [hspec()],
         out_specs=[vspec()] * len(shapes),
-        scratch_shapes=[pltpu.VMEM((LK, D), BF), pltpu.VMEM((LK, D), BF), pltpu.VMEM(arrays[-1].shape, F32),
-                        pltpu.VMEM(arrays[-1].shape, F32), pltpu.SemaphoreType.DMA((2,))],
+        scratch_shapes=[pltpu.VMEM((LK, D), BF), pltpu.VMEM((LK, D), BF), pltpu.VMEM((CD, 2 * CL, D), F32),
+                        pltpu.SemaphoreType.DMA],
         compiler_params=params(60),
         cost_estimate=cost(6 * 10**9, 16 << 20, 1 << 20),
         name="near",
     )(*scalars, *arrays)
 
 
-def prep_kernel(mine, other, u_out, d_out):
-    for i in range(8):
-        w, at = (mine, other)[i // NY], i % NY * 2 * CL
+def prep_kernel(w_hbm, u_out, d_out, w, sems):
+    fetch = [pltpu.make_async_copy(w_hbm.at[i, 2 * CL:, :], w.at[i], sems.at[i]) for i in range(CD)]
+    for copy in fetch:
+        copy.start()
+    for i in range(CD):
+        fetch[i].wait()
         rows = slice(i * CL, (i + 1) * CL)
-        d_out[0, rows, :], d_out[1, rows, :] = split2(w[at:at + CL, :])
-        hi, lo = split2(w[at + CL:at + 2 * CL, :])
+        d_out[0, rows, :], d_out[1, rows, :] = split2(w[i, :CL, :])
+        hi, lo = split2(w[i, CL:, :])
         for j in range(4):
             cols = slice(j * CL, (j + 1) * CL)
             u_out[0, cols, rows] = hi[:, cols]
             u_out[1, cols, rows] = lo[:, cols]
 
 
-def prep_call(mine, other):
+def prep_call(weights):
     return pl.pallas_call(
         prep_kernel,
         out_shape=[sds(2, D, FF, dtype=BF), sds(2, FF, D, dtype=BF)],
-        in_specs=[vspec()] * 2,
+        in_specs=[hspec()],
         out_specs=[vspec()] * 2,
+        scratch_shapes=[pltpu.VMEM((CD, 2 * CL, D), F32), pltpu.SemaphoreType.DMA((CD,))],
         compiler_params=params(60),
         cost_estimate=cost(10**7, 8 << 20),
         name="prep",
-    )(mine, other)
+    )(weights)
 
 
 def far_kernel(pos, exp_ref, count_ref, xe_ref, q_hbm, s_hbm, v_hbm, x_hbm, o_hbm, u_hbm, d_hbm,
@@ -385,7 +386,7 @@
 
 def pick_kernel(group, pos, *refs):
     tables, srcs, outs = refs[:NX], refs[NX:-NX], refs[-NX:]
-    z = pos[0]
+    z = pos[3]
     parts, at = [], 0
     for s in group:
         size = 2 if s == NZ // 2 else 1
@@ -452,8 +453,7 @@
            w_query, w_key, w_value, w_out, w_up, w_down):
     z, x, y, c = (lax.axis_index(a) for a in ("z", "x", "y", "c"))
     head = y * NC + c
-    pos = jnp.stack([(z * NX + x) * (CD * CL), head, c]).astype(jnp.int32)
-    zx = jnp.stack([z, x]).astype(jnp.int32)
+    pos = jnp.stack([(z * NX + x) * (CD * CL), head, c, z, x]).astype(jnp.int32)
     order = order.reshape(CD, CL)
 
     piece, edge = first_call(pos, order, node_feats)
@@ -468,45 +468,45 @@
         return [lax.ppermute(t, "c", SWAP) for t in arrays]
 
     up, down = both_z(piece, piece)
-    table, row, wa, wb = setup_call(zx, exp_blocks, w_query.T, w_key.T, w_value.T, w_out.T, w_up, w_down)
+    table, row, w = setup_call(pos, exp_blocks, w_query.T, w_key.T, w_value.T, w_out.T, w_up, w_down)
     tables = [table] + [lax.ppermute(table, "x", ring(NX, -k)) for k in range(1, NX)]
     held = {0: (piece,), 7: (up,), 1: (down,)}
-    up, down, edge, wa, wb, *tables = tie((up, down, edge, wa, wb, *tables))
-    wa = lax.all_gather(wa, "y", axis=0, tiled=True)
-    wb = lax.all_gather(wb, "y", axis=0, tiled=True)
+    up, down, w, edge, *tables = tie((up, down, w, edge, *tables))
+    w = lax.all_gather(w, ("y", "c"), axis=0, tiled=True).reshape(CD, D, D)
 
     def pick(group):
-        return pick_call(group, zx, tables, [t for s in group for t in held[s]])
+        return pick_call(group, pos, tables, [t for s in group for t in held[s]])
 
     def exchange(blocks):
         return [blocks[0]] + [lax.ppermute(blocks[k], "x", ring(NX, k)) for k in (1, 2, 3)]
 
     one = pick(GROUPS[0])
+    e_in = lax.ppermute(edge, ("z", "x", "y", "c"), [
+        (i * CD + h, (i + s) * CD + h)
+        for s, hs in ((1, (0, 1)), (-1, (6, 7)))
+        for i in range(NZ * NX) if 0 <= i + s < NZ * NX for h in hs])
     up, down = both_z(up, down)
     held[6], held[2] = (up,), (down,)
     up, down, *_ = tie((up, down, *one))
     one = exchange(one)
-    two = pick(GROUPS[1])
     up, down = both_z(up, down)
     held[5], held[3] = (up,), (down,)
-    up, down, *_ = tie((up, down, *one, *two))
+    up, down, e_in, *_ = tie((up, down, e_in, *one))
     held[4] = both_z(up[:half], down[half:])
-    arrived = one + exchange(two) + exchange(pick(GROUPS[2]))
+    two = pick(GROUPS[1])
+    (e_other,) = swap(tie((e_in, *two))[0])
+    arrived = one + exchange(two)
+    arrived = tie((e_other, *arrived))
+    e_other, arrived = arrived[0], arrived[1:]
 
     sending = send_call(row, arrived)
     xe = lax.all_to_all(sending, ("y", "c"), 0, 0, tiled=True)
 
-    _, wa, wb, edge, pos_late = tie((sending, wa, wb, edge, pos))
-    e_in = lax.ppermute(edge, ("z", "x", "y", "c"), [
-        (i * CD + h, (i + s) * CD + h)
-        for s, hs in ((1, (0, 1)), (-1, (6, 7)))
-        for i in range(NZ * NX) if 0 <= i + s < NZ * NX for h in hs])
-    e_other, wa_other, wb_other = swap(e_in, wa, wb)
+    _, w, pos_late = tie((sending, w, pos))
     x_own, q, wv, wo, state = near_call(
-        (pos_late, local_blocks, virt_blocks, node_count),
-        (order, node_feats, e_in, e_other, virt_feats, wa, wa_other))
-    state, wb, wb_other = tie((state, wb, wb_other))
-    wu, wd = prep_call(wb, wb_other)
+        (pos_late, local_blocks, virt_blocks, node_count), (order, node_feats, e_in, e_other, virt_feats, w))
+    state, w = tie((state, w))
+    wu, wd = prep_call(w)
     result = far_call((pos, exp_blocks, node_count), (xe, q, state, wv, x_own, wo, wu, wd))
     received = lax.all_to_all(result, ("y", "c"), 0, 0, tiled=True)
     return place_call(pos, received, order).T

time: 172 us -> 150 us (0.87); the launches traced: 170 us -> 150 us
  waiting for transfers between devices: 51.2 us -> 25.2 us
  starting transfers between devices: 42 us -> 52.2 us
    all_gather x2 -> x1, waiting for transfers between devices: 15.5 us -> 0.01 us  [shards(): w = lax.all_gather(w, ('y', 'c'), axis=0, tiled=True).reshape(CD, D, D)]
    all_to_all x1, starting transfers between devices: 4.69 us -> 13.7 us  [shards(): xe = lax.all_to_all(sending, ('y', 'c'), 0, 0, tiled=True)]
    ppermute x3 -> x1, starting transfers between devices: 1.64 us -> 8.3 us  [swap(): return [lax.ppermute(t, 'c', SWAP) for t in arrays]]
    ppermute x9 -> x6, starting transfers between devices: 14.6 us -> 8.35 us  [exchange(): lax.ppermute(blocks[k], 'x', ring(NX, k))]
    ppermute x9 -> x6, waiting for transfers between devices: 22.9 us -> 16.8 us  [exchange(): lax.ppermute(blocks[k], 'x', ring(NX, k))]
    ppermute x1, waiting for transfers between devices: 5.52 us -> 0.01 us  [shards(): lax.ppermute(edge, ('z', 'x', 'y', 'c'), [(i * CD + h, (i + s) * CD + h)...]
    ppermute x4, waiting for transfers between devices: 4.74 us -> 1.89 us  [both_z(): lax.ppermute(a, 'z', ring(NZ, 1))]
    ppermute x4, waiting for transfers between devices: 0.01 us -> 2.76 us  [both_z(): lax.ppermute(b, 'z', ring(NZ, -1))]
  transfers between devices with their start and end apart: 27 -> 21, of which waited for: 11 -> 9; matrix products, arithmetic and copies ran while one was open for 1% -> 0% of each run, Pallas kernels for 15% -> 16%
where the time goes in v3:
time: 150 us
  starting transfers between devices  52.2 us (35%)
  Pallas kernels  45 us (30%)
  waiting for transfers between devices  25.2 us (17%)
  between operations  13.6 us (9%)
  blocking collectives  10.7 us (7%)
  local copies, waits for them, and re-layouts  3.16 us (2%)
    ppermute x6, waiting for transfers between devices, exchange(): lax.ppermute(blocks[k], 'x', ring(NX, k))  16.8 us
    pallas_call x1, Pallas kernels, near_call(): pl.pallas_call(near_kernel, out_shape=shapes, in_specs=[sspec()] * len(sc...  14.8 us
    ppermute x4, starting transfers between devices, both_z(): lax.ppermute(b, 'z', ring(NZ, -1))  14 us
    pallas_call x1, Pallas kernels, far_call(): pl.pallas_call(far_kernel, out_shape=sds(D, CL), in_specs=[sspec()] * len...  13.8 us
    all_to_all x1, starting transfers between devices, shards(): xe = lax.all_to_all(sending, ('y', 'c'), 0, 0, tiled=True)  13.7 us
    all_to_all x1, blocking collectives, shards(): received = lax.all_to_all(result, ('y', 'c'), 0, 0, tiled=True)  10.7 us
    ppermute x6, starting transfers between devices, exchange(): lax.ppermute(blocks[k], 'x', ring(NX, k))  8.35 us
    ppermute x1, starting transfers between devices, swap(): return [lax.ppermute(t, 'c', SWAP) for t in arrays]  8.3 us
  transfers between devices with their start and end apart: 21, of which 9 were waited for; matrix products, arithmetic and copies ran while one was open for 0% of the time, Pallas kernels for 16%

profile of v3, /device:TPU:1, one launch (start us, length us, event | category | flops | bytes accessed | tf_op | source)
XLA Modules:
  0.0 149.9 jit_solution(6862894079094177421)
XLA Ops:
  6.5 0.6 stack.23.pos.refs_0_
  7.2 3.6 %first.1 = (f32[128,512]{1,0:T(8,128)}, f32[128,512]{1,0:T(8,128)}) custom-call(s32[5]{0:T(128)} %stack.23.pos.refs_0_, s32[8,128]{1,0:T(8,128)} %bitcast.17, f32[1024,512]{1,0:T(8,128)} %nodes_ref.1), custom_call_target="tpu_custom_call" | custom-call | flops 1000000000 | bytes 3145728 | tf_op jit(solution)/shard_map/first/pallas_call | solution.py:107
  10.8 0.0 copy-start
  10.8 6.5 %collective-permute-start.1 = (f32[128,512]{1,0:T(8,128)}, f32[128,512]{1,0:T(8,128)S(1)}, u32[]{:S(2)}, u32[]{:S(2)}) collective-permute-start(f32[128,512]{1,0:T(8,128)} %get-tuple-element.53.refs_5_), channel_id=1, source_target_pairs={{0,224},{32,0},{64,32},{96,64},{128,96},{160,128},{192,160},{224,1... | collective-permute-start | bytes 786440 | tf_op jit(solution)/shard_map/ppermute | solution.py:465
  17.3 3.0 %setup.1 = (s32[96]{0:T(128)}, s32[48]{0:T(128)}, f32[512,512]{1,0:T(8,128)}) custom-call(s32[5]{0:T(128)} %stack.23.pos.refs_0_, s32[8,6]{1,0:T(8,128)} %exp_ref.3, f32[64,512]{1,0:T(8,128)} %bitcast.24, f32[64,512]{1,0:T(8,128)} %bitcast.25, f32[64,512]{1,0:T(8,128)} %bitcast.26, f32[64,512]{1,0:T(8,128)} %bitcast.27, f32[512,128]{1,0:T(8,128)} %up.1, ...), custom_call_target="tpu_custom_call" | custom-call | flops 1000 | bytes 2097152 | tf_op jit(solution)/shard_map/setup/pallas_call | solution.py:158
  20.4 1.3 collective-permute-start.4
  21.6 2.4 %collective-permute-start.3 = (s32[96]{0:T(128)}, s32[96]{0:T(128)S(1)}, u32[]{:S(2)}, u32[]{:S(2)}) collective-permute-start(s32[96]{0:T(128)} %get-tuple-element.59.refs_1_), channel_id=1, source_target_pairs={{0,16},{8,24},{16,0},{24,8},{1,17},{9,25},{17,1},{25,9},{2,18},{10... | collective-permute-start | bytes 1160 | tf_op jit(solution)/shard_map/ppermute | solution.py:472
  24.1 1.2 collective-permute-start.2
  25.2 0.0 collective-permute-done.4.refs_4_
  25.3 0.3 collective-permute-done.3.refs_3_
  25.6 1.2 collective-permute-done.2.refs_2_
  26.8 0.0 collective-permute-done.1.refs_6_
  26.8 0.0 collective-permute-done.refs_7_
  26.8 0.0 all-gather.2.cloned.1.call-update
  26.9 0.1 collective-permute-start.5
  27.0 2.7 %collective-permute-start.6 = (f32[128,512]{1,0:T(8,128)S(1)}, f32[128,512]{1,0:T(8,128)S(1)}, u32[]{:S(2)}, u32[]{:S(2)}) collective-permute-start(f32[128,512]{1,0:T(8,128)S(1)} %collective-permute-done.1.refs_6_), channel_id=1, source_target_pairs={{0,224},{32,0},{64,32},{96,64},{128,96},{160,128},{192,160},{224,1... | collective-permute-start | bytes 786440 | tf_op jit(solution)/shard_map/ppermute | solution.py:465
  29.6 2.2 %collective-permute-start.9 = (f32[128,512]{1,0:T(8,128)S(1)}, f32[128,512]{1,0:T(8,128)S(1)}, u32[]{:S(2)}, u32[]{:S(2)}) collective-permute-start(f32[128,512]{1,0:T(8,128)S(1)} %copy-done.9), channel_id=1, source_target_pairs={{0,8},{1,9},{8,16},{9,17},{16,24},{17,25},{24,32},{25,33},{32,40},... | collective-permute-start | bytes 786440 | tf_op jit(solution)/shard_map/ppermute | solution.py:484
  31.8 0.6 copy-done.3
  32.5 0.7 pick.2
  33.1 1.0 collective-permute-start.10
  34.1 2.5 %collective-permute-start.11 = (f32[144,512]{1,0:T(8,128)S(1)}, f32[144,512]{1,0:T(8,128)S(1)}, u32[]{:S(2)}, u32[]{:S(2)}) collective-permute-start(f32[144,512]{1,0:T(8,128)S(1)} %get-tuple-element.65), channel_id=1, source_target_pairs={{0,16},{8,24},{16,0},{24,8},{1,17},{9,25},{17,1},{25,9},{2,18},{10... | collective-permute-start | bytes 884744 | tf_op jit(solution)/shard_map/ppermute | solution.py:481
  36.6 2.0 %collective-permute-start.12 = (f32[144,512]{1,0:T(8,128)S(1)}, f32[144,512]{1,0:T(8,128)S(1)}, u32[]{:S(2)}, u32[]{:S(2)}) collective-permute-start(f32[144,512]{1,0:T(8,128)S(1)} %get-tuple-element.66), channel_id=1, source_target_pairs={{0,24},{8,0},{16,8},{24,16},{1,25},{9,1},{17,9},{25,17},{2,26},{10... | collective-permute-start | bytes 884744 | tf_op jit(solution)/shard_map/ppermute | solution.py:481
  38.6 0.0 copy-start.8
  38.6 4.1 %collective-permute-start.8 = (f32[128,512]{1,0:T(8,128)S(1)}, f32[128,512]{1,0:T(8,128)S(1)}, u32[]{:S(2)}, u32[]{:S(2)}) collective-permute-start(f32[128,512]{1,0:T(8,128)S(1)} %collective-permute-done.6.refs_5_), channel_id=1, source_target_pairs={{0,224},{32,0},{64,32},{96,64},{128,96},{160,128},{192,160},{224,1... | collective-permute-start | bytes 786440 | tf_op jit(solution)/shard_map/ppermute | solution.py:465
  42.6 8.0 %collective-permute-done.11.refs_2_ = f32[144,512]{1,0:T(8,128)S(1)} collective-permute-done((f32[144,512]{1,0:T(8,128)S(1)}, f32[144,512]{1,0:T(8,128)S(1)}, u32[]{:S(2)}, u32[]{:S(2)}) %collective-permute-start.11) | collective-permute-done | bytes 294944 | tf_op jit(solution)/shard_map/ppermute | solution.py:481
  50.6 0.0 collective-permute-done.12.refs_3_
  50.7 0.8 collective-permute-start.14
  51.4 0.8 collective-permute-start.13
  52.2 2.8 %collective-permute-done.14.refs_10_ = f32[64,512]{1,0:T(8,128)S(1)} collective-permute-done((f32[64,512]{1,0:T(8,128)S(1)}, f32[64,512]{1,0:T(8,128)S(1)}, u32[]{:S(2)}, u32[]{:S(2)}) %collective-permute-start.14) | collective-permute-done | bytes 131104 | tf_op jit(solution)/shard_map/ppermute | solution.py:465
  55.0 1.9 %collective-permute-done.13.refs_9_ = f32[64,512]{1,0:T(8,128)S(1)} collective-permute-done((f32[64,512]{1,0:T(8,128)S(1)}, f32[64,512]{1,0:T(8,128)S(1)}, u32[]{:S(2)}, u32[]{:S(2)}) %collective-permute-start.13) | collective-permute-done | bytes 131104 | tf_op jit(solution)/shard_map/ppermute | solution.py:465
  56.8 0.7 pick.3
  57.6 0.4 collective-permute-start.16
  58.0 0.9 collective-permute-start.17
  58.9 1.6 %collective-permute-start.18 = (f32[240,512]{1,0:T(8,128)S(1)}, f32[240,512]{1,0:T(8,128)S(1)}, u32[]{:S(2)}, u32[]{:S(2)}) collective-permute-start(f32[240,512]{1,0:T(8,128)S(1)} %get-tuple-element.76), channel_id=1, source_target_pairs={{0,24},{8,0},{16,8},{24,16},{1,25},{9,1},{17,9},{25,17},{2,26},{10... | collective-permute-start | bytes 1474568 | tf_op jit(solution)/shard_map/ppermute | solution.py:481
  60.5 8.3 %collective-permute-start.15 = (f32[128,512]{1,0:T(8,128)S(1)}, f32[128,512]{1,0:T(8,128)S(1)}, u32[]{:S(2)}, u32[]{:S(2)}) collective-permute-start(f32[128,512]{1,0:T(8,128)S(1)} %collective-permute-done.9.e_in), channel_id=1, source_target_pairs={{0,1},{1,0},{2,3},{3,2},{4,5},{5,4},{6,7},{7,6},{8,9},{9,8},{10,11... | collective-permute-start | bytes 786440 | tf_op jit(solution)/shard_map/ppermute | solution.py:468
  68.8 1.2 collective-permute-done.15.e_other
  70.0 4.8 %collective-permute-done.17.refs_6_ = f32[240,512]{1,0:T(8,128)S(1)} collective-permute-done((f32[240,512]{1,0:T(8,128)S(1)}, f32[240,512]{1,0:T(8,128)S(1)}, u32[]{:S(2)}, u32[]{:S(2)}) %collective-permute-start.17) | collective-permute-done | bytes 491552 | tf_op jit(solution)/shard_map/ppermute | solution.py:481
  74.8 4.0 %collective-permute-done.18.refs_7_ = f32[240,512]{1,0:T(8,128)S(1)} collective-permute-done((f32[240,512]{1,0:T(8,128)S(1)}, f32[240,512]{1,0:T(8,128)S(1)}, u32[]{:S(2)}, u32[]{:S(2)}) %collective-permute-start.18) | collective-permute-done | bytes 491552 | tf_op jit(solution)/shard_map/ppermute | solution.py:481
  78.8 2.0 %send.1 = f32[768,512]{1,0:T(8,128)} custom-call(s32[48]{0:T(128)S(1)} %copy-done.4, f32[144,512]{1,0:T(8,128)S(1)} %get-tuple-element.78.refs_0_, f32[144,512]{1,0:T(8,128)S(1)} %collective-permute-done.10.refs_1_, f32[144,512]{1,0:T(8,128)S(1)} %collective-permute-done.11.refs_2_, f32[144,512]{1,0:T(8,128)S(1)} %collective-permute-done.12.refs_3_, ...), custom_call_target="tpu_custom_call" | custom-call | bytes 6291456 | tf_op jit(solution)/shard_map/send/pallas_call | solution.py:433
  80.8 13.7 %all-to-all-start = ((f32[8,96,512]{2,1,0:T(8,128)}), f32[8,96,512]{2,1,0:T(8,128)S(1)}, u32[]{:S(2)}, u32[]{:S(2)}) async-start(f32[8,96,512]{2,1,0:T(8,128)} %bitcast.10), calls=%async_computation | async-start | bytes 3145728 | tf_op jit(solution)/shard_map/all_to_all | solution.py:503
  94.5 0.7 copy.14.local_ref
  95.2 14.8 %near.1 = (f32[128,512]{1,0:T(8,128)}, bf16[2,4,256,512]{3,2,1,0:T(8,128)(2,1)}, bf16[2,4,128,512]{3,2,1,0:T(8,128)(2,1)}, bf16[2,512,512]{2,1,0:T(8,128)(2,1)}, f32[4,256,128]{2,1,0:T(8,128)}) custom-call(s32[5]{0:T(128)} %stack.23.pos.refs_0_, s32[8,3]{1,0:T(8,128)} %copy.14.local_ref, s32[8]{0:T(128)} %virt_ref.1, s32[256]{0:T(256)} %count_ref.3, ...), custom_call_target="tpu_custom_call" | custom-call | flops 6000000000 | bytes 16777216 | tf_op jit(solution)/shard_map/near/pallas_call | solution.py:239
  109.9 4.3 %prep.1 = (bf16[2,512,1024]{2,1,0:T(8,128)(2,1)}, bf16[2,1024,512]{2,1,0:T(8,128)(2,1)}) custom-call(f32[8,512,512]{2,1,0:T(8,128)} %bitcast.21), custom_call_target="tpu_custom_call" | custom-call | flops 10000000 | bytes 8388608 | tf_op jit(solution)/shard_map/prep/pallas_call | solution.py:268
  114.2 1.0 all-to-all-done
  115.2 1.2 copy-done.6
  116.4 13.8 %far.1 = f32[512,128]{1,0:T(8,128)} custom-call(s32[5]{0:T(128)} %stack.23.pos.refs_0_, s32[8,6]{1,0:T(8,128)} %exp_ref.3, s32[256]{0:T(256)} %count_ref.3, f32[768,512]{1,0:T(8,128)} %bitcast.22, bf16[2,4,256,512]{3,2,1,0:T(8,128)(2,1)} %get-tuple-element.90.q_hbm, f32[4,256,128]{2,1,0:T(8,128)} %get-tuple-element.92.s_hbm, ...), custom_call_target="tpu_custom_call" | custom-call | flops 6000000000 | bytes 16777216 | tf_op jit(solution)/shard_map/far/pallas_call | solution.py:346
  130.2 10.7 %all_to_all.22 = f32[8,64,128]{2,1,0:T(8,128)S(1)} all-to-all(f32[8,64,128]{2,1,0:T(8,128)} %bitcast.23), channel_id=1, replica_groups=mesh['z'=8,'x'=4,'y'=4,'c'=2] {'y','c'}, dimensions={0} | all-to-all | bytes 524288 | tf_op jit(solution)/shard_map/all_to_all | solution.py:511
  140.9 2.1 %place.1 = f32[64,1024]{1,0:T(8,128)} custom-call(s32[5]{0:T(128)S(1)} %copy-done.2, f32[512,128]{1,0:T(8,128)S(1)} %bitcast.16, s32[8,128]{1,0:T(8,128)S(1)} %bitcast.19), custom_call_target="tpu_custom_call" | custom-call | flops 400000000 | bytes 1048576 | tf_op jit(solution)/shard_map/place/pallas_call | solution.py:376
  (31 shorter events, 0.1 us)
Async XLA Ops:
  6.5 88.6 %all-gather.2.cloned.1.call-start = ((), (), s32[]{:S(2)}) async-start(), calls=%async_computation.2 | async-start | bytes 9437184 | tf_op jit(solution)/shard_map/all_gather | solution.py:475
  7.2 24.6 %copy-start.1 = (s32[5]{0:T(128)S(1)}, s32[5]{0:T(128)}, u32[]{:S(2)}) copy-start(s32[5]{0:T(128)} %stack.23.pos.refs_0_) | copy-start | bytes 64
  10.8 18.8 %copy-start.9 = (f32[128,512]{1,0:T(8,128)S(1)}, f32[128,512]{1,0:T(8,128)}, u32[]{:S(2)}) copy-start(f32[128,512]{1,0:T(8,128)} %get-tuple-element.69) | copy-start | bytes 786436
  10.8 21.0 %copy-start = (f32[128,512]{1,0:T(8,128)S(1)}, f32[128,512]{1,0:T(8,128)}, u32[]{:S(2)}) copy-start(f32[128,512]{1,0:T(8,128)} %get-tuple-element.53.refs_5_) | copy-start | bytes 786436
  10.8 16.0 %collective-permute-start.1 = (f32[128,512]{1,0:T(8,128)}, f32[128,512]{1,0:T(8,128)S(1)}, u32[]{:S(2)}, u32[]{:S(2)}) collective-permute-start(f32[128,512]{1,0:T(8,128)} %get-tuple-element.53.refs_5_), channel_id=1, source_target_pairs={{0,224},{32,0},{64,32},{96,64},{128,96},{160,128},{192,160},{224,1... | collective-permute-start | bytes 786440 | tf_op jit(solution)/shard_map/ppermute | solution.py:465
  17.3 9.5 %collective-permute-start = (f32[128,512]{1,0:T(8,128)}, f32[128,512]{1,0:T(8,128)S(1)}, u32[]{:S(2)}, u32[]{:S(2)}) collective-permute-start(f32[128,512]{1,0:T(8,128)} %get-tuple-element.53.refs_5_), channel_id=1, source_target_pairs={{0,32},{32,64},{64,96},{96,128},{128,160},{160,192},{192,224},{224... | collective-permute-start | bytes 786440 | tf_op jit(solution)/shard_map/ppermute | solution.py:465
  20.3 58.5 %copy-start.4 = (s32[48]{0:T(128)S(1)}, s32[48]{0:T(128)}, u32[]{:S(2)}) copy-start(s32[48]{0:T(128)} %get-tuple-element.52.row) | copy-start | bytes 580
  20.4 4.9 %collective-permute-start.4 = (s32[96]{0:T(128)}, s32[96]{0:T(128)S(1)}, u32[]{:S(2)}, u32[]{:S(2)}) collective-permute-start(s32[96]{0:T(128)} %get-tuple-element.59.refs_1_), channel_id=1, source_target_pairs={{0,8},{8,16},{16,24},{24,0},{1,9},{9,17},{17,25},{25,1},{2,10},{10... | collective-permute-start | bytes 1160 | tf_op jit(solution)/shard_map/ppermute | solution.py:472
  21.6 4.0 %collective-permute-start.3 = (s32[96]{0:T(128)}, s32[96]{0:T(128)S(1)}, u32[]{:S(2)}, u32[]{:S(2)}) collective-permute-start(s32[96]{0:T(128)} %get-tuple-element.59.refs_1_), channel_id=1, source_target_pairs={{0,16},{8,24},{16,0},{24,8},{1,17},{9,25},{17,1},{25,9},{2,18},{10... | collective-permute-start | bytes 1160 | tf_op jit(solution)/shard_map/ppermute | solution.py:472
  24.1 2.7 %collective-permute-start.2 = (s32[96]{0:T(128)}, s32[96]{0:T(128)S(1)}, u32[]{:S(2)}, u32[]{:S(2)}) collective-permute-start(s32[96]{0:T(128)} %get-tuple-element.59.refs_1_), channel_id=1, source_target_pairs={{0,24},{8,0},{16,8},{24,16},{1,25},{9,1},{17,9},{25,17},{2,26},{10... | collective-permute-start | bytes 1160 | tf_op jit(solution)/shard_map/ppermute | solution.py:472
  26.9 9.7 %collective-permute-start.5 = (f32[128,512]{1,0:T(8,128)S(1)}, f32[128,512]{1,0:T(8,128)S(1)}, u32[]{:S(2)}, u32[]{:S(2)}) collective-permute-start(f32[128,512]{1,0:T(8,128)S(1)} %collective-permute-done.refs_7_), channel_id=1, source_target_pairs={{0,32},{32,64},{64,96},{96,128},{128,160},{160,192},{192,224},{224... | collective-permute-start | bytes 786440 | tf_op jit(solution)/shard_map/ppermute | solution.py:465
  27.0 11.6 %collective-permute-start.6 = (f32[128,512]{1,0:T(8,128)S(1)}, f32[128,512]{1,0:T(8,128)S(1)}, u32[]{:S(2)}, u32[]{:S(2)}) collective-permute-start(f32[128,512]{1,0:T(8,128)S(1)} %collective-permute-done.1.refs_6_), channel_id=1, source_target_pairs={{0,224},{32,0},{64,32},{96,64},{128,96},{160,128},{192,160},{224,1... | collective-permute-start | bytes 786440 | tf_op jit(solution)/shard_map/ppermute | solution.py:465
  29.6 8.9 %collective-permute-start.9 = (f32[128,512]{1,0:T(8,128)S(1)}, f32[128,512]{1,0:T(8,128)S(1)}, u32[]{:S(2)}, u32[]{:S(2)}) collective-permute-start(f32[128,512]{1,0:T(8,128)S(1)} %copy-done.9), channel_id=1, source_target_pairs={{0,8},{1,9},{8,16},{9,17},{16,24},{17,25},{24,32},{25,33},{32,40},... | collective-permute-start | bytes 786440 | tf_op jit(solution)/shard_map/ppermute | solution.py:484
  31.8 0.6 copy-start.3
  33.1 9.5 %collective-permute-start.10 = (f32[144,512]{1,0:T(8,128)S(1)}, f32[144,512]{1,0:T(8,128)S(1)}, u32[]{:S(2)}, u32[]{:S(2)}) collective-permute-start(f32[144,512]{1,0:T(8,128)S(1)} %get-tuple-element.64), channel_id=1, source_target_pairs={{0,8},{8,16},{16,24},{24,0},{1,9},{9,17},{17,25},{25,1},{2,10},{10... | collective-permute-start | bytes 884744 | tf_op jit(solution)/shard_map/ppermute | solution.py:481
  34.1 16.5 %collective-permute-start.11 = (f32[144,512]{1,0:T(8,128)S(1)}, f32[144,512]{1,0:T(8,128)S(1)}, u32[]{:S(2)}, u32[]{:S(2)}) collective-permute-start(f32[144,512]{1,0:T(8,128)S(1)} %get-tuple-element.65), channel_id=1, source_target_pairs={{0,16},{8,24},{16,0},{24,8},{1,17},{9,25},{17,1},{25,9},{2,18},{10... | collective-permute-start | bytes 884744 | tf_op jit(solution)/shard_map/ppermute | solution.py:481
  36.6 14.0 %collective-permute-start.12 = (f32[144,512]{1,0:T(8,128)S(1)}, f32[144,512]{1,0:T(8,128)S(1)}, u32[]{:S(2)}, u32[]{:S(2)}) collective-permute-start(f32[144,512]{1,0:T(8,128)S(1)} %get-tuple-element.66), channel_id=1, source_target_pairs={{0,24},{8,0},{16,8},{24,16},{1,25},{9,1},{17,9},{25,17},{2,26},{10... | collective-permute-start | bytes 884744 | tf_op jit(solution)/shard_map/ppermute | solution.py:481
  38.5 12.1 %collective-permute-start.7 = (f32[128,512]{1,0:T(8,128)S(1)}, f32[128,512]{1,0:T(8,128)S(1)}, u32[]{:S(2)}, u32[]{:S(2)}) collective-permute-start(f32[128,512]{1,0:T(8,128)S(1)} %collective-permute-done.5.refs_6_), channel_id=1, source_target_pairs={{0,32},{32,64},{64,96},{96,128},{128,160},{160,192},{192,224},{224... | collective-permute-start | bytes 786440 | tf_op jit(solution)/shard_map/ppermute | solution.py:465
  38.6 42.3 %copy-start.8 = (f32[128,512]{1,0:T(8,128)}, f32[128,512]{1,0:T(8,128)S(1)}, u32[]{:S(2)}) copy-start(f32[128,512]{1,0:T(8,128)S(1)} %collective-permute-done.9.e_in) | copy-start | bytes 786436
  38.6 12.1 %collective-permute-start.8 = (f32[128,512]{1,0:T(8,128)S(1)}, f32[128,512]{1,0:T(8,128)S(1)}, u32[]{:S(2)}, u32[]{:S(2)}) collective-permute-start(f32[128,512]{1,0:T(8,128)S(1)} %collective-permute-done.6.refs_5_), channel_id=1, source_target_pairs={{0,224},{32,0},{64,32},{96,64},{128,96},{160,128},{192,160},{224,1... | collective-permute-start | bytes 786440 | tf_op jit(solution)/shard_map/ppermute | solution.py:465
  50.7 4.3 %collective-permute-start.14 = (f32[64,512]{1,0:T(8,128)S(1)}, f32[64,512]{1,0:T(8,128)S(1)}, u32[]{:S(2)}, u32[]{:S(2)}) collective-permute-start(f32[64,512]{1,0:T(8,128)S(1)} %slice.7), channel_id=1, source_target_pairs={{0,224},{32,0},{64,32},{96,64},{128,96},{160,128},{192,160},{224,1... | collective-permute-start | bytes 393224 | tf_op jit(solution)/shard_map/ppermute | solution.py:465
  51.4 5.4 %collective-permute-start.13 = (f32[64,512]{1,0:T(8,128)S(1)}, f32[64,512]{1,0:T(8,128)S(1)}, u32[]{:S(2)}, u32[]{:S(2)}) collective-permute-start(f32[64,512]{1,0:T(8,128)S(1)} %slice.6), channel_id=1, source_target_pairs={{0,32},{32,64},{64,96},{96,128},{128,160},{160,192},{192,224},{224... | collective-permute-start | bytes 393224 | tf_op jit(solution)/shard_map/ppermute | solution.py:465
  57.6 12.4 %collective-permute-start.16 = (f32[240,512]{1,0:T(8,128)S(1)}, f32[240,512]{1,0:T(8,128)S(1)}, u32[]{:S(2)}, u32[]{:S(2)}) collective-permute-start(f32[240,512]{1,0:T(8,128)S(1)} %get-tuple-element.74), channel_id=1, source_target_pairs={{0,8},{8,16},{16,24},{24,0},{1,9},{9,17},{17,25},{25,1},{2,10},{10... | collective-permute-start | bytes 1474568 | tf_op jit(solution)/shard_map/ppermute | solution.py:481
  58.0 16.8 %collective-permute-start.17 = (f32[240,512]{1,0:T(8,128)S(1)}, f32[240,512]{1,0:T(8,128)S(1)}, u32[]{:S(2)}, u32[]{:S(2)}) collective-permute-start(f32[240,512]{1,0:T(8,128)S(1)} %get-tuple-element.75), channel_id=1, source_target_pairs={{0,16},{8,24},{16,0},{24,8},{1,17},{9,25},{17,1},{25,9},{2,18},{10... | collective-permute-start | bytes 1474568 | tf_op jit(solution)/shard_map/ppermute | solution.py:481
  58.9 19.9 %collective-permute-start.18 = (f32[240,512]{1,0:T(8,128)S(1)}, f32[240,512]{1,0:T(8,128)S(1)}, u32[]{:S(2)}, u32[]{:S(2)}) collective-permute-start(f32[240,512]{1,0:T(8,128)S(1)} %get-tuple-element.76), channel_id=1, source_target_pairs={{0,24},{8,0},{16,8},{24,16},{1,25},{9,1},{17,9},{25,17},{2,26},{10... | collective-permute-start | bytes 1474568 | tf_op jit(solution)/shard_map/ppermute | solution.py:481
  60.5 9.5 %collective-permute-start.15 = (f32[128,512]{1,0:T(8,128)S(1)}, f32[128,512]{1,0:T(8,128)S(1)}, u32[]{:S(2)}, u32[]{:S(2)}) collective-permute-start(f32[128,512]{1,0:T(8,128)S(1)} %collective-permute-done.9.e_in), channel_id=1, source_target_pairs={{0,1},{1,0},{2,3},{3,2},{4,5},{5,4},{6,7},{7,6},{8,9},{9,8},{10,11... | collective-permute-start | bytes 786440 | tf_op jit(solution)/shard_map/ppermute | solution.py:468
  70.0 10.8 %copy-start.10 = (f32[128,512]{1,0:T(8,128)}, f32[128,512]{1,0:T(8,128)S(1)}, u32[]{:S(2)}) copy-start(f32[128,512]{1,0:T(8,128)S(1)} %collective-permute-done.15.e_other) | copy-start | bytes 786436
  80.8 13.7 %copy-start.7 = (s32[8,3]{0,1:T(4,128)S(1)}, s32[8,3]{0,1:T(4,128)}, u32[]{:S(2)}) copy-start(s32[8,3]{0,1:T(4,128)} %param.16) | copy-start | bytes 292
  80.8 34.4 %all-to-all-start = ((f32[8,96,512]{2,1,0:T(8,128)}), f32[8,96,512]{2,1,0:T(8,128)S(1)}, u32[]{:S(2)}, u32[]{:S(2)}) async-start(f32[8,96,512]{2,1,0:T(8,128)} %bitcast.10), calls=%async_computation | async-start | bytes 3145728 | tf_op jit(solution)/shard_map/all_to_all | solution.py:503
  115.2 1.2 copy-start.6
  116.4 24.5 %copy-start.2 = (s32[5]{0:T(128)S(1)}, s32[5]{0:T(128)}, u32[]{:S(2)}) copy-start(s32[5]{0:T(128)} %stack.23.pos.refs_0_) | copy-start | bytes 64
  116.4 24.5 %copy-start.5 = (s32[1024]{0:T(1024)S(1)}, s32[1024]{0:T(1024)}, u32[]{:S(2)}) copy-start(s32[1024]{0:T(1024)} %param.14) | copy-start | bytes 12292
Sparse Core Ops, SparseCore 0:
  27.0 53.3 all-gather.1

commit v4 on v3

--- a/solution.py
+++ b/solution.py
@@ -76,7 +76,8 @@
     return jnp.concatenate(parts, 1)
 
 
-def first_kernel(pos, order_hbm, nodes_hbm, piece_out, edge_out, order_ref, nodes, sems):
+def first_kernel(pos, exp_ref, order_hbm, nodes_hbm, piece_out, edge_out, table, row,
+                 order_ref, nodes, seen, starts, widths, sems):
     base, head, c = pos[0], pos[1], pos[2]
     step = 2 * CL
     parts = CD * CL // step
@@ -85,6 +86,32 @@
                               sems.at[i + 1]) for i in range(parts)]
     for copy in fetch:
         copy.start()
+    z, x = pos[3], pos[4]
+    start = 0
+    for group in GROUPS:
+        for p, s in enumerate(group):
+            starts[s] = start + p * CAP
+            widths[s] = len(group) * CAP
+        start += NX * len(group) * CAP
+    for i in range(NX * NZ * CAP):
+        table[i] = 0
+    for i in range(NZ * NX):
+        seen[i] = 0
+
+    def place(i, carry):
+        for e in range(NE):
+            block = exp_ref[i, e]
+            owner = lax.shift_right_logical(block, 3)
+            rank = seen[owner]
+            seen[owner] = rank + 1
+            oz = lax.shift_right_logical(owner, 2)
+            back = lax.bitwise_and(x - lax.bitwise_and(owner, NX - 1), NX - 1)
+            table[back * (NZ * CAP) + oz * CAP + rank] = lax.bitwise_and(block, CD - 1)
+            off = lax.bitwise_and(oz - z, NZ - 1)
+            row[i * NE + e] = (starts[off] + back * widths[off] + rank) * PR
+        return carry
+
+    lax.fori_loop(0, CD, place, 0)
     fetch[0].wait()
     order = (order_ref[...] - base).astype(F32)
     mine = pltpu.roll(order, lax.rem(CL - head * PR, CL), 1)
@@ -103,70 +130,43 @@
     edge_out[...] = rows[CL:]
 
 
-def first_call(pos, order, nodes):
+def first_call(pos, exp_blocks, order, nodes):
     return pl.pallas_call(
         first_kernel,
-        out_shape=[sds(CL, D), sds(CL, D)],
-        in_specs=[sspec(), hspec(), hspec()],
-        out_specs=[vspec()] * 2,
+        out_shape=[sds(CL, D), sds(CL, D), sds(NX * NZ * CAP, dtype=jnp.int32), sds(CD * NE, dtype=jnp.int32)],
+        in_specs=[sspec(), sspec(), hspec(), hspec()],
+        out_specs=[vspec()] * 2 + [sspec()] * 2,
         scratch_shapes=[pltpu.VMEM((CD, CL), jnp.int32), pltpu.VMEM((CD * CL, D), F32),
-                        pltpu.SemaphoreType.DMA((5,))],
+                        pltpu.SMEM((NZ * NX,), jnp.int32), pltpu.SMEM((NZ,), jnp.int32),
+                        pltpu.SMEM((NZ,), jnp.int32), pltpu.SemaphoreType.DMA((5,))],
         compiler_params=params(60),
         cost_estimate=cost(10**9, 3 << 20),
         name="first",
-    )(pos, order, nodes)
-
-
-def setup_kernel(pos, exp_ref, q, k, v, o, up, down, table, row, out, seen, starts, widths, sems):
+    )(pos, exp_blocks, order, nodes)
+
+
+def pack_kernel(q, k, v, o, up, down, out, sems):
     pairs = [(w, out.at[i * HD:(i + 1) * HD, :]) for i, w in enumerate((q, k, v, o))]
     pairs.append((down, out.at[2 * CL:3 * CL, :]))
     pairs += [(up.at[j * CL:(j + 1) * CL, :], out.at[3 * CL:, j * CL:(j + 1) * CL]) for j in range(4)]
     copies = [pltpu.make_async_copy(src, dst, sems.at[i]) for i, (src, dst) in enumerate(pairs)]
     for copy in copies:
         copy.start()
-    z, x = pos[3], pos[4]
-    start = 0
-    for group in GROUPS:
-        for p, s in enumerate(group):
-            starts[s] = start + p * CAP
-            widths[s] = len(group) * CAP
-        start += NX * len(group) * CAP
-    for i in range(NX * NZ * CAP):
-        table[i] = 0
-    for i in range(NZ * NX):
-        seen[i] = 0
-
-    def place(i, carry):
-        for e in range(NE):
-            block = exp_ref[i, e]
-            owner = lax.shift_right_logical(block, 3)
-            rank = seen[owner]
-            seen[owner] = rank + 1
-            oz = lax.shift_right_logical(owner, 2)
-            back = lax.bitwise_and(x - lax.bitwise_and(owner, NX - 1), NX - 1)
-            table[back * (NZ * CAP) + oz * CAP + rank] = lax.bitwise_and(block, CD - 1)
-            off = lax.bitwise_and(oz - z, NZ - 1)
-            row[i * NE + e] = (starts[off] + back * widths[off] + rank) * PR
-        return carry
-
-    lax.fori_loop(0, CD, place, 0)
     for copy in copies:
         copy.wait()
 
 
-def setup_call(pos, exp_blocks, *w):
-    return pl.pallas_call(
-        setup_kernel,
-        out_shape=[sds(NX * NZ * CAP, dtype=jnp.int32), sds(CD * NE, dtype=jnp.int32),
-                   sds(D, D)],
-        in_specs=[sspec()] * 2 + [hspec()] * 6,
-        out_specs=[sspec()] * 2 + [vspec()],
-        scratch_shapes=[pltpu.SMEM((NZ * NX,), jnp.int32), pltpu.SMEM((NZ,), jnp.int32), pltpu.SMEM((NZ,), jnp.int32),
-                        pltpu.SemaphoreType.DMA((9,))],
+def pack_call(*w):
+    return pl.pallas_call(
+        pack_kernel,
+        out_shape=sds(D, D),
+        in_specs=[hspec()] * 6,
+        out_specs=vspec(),
+        scratch_shapes=[pltpu.SemaphoreType.DMA((9,))],
         compiler_params=params(60),
         cost_estimate=cost(1000, 2 << 20),
-        name="setup",
-    )(pos, exp_blocks, *w)
+        name="pack",
+    )(*w)
 
 
 def near_kernel(pos, local_ref, virt_ref, count_ref, order_ref, nodes_ref, e_in, e_other, virtual_ref, w_hbm,
@@ -279,9 +279,10 @@
 
 def far_kernel(pos, exp_ref, count_ref, xe_ref, q_hbm, s_hbm, v_hbm, x_hbm, o_hbm, u_hbm, d_hbm,
                out_ref, kh, kl, att, q, st, v, x, wo, u, d, sems):
-    copies = [pltpu.make_async_copy(src, dst, sems.at[i]) for i, (src, dst) in enumerate(zip(
-        (q_hbm, s_hbm, v_hbm, x_hbm, o_hbm, u_hbm, d_hbm), (q, st, v, x, wo, u, d)))]
-    for copy in copies[:3]:
+    first = [pltpu.make_async_copy(q_hbm.at[:, p], q.at[:, p], sems.at[p]) for p in range(NY)]
+    later = [pltpu.make_async_copy(src, dst, sems.at[NY + i]) for i, (src, dst) in enumerate(zip(
+        (s_hbm, v_hbm, x_hbm, o_hbm, u_hbm, d_hbm), (st, v, x, wo, u, d)))]
+    for copy in first:
         copy.start()
     head = pos[1]
     hi, lo = split2(xe_ref[...])
@@ -317,20 +318,22 @@
         o = (dot3(*split2(a), v[0, p], v[1, p], NT) + st[p] * scale) / total
         att[p] = jnp.where(lowq, o[:CL], o[CL:])
 
-    for copy in copies[:3]:
-        copy.wait()
-    for copy in copies[3:]:
+    first[0].wait()
+    ahead = scores(0)
+    for copy in later:
         copy.start()
-
-    def body(i, carry):
-        one, two = scores(2 * i), scores(2 * i + 1)
-        attend(2 * i, one)
-        attend(2 * i + 1, two)
-        return carry
-
-    lax.fori_loop(0, NY // 2, body, 0)
+    for p in range(NY):
+        s = ahead
+        if p + 1 < NY:
+            first[p + 1].wait()
+            ahead = scores(p + 1)
+        if p == 0:
+            later[0].wait()
+            later[1].wait()
+        attend(p, s)
+
     ah, al = split2(jnp.concatenate([att[p] for p in range(NY)], 1))
-    for copy in copies[3:]:
+    for copy in later[2:]:
         copy.wait()
     r = x[...] + dot3(ah, al, wo[0], wo[1], NT)
     mean = jnp.sum(r, axis=1, keepdims=True) * (1.0 / D)
@@ -349,8 +352,8 @@
         in_specs=[sspec()] * len(scalars) + [vspec()] + [hspec()] * (len(arrays) - 1),
         out_specs=vspec(),
         scratch_shapes=[pltpu.VMEM((EK, D), BF), pltpu.VMEM((EK, D), BF), pltpu.VMEM((NY, CL, 2 * HD), F32)]
-        + [pltpu.VMEM(a.shape, a.dtype) for a in arrays[1:]] + [pltpu.SemaphoreType.DMA((len(arrays) - 1,))],
-        compiler_params=params(60),
+        + [pltpu.VMEM(a.shape, a.dtype) for a in arrays[1:]] + [pltpu.SemaphoreType.DMA((NY + len(arrays) - 2,))],
+        compiler_params=params(50),
         cost_estimate=cost(6 * 10**9, 16 << 20, 1 << 20),
         name="far",
     )(*scalars, *arrays)
@@ -456,7 +459,7 @@
     pos = jnp.stack([(z * NX + x) * (CD * CL), head, c, z, x]).astype(jnp.int32)
     order = order.reshape(CD, CL)
 
-    piece, edge = first_call(pos, order, node_feats)
+    piece, edge, table, row = first_call(pos, exp_blocks, order, node_feats)
 
     half = CL // 2
     tie = lax.optimization_barrier
@@ -468,7 +471,7 @@
         return [lax.ppermute(t, "c", SWAP) for t in arrays]
 
     up, down = both_z(piece, piece)
-    table, row, w = setup_call(pos, exp_blocks, w_query.T, w_key.T, w_value.T, w_out.T, w_up, w_down)
+    w = pack_call(w_query.T, w_key.T, w_value.T, w_out.T, w_up, w_down)
     tables = [table] + [lax.ppermute(table, "x", ring(NX, -k)) for k in range(1, NX)]
     held = {0: (piece,), 7: (up,), 1: (down,)}
     up, down, w, edge, *tables = tie((up, down, w, edge, *tables))

time: 150 us -> 148 us (0.987)
  waiting for transfers between devices: 25.2 us -> 31.6 us
  starting transfers between devices: 52.2 us -> 45.9 us
  local copies, waits for them, and re-layouts: 3.16 us -> 1.42 us
    ppermute x6, waiting for transfers between devices: 16.8 us -> 24.1 us  [exchange(): lax.ppermute(blocks[k], 'x', ring(NX, k))]
    all_to_all x1, starting transfers between devices: 13.7 us -> 10.2 us  [shards(): xe = lax.all_to_all(sending, ('y', 'c'), 0, 0, tiled=True)]
    ppermute x1, starting transfers between devices: 8.3 us -> 5.24 us  [swap(): return [lax.ppermute(t, 'c', SWAP) for t in arrays]]
    unnamed x23 -> x33, local copies, waits for them, and re-layouts: 2.51 us -> 0.74 us
    ppermute x3, waiting for transfers between devices: 1.59 us -> 0.01 us  [shards(): lax.ppermute(table, 'x', ring(NX, -k))]
  transfers between devices with their start and end apart: 21 -> 21, of which waited for: 9 -> 9; matrix products, arithmetic and copies ran while one was open for 0% -> 0% of each run, Pallas kernels for 16% -> 15%
where the time goes in v4:
time: 148 us
  starting transfers between devices  45.9 us (31%)
  Pallas kernels  45.1 us (30%)
  waiting for transfers between devices  31.6 us (21%)
  between operations  13.7 us (9%)
  blocking collectives  10.3 us (7%)
    ppermute x6, waiting for transfers between devices, exchange(): lax.ppermute(blocks[k], 'x', ring(NX, k))  24.1 us
    pallas_call x1, Pallas kernels, near_call(): pl.pallas_call(near_kernel, out_shape=shapes, in_specs=[sspec()] * len(sc...  14.7 us
    pallas_call x1, Pallas kernels, far_call(): pl.pallas_call(far_kernel, out_shape=sds(D, CL), in_specs=[sspec()] * len...  14.6 us
    ppermute x4, starting transfers between devices, both_z(): lax.ppermute(b, 'z', ring(NZ, -1))  13.5 us
    all_to_all x1, blocking collectives, shards(): received = lax.all_to_all(result, ('y', 'c'), 0, 0, tiled=True)  10.3 us
    all_to_all x1, starting transfers between devices, shards(): xe = lax.all_to_all(sending, ('y', 'c'), 0, 0, tiled=True)  10.2 us
    ppermute x6, starting transfers between devices, exchange(): lax.ppermute(blocks[k], 'x', ring(NX, k))  7.54 us
    ppermute x1, starting transfers between devices, swap(): return [lax.ppermute(t, 'c', SWAP) for t in arrays]  5.24 us
  transfers between devices with their start and end apart: 21, of which 9 were waited for; matrix products, arithmetic and copies ran while one was open for 0% of the time, Pallas kernels for 15%

profile of v4, /device:TPU:1, one launch (start us, length us, event | category | flops | bytes accessed | tf_op | source)
XLA Modules:
  0.0 148.0 jit_solution(14651919168359997187)
XLA Ops:
  6.5 0.7 stack.23.pos.refs_0_
  7.2 3.6 %first.1 = (f32[128,512]{1,0:T(8,128)}, f32[128,512]{1,0:T(8,128)}, s32[96]{0:T(128)}, s32[48]{0:T(128)}) custom-call(s32[5]{0:T(128)} %stack.23.pos.refs_0_, s32[8,6]{1,0:T(8,128)} %exp_ref.3, s32[8,128]{1,0:T(8,128)} %bitcast.18, f32[1024,512]{1,0:T(8,128)} %nodes_ref.1), custom_call_target="tpu_custom_call" | custom-call | flops 1000000000 | bytes 3145728 | tf_op jit(solution)/shard_map/first/pallas_call | solution.py:134
  10.8 0.0 copy-start
  10.8 6.5 %collective-permute-start.1 = (f32[128,512]{1,0:T(8,128)}, f32[128,512]{1,0:T(8,128)S(1)}, u32[]{:S(2)}, u32[]{:S(2)}) collective-permute-start(f32[128,512]{1,0:T(8,128)} %get-tuple-element.52.refs_5_), channel_id=1, source_target_pairs={{0,224},{32,0},{64,32},{96,64},{128,96},{160,128},{192,160},{224,1... | collective-permute-start | bytes 786440 | tf_op jit(solution)/shard_map/ppermute | solution.py:468
  17.3 1.2 collective-permute-start.4
  18.5 2.5 %collective-permute-start.3 = (s32[96]{0:T(128)}, s32[96]{0:T(128)S(1)}, u32[]{:S(2)}, u32[]{:S(2)}) collective-permute-start(s32[96]{0:T(128)} %get-tuple-element.57.refs_1_), channel_id=1, source_target_pairs={{0,16},{8,24},{16,0},{24,8},{1,17},{9,25},{17,1},{25,9},{2,18},{10... | collective-permute-start | bytes 1160 | tf_op jit(solution)/shard_map/ppermute | solution.py:475
  21.0 1.2 collective-permute-start.2
  22.1 2.3 %pack.1 = f32[512,512]{1,0:T(8,128)} custom-call(f32[64,512]{1,0:T(8,128)} %bitcast.23, f32[64,512]{1,0:T(8,128)} %bitcast.24, f32[64,512]{1,0:T(8,128)} %bitcast.25, f32[64,512]{1,0:T(8,128)} %bitcast.26, f32[512,128]{1,0:T(8,128)} %up.1, f32[128,512]{1,0:T(8,128)} %down.1), custom_call_target="tpu_custom_call" | custom-call | flops 1000 | bytes 2097152 | tf_op jit(solution)/shard_map/pack/pallas_call | solution.py:160
  24.4 0.0 collective-permute-done.4.refs_4_
  24.4 0.0 collective-permute-done.3.refs_3_
  24.4 0.0 collective-permute-done.1.refs_6_
  24.5 1.1 collective-permute-done.refs_7_
  25.6 0.0 all-gather.2.cloned.1.call-update
  25.6 0.1 collective-permute-start.5
  25.7 2.7 %collective-permute-start.6 = (f32[128,512]{1,0:T(8,128)S(1)}, f32[128,512]{1,0:T(8,128)S(1)}, u32[]{:S(2)}, u32[]{:S(2)}) collective-permute-start(f32[128,512]{1,0:T(8,128)S(1)} %collective-permute-done.1.refs_6_), channel_id=1, source_target_pairs={{0,224},{32,0},{64,32},{96,64},{128,96},{160,128},{192,160},{224,1... | collective-permute-start | bytes 786440 | tf_op jit(solution)/shard_map/ppermute | solution.py:468
  28.4 3.1 %collective-permute-start.9 = (f32[128,512]{1,0:T(8,128)S(1)}, f32[128,512]{1,0:T(8,128)S(1)}, u32[]{:S(2)}, u32[]{:S(2)}) collective-permute-start(f32[128,512]{1,0:T(8,128)S(1)} %copy-done.14), channel_id=1, source_target_pairs={{0,8},{1,9},{8,16},{9,17},{16,24},{17,25},{24,32},{25,33},{32,40},... | collective-permute-start | bytes 786440 | tf_op jit(solution)/shard_map/ppermute | solution.py:487
  31.5 0.7 pick.2
  32.2 1.3 collective-permute-start.10
  33.5 1.3 collective-permute-start.11
  34.8 2.0 %collective-permute-start.12 = (f32[144,512]{1,0:T(8,128)S(1)}, f32[144,512]{1,0:T(8,128)S(1)}, u32[]{:S(2)}, u32[]{:S(2)}) collective-permute-start(f32[144,512]{1,0:T(8,128)S(1)} %get-tuple-element.64), channel_id=1, source_target_pairs={{0,24},{8,0},{16,8},{24,16},{1,25},{9,1},{17,9},{25,17},{2,26},{10... | collective-permute-start | bytes 884744 | tf_op jit(solution)/shard_map/ppermute | solution.py:484
  36.8 0.0 copy-start.13
  36.8 4.3 %collective-permute-start.8 = (f32[128,512]{1,0:T(8,128)S(1)}, f32[128,512]{1,0:T(8,128)S(1)}, u32[]{:S(2)}, u32[]{:S(2)}) collective-permute-start(f32[128,512]{1,0:T(8,128)S(1)} %collective-permute-done.6.refs_5_), channel_id=1, source_target_pairs={{0,224},{32,0},{64,32},{96,64},{128,96},{160,128},{192,160},{224,1... | collective-permute-start | bytes 786440 | tf_op jit(solution)/shard_map/ppermute | solution.py:468
  41.1 9.4 %collective-permute-done.11.refs_2_ = f32[144,512]{1,0:T(8,128)S(1)} collective-permute-done((f32[144,512]{1,0:T(8,128)S(1)}, f32[144,512]{1,0:T(8,128)S(1)}, u32[]{:S(2)}, u32[]{:S(2)}) %collective-permute-start.11) | collective-permute-done | bytes 294944 | tf_op jit(solution)/shard_map/ppermute | solution.py:484
  50.5 0.1 collective-permute-start.14
  50.6 1.5 collective-permute-start.13
  52.0 2.8 %collective-permute-done.14.refs_10_ = f32[64,512]{1,0:T(8,128)S(1)} collective-permute-done((f32[64,512]{1,0:T(8,128)S(1)}, f32[64,512]{1,0:T(8,128)S(1)}, u32[]{:S(2)}, u32[]{:S(2)}) %collective-permute-start.14) | collective-permute-done | bytes 131104 | tf_op jit(solution)/shard_map/ppermute | solution.py:468
  54.8 1.6 %collective-permute-done.13.refs_9_ = f32[64,512]{1,0:T(8,128)S(1)} collective-permute-done((f32[64,512]{1,0:T(8,128)S(1)}, f32[64,512]{1,0:T(8,128)S(1)}, u32[]{:S(2)}, u32[]{:S(2)}) %collective-permute-start.13) | collective-permute-done | bytes 131104 | tf_op jit(solution)/shard_map/ppermute | solution.py:468
  56.4 0.7 pick.3
  57.1 0.3 collective-permute-start.16
  57.4 1.0 collective-permute-start.17
  58.4 1.6 %collective-permute-start.18 = (f32[240,512]{1,0:T(8,128)S(1)}, f32[240,512]{1,0:T(8,128)S(1)}, u32[]{:S(2)}, u32[]{:S(2)}) collective-permute-start(f32[240,512]{1,0:T(8,128)S(1)} %get-tuple-element.74), channel_id=1, source_target_pairs={{0,24},{8,0},{16,8},{24,16},{1,25},{9,1},{17,9},{25,17},{2,26},{10... | collective-permute-start | bytes 1474568 | tf_op jit(solution)/shard_map/ppermute | solution.py:484
  60.0 5.2 %collective-permute-start.15 = (f32[128,512]{1,0:T(8,128)S(1)}, f32[128,512]{1,0:T(8,128)S(1)}, u32[]{:S(2)}, u32[]{:S(2)}) collective-permute-start(f32[128,512]{1,0:T(8,128)S(1)} %collective-permute-done.9.e_in), channel_id=1, source_target_pairs={{0,1},{1,0},{2,3},{3,2},{4,5},{5,4},{6,7},{7,6},{8,9},{9,8},{10,11... | collective-permute-start | bytes 786440 | tf_op jit(solution)/shard_map/ppermute | solution.py:471
  65.3 1.2 collective-permute-done.15.e_other
  66.4 2.2 %collective-permute-done.16.refs_5_ = f32[240,512]{1,0:T(8,128)S(1)} collective-permute-done((f32[240,512]{1,0:T(8,128)S(1)}, f32[240,512]{1,0:T(8,128)S(1)}, u32[]{:S(2)}, u32[]{:S(2)}) %collective-permute-start.16) | collective-permute-done | bytes 491552 | tf_op jit(solution)/shard_map/ppermute | solution.py:484
  68.6 7.5 %collective-permute-done.17.refs_6_ = f32[240,512]{1,0:T(8,128)S(1)} collective-permute-done((f32[240,512]{1,0:T(8,128)S(1)}, f32[240,512]{1,0:T(8,128)S(1)}, u32[]{:S(2)}, u32[]{:S(2)}) %collective-permute-start.17) | collective-permute-done | bytes 491552 | tf_op jit(solution)/shard_map/ppermute | solution.py:484
  76.1 5.0 %collective-permute-done.18.refs_7_ = f32[240,512]{1,0:T(8,128)S(1)} collective-permute-done((f32[240,512]{1,0:T(8,128)S(1)}, f32[240,512]{1,0:T(8,128)S(1)}, u32[]{:S(2)}, u32[]{:S(2)}) %collective-permute-start.18) | collective-permute-done | bytes 491552 | tf_op jit(solution)/shard_map/ppermute | solution.py:484
  81.1 2.0 %send.1 = f32[768,512]{1,0:T(8,128)} custom-call(s32[48]{0:T(128)S(1)} %copy-done.4, f32[144,512]{1,0:T(8,128)S(1)} %get-tuple-element.76.refs_0_, f32[144,512]{1,0:T(8,128)S(1)} %collective-permute-done.10.refs_1_, f32[144,512]{1,0:T(8,128)S(1)} %collective-permute-done.11.refs_2_, f32[144,512]{1,0:T(8,128)S(1)} %collective-permute-done.12.refs_3_, ...), custom_call_target="tpu_custom_call" | custom-call | bytes 6291456 | tf_op jit(solution)/shard_map/send/pallas_call | solution.py:436
  83.2 10.2 %all-to-all-start = ((f32[8,96,512]{2,1,0:T(8,128)}), f32[8,96,512]{2,1,0:T(8,128)}, u32[]{:S(2)}, u32[]{:S(2)}) async-start(f32[8,96,512]{2,1,0:T(8,128)} %bitcast.10), calls=%async_computation | async-start | bytes 3145728 | tf_op jit(solution)/shard_map/all_to_all | solution.py:506
  93.4 0.7 copy.14.local_ref
  94.0 14.7 %near.1 = (f32[128,512]{1,0:T(8,128)}, bf16[2,4,256,512]{3,2,1,0:T(8,128)(2,1)}, bf16[2,4,128,512]{3,2,1,0:T(8,128)(2,1)}, bf16[2,512,512]{2,1,0:T(8,128)(2,1)}, f32[4,256,128]{2,1,0:T(8,128)}) custom-call(s32[5]{0:T(128)} %stack.23.pos.refs_0_, s32[8,3]{1,0:T(8,128)} %copy.14.local_ref, s32[8]{0:T(128)} %virt_ref.1, s32[256]{0:T(256)} %count_ref.3, ...), custom_call_target="tpu_custom_call" | custom-call | flops 6000000000 | bytes 16777216 | tf_op jit(solution)/shard_map/near/pallas_call | solution.py:239
  108.8 0.0 copy-start.5
  108.8 0.0 copy-start.7
  108.9 4.4 %prep.1 = (bf16[2,512,1024]{2,1,0:T(8,128)(2,1)}, bf16[2,1024,512]{2,1,0:T(8,128)(2,1)}) custom-call(f32[8,512,512]{2,1,0:T(8,128)} %bitcast.22), custom_call_target="tpu_custom_call" | custom-call | flops 10000000 | bytes 8388608 | tf_op jit(solution)/shard_map/prep/pallas_call | solution.py:268
  113.3 0.9 all-to-all-done
  114.2 0.0 copy-start.6
  114.2 14.6 %far.1 = f32[512,128]{1,0:T(8,128)S(1)} custom-call(s32[5]{0:T(128)S(1)} %copy-done.2, s32[8,6]{1,0:T(8,128)S(1)} %copy-done.5, s32[256]{0:T(256)S(1)} %copy-done.7, f32[768,512]{1,0:T(8,128)} %bitcast.11.xe_ref, bf16[2,4,256,512]{3,2,1,0:T(8,128)(2,1)} %get-tuple-element.88.q_hbm, f32[4,256,128]{2,1,0:T(8,128)S(1)} %copy-done.10, ...), custom_call_target="tpu_custom_call" | custom-call | flops 6000000000 | bytes 16777216 | tf_op jit(solution)/shard_map/far/pallas_call | solution.py:349
  128.8 10.3 %all_to_all.22 = f32[8,64,128]{2,1,0:T(8,128)S(1)} all-to-all(f32[8,64,128]{2,1,0:T(8,128)S(1)} %bitcast.16), channel_id=1, replica_groups=mesh['z'=8,'x'=4,'y'=4,'c'=2] {'y','c'}, dimensions={0} | all-to-all | bytes 524288 | tf_op jit(solution)/shard_map/all_to_all | solution.py:514
  139.1 2.1 %place.1 = f32[64,1024]{1,0:T(8,128)} custom-call(s32[5]{0:T(128)S(1)} %copy-done.2, f32[512,128]{1,0:T(8,128)S(1)} %bitcast.17, s32[8,128]{1,0:T(8,128)S(1)} %bitcast.20), custom_call_target="tpu_custom_call" | custom-call | flops 400000000 | bytes 1048576 | tf_op jit(solution)/shard_map/place/pallas_call | solution.py:379
  (41 shorter events, 0.1 us)
Async XLA Ops:
  6.5 87.5 %all-gather.2.cloned.1.call-start = ((), (), s32[]{:S(2)}) async-start(), calls=%async_computation.2 | async-start | bytes 9437184 | tf_op jit(solution)/shard_map/all_gather | solution.py:478
  10.8 17.6 %copy-start.14 = (f32[128,512]{1,0:T(8,128)S(1)}, f32[128,512]{1,0:T(8,128)}, u32[]{:S(2)}) copy-start(f32[128,512]{1,0:T(8,128)} %get-tuple-element.67) | copy-start | bytes 786436
  10.8 20.7 %copy-start = (f32[128,512]{1,0:T(8,128)S(1)}, f32[128,512]{1,0:T(8,128)}, u32[]{:S(2)}) copy-start(f32[128,512]{1,0:T(8,128)} %get-tuple-element.52.refs_5_) | copy-start | bytes 786436
  10.8 20.7 %copy-start.1 = (s32[5]{0:T(128)S(1)}, s32[5]{0:T(128)}, u32[]{:S(2)}) copy-start(s32[5]{0:T(128)} %stack.23.pos.refs_0_) | copy-start | bytes 64
  10.8 20.7 %copy-start.3 = (s32[96]{0:T(128)S(1)}, s32[96]{0:T(128)}, u32[]{:S(2)}) copy-start(s32[96]{0:T(128)} %get-tuple-element.57.refs_1_) | copy-start | bytes 1156
  10.8 13.6 %collective-permute-start.1 = (f32[128,512]{1,0:T(8,128)}, f32[128,512]{1,0:T(8,128)S(1)}, u32[]{:S(2)}, u32[]{:S(2)}) collective-permute-start(f32[128,512]{1,0:T(8,128)} %get-tuple-element.52.refs_5_), channel_id=1, source_target_pairs={{0,224},{32,0},{64,32},{96,64},{128,96},{160,128},{192,160},{224,1... | collective-permute-start | bytes 786440 | tf_op jit(solution)/shard_map/ppermute | solution.py:468
  17.3 8.3 %collective-permute-start = (f32[128,512]{1,0:T(8,128)}, f32[128,512]{1,0:T(8,128)S(1)}, u32[]{:S(2)}, u32[]{:S(2)}) collective-permute-start(f32[128,512]{1,0:T(8,128)} %get-tuple-element.52.refs_5_), channel_id=1, source_target_pairs={{0,32},{32,64},{64,96},{96,128},{128,160},{160,192},{192,224},{224... | collective-permute-start | bytes 786440 | tf_op jit(solution)/shard_map/ppermute | solution.py:468
  17.3 7.1 %collective-permute-start.4 = (s32[96]{0:T(128)}, s32[96]{0:T(128)S(1)}, u32[]{:S(2)}, u32[]{:S(2)}) collective-permute-start(s32[96]{0:T(128)} %get-tuple-element.57.refs_1_), channel_id=1, source_target_pairs={{0,8},{8,16},{16,24},{24,0},{1,9},{9,17},{17,25},{25,1},{2,10},{10... | collective-permute-start | bytes 1160 | tf_op jit(solution)/shard_map/ppermute | solution.py:475
  18.5 5.9 %collective-permute-start.3 = (s32[96]{0:T(128)}, s32[96]{0:T(128)S(1)}, u32[]{:S(2)}, u32[]{:S(2)}) collective-permute-start(s32[96]{0:T(128)} %get-tuple-element.57.refs_1_), channel_id=1, source_target_pairs={{0,16},{8,24},{16,0},{24,8},{1,17},{9,25},{17,1},{25,9},{2,18},{10... | collective-permute-start | bytes 1160 | tf_op jit(solution)/shard_map/ppermute | solution.py:475
  21.0 3.5 %collective-permute-start.2 = (s32[96]{0:T(128)}, s32[96]{0:T(128)S(1)}, u32[]{:S(2)}, u32[]{:S(2)}) collective-permute-start(s32[96]{0:T(128)} %get-tuple-element.57.refs_1_), channel_id=1, source_target_pairs={{0,24},{8,0},{16,8},{24,16},{1,25},{9,1},{17,9},{25,17},{2,26},{10... | collective-permute-start | bytes 1160 | tf_op jit(solution)/shard_map/ppermute | solution.py:475
  24.4 56.7 %copy-start.4 = (s32[48]{0:T(128)S(1)}, s32[48]{0:T(128)}, u32[]{:S(2)}) copy-start(s32[48]{0:T(128)} %get-tuple-element.51.row) | copy-start | bytes 580
  25.6 9.2 %collective-permute-start.5 = (f32[128,512]{1,0:T(8,128)S(1)}, f32[128,512]{1,0:T(8,128)S(1)}, u32[]{:S(2)}, u32[]{:S(2)}) collective-permute-start(f32[128,512]{1,0:T(8,128)S(1)} %collective-permute-done.refs_7_), channel_id=1, source_target_pairs={{0,32},{32,64},{64,96},{96,128},{128,160},{160,192},{192,224},{224... | collective-permute-start | bytes 786440 | tf_op jit(solution)/shard_map/ppermute | solution.py:468
  25.7 11.1 %collective-permute-start.6 = (f32[128,512]{1,0:T(8,128)S(1)}, f32[128,512]{1,0:T(8,128)S(1)}, u32[]{:S(2)}, u32[]{:S(2)}) collective-permute-start(f32[128,512]{1,0:T(8,128)S(1)} %collective-permute-done.1.refs_6_), channel_id=1, source_target_pairs={{0,224},{32,0},{64,32},{96,64},{128,96},{160,128},{192,160},{224,1... | collective-permute-start | bytes 786440 | tf_op jit(solution)/shard_map/ppermute | solution.py:468
  28.4 8.4 %collective-permute-start.9 = (f32[128,512]{1,0:T(8,128)S(1)}, f32[128,512]{1,0:T(8,128)S(1)}, u32[]{:S(2)}, u32[]{:S(2)}) collective-permute-start(f32[128,512]{1,0:T(8,128)S(1)} %copy-done.14), channel_id=1, source_target_pairs={{0,8},{1,9},{8,16},{9,17},{16,24},{17,25},{24,32},{25,33},{32,40},... | collective-permute-start | bytes 786440 | tf_op jit(solution)/shard_map/ppermute | solution.py:487
  32.2 8.9 %collective-permute-start.10 = (f32[144,512]{1,0:T(8,128)S(1)}, f32[144,512]{1,0:T(8,128)S(1)}, u32[]{:S(2)}, u32[]{:S(2)}) collective-permute-start(f32[144,512]{1,0:T(8,128)S(1)} %get-tuple-element.62), channel_id=1, source_target_pairs={{0,8},{8,16},{16,24},{24,0},{1,9},{9,17},{17,25},{25,1},{2,10},{10... | collective-permute-start | bytes 884744 | tf_op jit(solution)/shard_map/ppermute | solution.py:484
  33.5 17.0 %collective-permute-start.11 = (f32[144,512]{1,0:T(8,128)S(1)}, f32[144,512]{1,0:T(8,128)S(1)}, u32[]{:S(2)}, u32[]{:S(2)}) collective-permute-start(f32[144,512]{1,0:T(8,128)S(1)} %get-tuple-element.63), channel_id=1, source_target_pairs={{0,16},{8,24},{16,0},{24,8},{1,17},{9,25},{17,1},{25,9},{2,18},{10... | collective-permute-start | bytes 884744 | tf_op jit(solution)/shard_map/ppermute | solution.py:484
  34.8 15.7 %collective-permute-start.12 = (f32[144,512]{1,0:T(8,128)S(1)}, f32[144,512]{1,0:T(8,128)S(1)}, u32[]{:S(2)}, u32[]{:S(2)}) collective-permute-start(f32[144,512]{1,0:T(8,128)S(1)} %get-tuple-element.64), channel_id=1, source_target_pairs={{0,24},{8,0},{16,8},{24,16},{1,25},{9,1},{17,9},{25,17},{2,26},{10... | collective-permute-start | bytes 884744 | tf_op jit(solution)/shard_map/ppermute | solution.py:484
  36.8 13.7 %collective-permute-start.7 = (f32[128,512]{1,0:T(8,128)S(1)}, f32[128,512]{1,0:T(8,128)S(1)}, u32[]{:S(2)}, u32[]{:S(2)}) collective-permute-start(f32[128,512]{1,0:T(8,128)S(1)} %collective-permute-done.5.refs_6_), channel_id=1, source_target_pairs={{0,32},{32,64},{64,96},{96,128},{128,160},{160,192},{192,224},{224... | collective-permute-start | bytes 786440 | tf_op jit(solution)/shard_map/ppermute | solution.py:468
  36.8 46.4 %copy-start.13 = (f32[128,512]{1,0:T(8,128)}, f32[128,512]{1,0:T(8,128)S(1)}, u32[]{:S(2)}) copy-start(f32[128,512]{1,0:T(8,128)S(1)} %collective-permute-done.9.e_in) | copy-start | bytes 786436
  36.8 13.6 %collective-permute-start.8 = (f32[128,512]{1,0:T(8,128)S(1)}, f32[128,512]{1,0:T(8,128)S(1)}, u32[]{:S(2)}, u32[]{:S(2)}) collective-permute-start(f32[128,512]{1,0:T(8,128)S(1)} %collective-permute-done.6.refs_5_), channel_id=1, source_target_pairs={{0,224},{32,0},{64,32},{96,64},{128,96},{160,128},{192,160},{224,1... | collective-permute-start | bytes 786440 | tf_op jit(solution)/shard_map/ppermute | solution.py:468
  50.5 4.3 %collective-permute-start.14 = (f32[64,512]{1,0:T(8,128)S(1)}, f32[64,512]{1,0:T(8,128)S(1)}, u32[]{:S(2)}, u32[]{:S(2)}) collective-permute-start(f32[64,512]{1,0:T(8,128)S(1)} %slice.7), channel_id=1, source_target_pairs={{0,224},{32,0},{64,32},{96,64},{128,96},{160,128},{192,160},{224,1... | collective-permute-start | bytes 393224 | tf_op jit(solution)/shard_map/ppermute | solution.py:468
  50.6 5.8 %collective-permute-start.13 = (f32[64,512]{1,0:T(8,128)S(1)}, f32[64,512]{1,0:T(8,128)S(1)}, u32[]{:S(2)}, u32[]{:S(2)}) collective-permute-start(f32[64,512]{1,0:T(8,128)S(1)} %slice.6), channel_id=1, source_target_pairs={{0,32},{32,64},{64,96},{96,128},{128,160},{160,192},{192,224},{224... | collective-permute-start | bytes 393224 | tf_op jit(solution)/shard_map/ppermute | solution.py:468
  57.1 11.6 %collective-permute-start.16 = (f32[240,512]{1,0:T(8,128)S(1)}, f32[240,512]{1,0:T(8,128)S(1)}, u32[]{:S(2)}, u32[]{:S(2)}) collective-permute-start(f32[240,512]{1,0:T(8,128)S(1)} %get-tuple-element.72), channel_id=1, source_target_pairs={{0,8},{8,16},{16,24},{24,0},{1,9},{9,17},{17,25},{25,1},{2,10},{10... | collective-permute-start | bytes 1474568 | tf_op jit(solution)/shard_map/ppermute | solution.py:484
  57.4 18.7 %collective-permute-start.17 = (f32[240,512]{1,0:T(8,128)S(1)}, f32[240,512]{1,0:T(8,128)S(1)}, u32[]{:S(2)}, u32[]{:S(2)}) collective-permute-start(f32[240,512]{1,0:T(8,128)S(1)} %get-tuple-element.73), channel_id=1, source_target_pairs={{0,16},{8,24},{16,0},{24,8},{1,17},{9,25},{17,1},{25,9},{2,18},{10... | collective-permute-start | bytes 1474568 | tf_op jit(solution)/shard_map/ppermute | solution.py:484
  58.4 22.8 %collective-permute-start.18 = (f32[240,512]{1,0:T(8,128)S(1)}, f32[240,512]{1,0:T(8,128)S(1)}, u32[]{:S(2)}, u32[]{:S(2)}) collective-permute-start(f32[240,512]{1,0:T(8,128)S(1)} %get-tuple-element.74), channel_id=1, source_target_pairs={{0,24},{8,0},{16,8},{24,16},{1,25},{9,1},{17,9},{25,17},{2,26},{10... | collective-permute-start | bytes 1474568 | tf_op jit(solution)/shard_map/ppermute | solution.py:484
  60.0 6.4 %collective-permute-start.15 = (f32[128,512]{1,0:T(8,128)S(1)}, f32[128,512]{1,0:T(8,128)S(1)}, u32[]{:S(2)}, u32[]{:S(2)}) collective-permute-start(f32[128,512]{1,0:T(8,128)S(1)} %collective-permute-done.9.e_in), channel_id=1, source_target_pairs={{0,1},{1,0},{2,3},{3,2},{4,5},{5,4},{6,7},{7,6},{8,9},{9,8},{10,11... | collective-permute-start | bytes 786440 | tf_op jit(solution)/shard_map/ppermute | solution.py:471
  66.4 16.8 %copy-start.15 = (f32[128,512]{1,0:T(8,128)}, f32[128,512]{1,0:T(8,128)S(1)}, u32[]{:S(2)}) copy-start(f32[128,512]{1,0:T(8,128)S(1)} %collective-permute-done.15.e_other) | copy-start | bytes 786436
  83.2 10.2 %copy-start.12 = (s32[8,3]{0,1:T(4,128)S(1)}, s32[8,3]{0,1:T(4,128)}, u32[]{:S(2)}) copy-start(s32[8,3]{0,1:T(4,128)} %param.16) | copy-start | bytes 292
  83.2 31.0 %all-to-all-start = ((f32[8,96,512]{2,1,0:T(8,128)}), f32[8,96,512]{2,1,0:T(8,128)}, u32[]{:S(2)}, u32[]{:S(2)}) async-start(f32[8,96,512]{2,1,0:T(8,128)} %bitcast.10), calls=%async_computation | async-start | bytes 3145728 | tf_op jit(solution)/shard_map/all_to_all | solution.py:506
  108.8 5.4 %copy-start.2 = (s32[5]{0:T(128)S(1)}, s32[5]{0:T(128)}, u32[]{:S(2)}) copy-start(s32[5]{0:T(128)} %stack.23.pos.refs_0_) | copy-start | bytes 64
  108.8 5.4 %copy-start.5 = (s32[8,6]{1,0:T(8,128)S(1)}, s32[8,6]{1,0:T(8,128)}, u32[]{:S(2)}) copy-start(s32[8,6]{1,0:T(8,128)} %exp_ref.3) | copy-start | bytes 580
  108.8 5.4 %copy-start.7 = (s32[256]{0:T(256)S(1)}, s32[256]{0:T(256)}, u32[]{:S(2)}) copy-start(s32[256]{0:T(256)} %count_ref.3) | copy-start | bytes 3076
  108.8 5.4 %copy-start.8 = (bf16[2,4,128,512]{3,2,1,0:T(8,128)(2,1)S(1)}, bf16[2,4,128,512]{3,2,1,0:T(8,128)(2,1)}, u32[]{:S(2)}) copy-start(bf16[2,4,128,512]{3,2,1,0:T(8,128)(2,1)} %get-tuple-element.91.v_hbm) | copy-start | bytes 3145732
  108.8 5.4 %copy-start.9 = (bf16[2,512,512]{2,1,0:T(8,128)(2,1)S(1)}, bf16[2,512,512]{2,1,0:T(8,128)(2,1)}, u32[]{:S(2)}) copy-start(bf16[2,512,512]{2,1,0:T(8,128)(2,1)} %get-tuple-element.93.o_hbm) | copy-start | bytes 3145732
  108.8 5.4 %copy-start.10 = (f32[4,256,128]{2,1,0:T(8,128)S(1)}, f32[4,256,128]{2,1,0:T(8,128)}, u32[]{:S(2)}) copy-start(f32[4,256,128]{2,1,0:T(8,128)} %get-tuple-element.90.s_hbm) | copy-start | bytes 1572868
  108.8 5.4 %copy-start.11 = (f32[128,512]{1,0:T(8,128)S(1)}, f32[128,512]{1,0:T(8,128)}, u32[]{:S(2)}) copy-start(f32[128,512]{1,0:T(8,128)} %get-tuple-element.92.x_hbm) | copy-start | bytes 786436
  114.2 24.9 %copy-start.6 = (s32[1024]{0:T(1024)S(1)}, s32[1024]{0:T(1024)}, u32[]{:S(2)}) copy-start(s32[1024]{0:T(1024)} %param.14) | copy-start | bytes 12292
Sparse Core Ops, SparseCore 0:
  25.7 51.3 all-gather.1

commit v5 on v4

--- a/solution.py
+++ b/solution.py
@@ -26,7 +26,7 @@
 NT = (((1,), (1,)), ((), ()))
 NN = (((1,), (0,)), ((), ()))
 
-GROUPS = ((0, 1, 7), (2, 6, 3, 5, 4))
+GROUPS = ((0, 1, 7), (2, 6), (3, 5, 4))
 
 
 def split2(v):
@@ -318,20 +318,20 @@
         o = (dot3(*split2(a), v[0, p], v[1, p], NT) + st[p] * scale) / total
         att[p] = jnp.where(lowq, o[:CL], o[CL:])
 
-    first[0].wait()
-    ahead = scores(0)
+    for copy in first:
+        copy.wait()
     for copy in later:
         copy.start()
-    for p in range(NY):
-        s = ahead
-        if p + 1 < NY:
-            first[p + 1].wait()
-            ahead = scores(p + 1)
-        if p == 0:
-            later[0].wait()
-            later[1].wait()
-        attend(p, s)
-
+    later[0].wait()
+    later[1].wait()
+
+    def body(i, carry):
+        one, two = scores(2 * i), scores(2 * i + 1)
+        attend(2 * i, one)
+        attend(2 * i + 1, two)
+        return carry
+
+    lax.fori_loop(0, NY // 2, body, 0)
     ah, al = split2(jnp.concatenate([att[p] for p in range(NY)], 1))
     for copy in later[2:]:
         copy.wait()
@@ -492,15 +492,14 @@
     held[6], held[2] = (up,), (down,)
     up, down, *_ = tie((up, down, *one))
     one = exchange(one)
+    two = pick(GROUPS[1])
     up, down = both_z(up, down)
     held[5], held[3] = (up,), (down,)
-    up, down, e_in, *_ = tie((up, down, e_in, *one))
+    up, down, e_in, *_ = tie((up, down, e_in, *one, *two))
     held[4] = both_z(up[:half], down[half:])
-    two = pick(GROUPS[1])
-    (e_other,) = swap(tie((e_in, *two))[0])
-    arrived = one + exchange(two)
-    arrived = tie((e_other, *arrived))
-    e_other, arrived = arrived[0], arrived[1:]
+    three = pick(GROUPS[2])
+    (e_other,) = swap(tie((e_in, *three))[0])
+    e_other, *arrived = tie((e_other, *one, *exchange(two), *exchange(three)))
 
     sending = send_call(row, arrived)
     xe = lax.all_to_all(sending, ("y", "c"), 0, 0, tiled=True)

time: 148 us -> 142 us (0.959)
  waiting for transfers between devices: 31.6 us -> 20.5 us
  starting transfers between devices: 45.9 us -> 51.6 us
    ppermute x6 -> x9, waiting for transfers between devices: 24.1 us -> 15 us  [exchange(): lax.ppermute(blocks[k], 'x', ring(NX, k))]
    ppermute x6 -> x9, starting transfers between devices: 7.54 us -> 10.2 us  [exchange(): lax.ppermute(blocks[k], 'x', ring(NX, k))]
    pallas_call x1, Pallas kernels: 14.6 us -> 12.8 us  [far_call(): pl.pallas_call(far_kernel, out_shape=sds(D, CL), in_specs=[sspec()] * len...]
    ppermute x1, starting transfers between devices: 5.24 us -> 6.91 us  [swap(): return [lax.ppermute(t, 'c', SWAP) for t in arrays]]
  transfers between devices with their start and end apart: 21 -> 24, of which waited for: 9 -> 6; matrix products, arithmetic and copies ran while one was open for 0% -> 0% of each run, Pallas kernels for 15% -> 17%
where the time goes in v5:
time: 142 us
  starting transfers between devices  51.6 us (36%)
  Pallas kernels  44 us (31%)
  waiting for transfers between devices  20.5 us (14%)
  between operations  13.8 us (10%)
  blocking collectives  10.3 us (7%)
    ppermute x9, waiting for transfers between devices, exchange(): lax.ppermute(blocks[k], 'x', ring(NX, k))  15 us
    pallas_call x1, Pallas kernels, near_call(): pl.pallas_call(near_kernel, out_shape=shapes, in_specs=[sspec()] * len(sc...  14.8 us
    ppermute x4, starting transfers between devices, both_z(): lax.ppermute(b, 'z', ring(NZ, -1))  13.5 us
    pallas_call x1, Pallas kernels, far_call(): pl.pallas_call(far_kernel, out_shape=sds(D, CL), in_specs=[sspec()] * len...  12.8 us
    all_to_all x1, starting transfers between devices, shards(): xe = lax.all_to_all(sending, ('y', 'c'), 0, 0, tiled=True)  11.6 us
    all_to_all x1, blocking collectives, shards(): received = lax.all_to_all(result, ('y', 'c'), 0, 0, tiled=True)  10.3 us
    ppermute x9, starting transfers between devices, exchange(): lax.ppermute(blocks[k], 'x', ring(NX, k))  10.2 us
    ppermute x1, starting transfers between devices, swap(): return [lax.ppermute(t, 'c', SWAP) for t in arrays]  6.91 us
  transfers between devices with their start and end apart: 24, of which 6 were waited for; matrix products, arithmetic and copies ran while one was open for 0% of the time, Pallas kernels for 17%

profile of v5, /device:TPU:1, one launch (start us, length us, event | category | flops | bytes accessed | tf_op | source)
XLA Modules:
  0.0 141.6 jit_solution(8584981441456824648)
XLA Ops:
  6.5 0.6 stack.23.pos.refs_0_
  7.1 3.6 %first.1 = (f32[128,512]{1,0:T(8,128)}, f32[128,512]{1,0:T(8,128)}, s32[96]{0:T(128)}, s32[48]{0:T(128)}) custom-call(s32[5]{0:T(128)} %stack.23.pos.refs_0_, s32[8,6]{1,0:T(8,128)} %exp_ref.3, s32[8,128]{1,0:T(8,128)} %bitcast.18, f32[1024,512]{1,0:T(8,128)} %nodes_ref.1), custom_call_target="tpu_custom_call" | custom-call | flops 1000000000 | bytes 3145728 | tf_op jit(solution)/shard_map/first/pallas_call | solution.py:134
  10.7 0.0 copy-start
  10.7 6.5 %collective-permute-start.1 = (f32[128,512]{1,0:T(8,128)}, f32[128,512]{1,0:T(8,128)S(1)}, u32[]{:S(2)}, u32[]{:S(2)}) collective-permute-start(f32[128,512]{1,0:T(8,128)} %get-tuple-element.60.refs_5_), channel_id=1, source_target_pairs={{0,224},{32,0},{64,32},{96,64},{128,96},{160,128},{192,160},{224,1... | collective-permute-start | bytes 786440 | tf_op jit(solution)/shard_map/ppermute | solution.py:468
  17.2 1.2 collective-permute-start.4
  18.4 2.4 %collective-permute-start.3 = (s32[96]{0:T(128)}, s32[96]{0:T(128)S(1)}, u32[]{:S(2)}, u32[]{:S(2)}) collective-permute-start(s32[96]{0:T(128)} %get-tuple-element.65.refs_1_), channel_id=1, source_target_pairs={{0,16},{8,24},{16,0},{24,8},{1,17},{9,25},{17,1},{25,9},{2,18},{10... | collective-permute-start | bytes 1160 | tf_op jit(solution)/shard_map/ppermute | solution.py:475
  20.9 1.2 collective-permute-start.2
  22.0 2.3 %pack.1 = f32[512,512]{1,0:T(8,128)} custom-call(f32[64,512]{1,0:T(8,128)} %bitcast.23, f32[64,512]{1,0:T(8,128)} %bitcast.24, f32[64,512]{1,0:T(8,128)} %bitcast.25, f32[64,512]{1,0:T(8,128)} %bitcast.26, f32[512,128]{1,0:T(8,128)} %up.1, f32[128,512]{1,0:T(8,128)} %down.1), custom_call_target="tpu_custom_call" | custom-call | flops 1000 | bytes 2097152 | tf_op jit(solution)/shard_map/pack/pallas_call | solution.py:160
  24.3 0.0 collective-permute-done.3.refs_3_
  24.3 0.0 collective-permute-done.2.refs_2_
  24.4 1.1 collective-permute-done.refs_7_
  25.5 0.0 all-gather.2.cloned.1.call-update
  25.5 0.1 collective-permute-start.5
  25.6 2.7 %collective-permute-start.6 = (f32[128,512]{1,0:T(8,128)S(1)}, f32[128,512]{1,0:T(8,128)S(1)}, u32[]{:S(2)}, u32[]{:S(2)}) collective-permute-start(f32[128,512]{1,0:T(8,128)S(1)} %collective-permute-done.1.refs_6_), channel_id=1, source_target_pairs={{0,224},{32,0},{64,32},{96,64},{128,96},{160,128},{192,160},{224,1... | collective-permute-start | bytes 786440 | tf_op jit(solution)/shard_map/ppermute | solution.py:468
  28.3 3.1 %collective-permute-start.9 = (f32[128,512]{1,0:T(8,128)S(1)}, f32[128,512]{1,0:T(8,128)S(1)}, u32[]{:S(2)}, u32[]{:S(2)}) collective-permute-start(f32[128,512]{1,0:T(8,128)S(1)} %copy-done.14), channel_id=1, source_target_pairs={{0,8},{1,9},{8,16},{9,17},{16,24},{17,25},{24,32},{25,33},{32,40},... | collective-permute-start | bytes 786440 | tf_op jit(solution)/shard_map/ppermute | solution.py:487
  31.4 0.7 pick.3
  32.1 1.3 collective-permute-start.10
  33.4 1.3 collective-permute-start.11
  34.7 2.0 %collective-permute-start.12 = (f32[144,512]{1,0:T(8,128)S(1)}, f32[144,512]{1,0:T(8,128)S(1)}, u32[]{:S(2)}, u32[]{:S(2)}) collective-permute-start(f32[144,512]{1,0:T(8,128)S(1)} %get-tuple-element.72), channel_id=1, source_target_pairs={{0,24},{8,0},{16,8},{24,16},{1,25},{9,1},{17,9},{25,17},{2,26},{10... | collective-permute-start | bytes 884744 | tf_op jit(solution)/shard_map/ppermute | solution.py:484
  36.7 0.0 copy-start.13
  36.7 4.3 %collective-permute-start.8 = (f32[128,512]{1,0:T(8,128)S(1)}, f32[128,512]{1,0:T(8,128)S(1)}, u32[]{:S(2)}, u32[]{:S(2)}) collective-permute-start(f32[128,512]{1,0:T(8,128)S(1)} %collective-permute-done.6.refs_5_), channel_id=1, source_target_pairs={{0,224},{32,0},{64,32},{96,64},{128,96},{160,128},{192,160},{224,1... | collective-permute-start | bytes 786440 | tf_op jit(solution)/shard_map/ppermute | solution.py:468
  41.0 0.6 pick.4
  41.6 1.5 %collective-permute-start.16 = (f32[96,512]{1,0:T(8,128)S(1)}, f32[96,512]{1,0:T(8,128)S(1)}, u32[]{:S(2)}, u32[]{:S(2)}) collective-permute-start(f32[96,512]{1,0:T(8,128)S(1)} %get-tuple-element.77), channel_id=1, source_target_pairs={{0,8},{8,16},{16,24},{24,0},{1,9},{9,17},{17,25},{25,1},{2,10},{10... | collective-permute-start | bytes 589832 | tf_op jit(solution)/shard_map/ppermute | solution.py:484
  43.2 7.2 %collective-permute-done.11.refs_2_ = f32[144,512]{1,0:T(8,128)S(1)} collective-permute-done((f32[144,512]{1,0:T(8,128)S(1)}, f32[144,512]{1,0:T(8,128)S(1)}, u32[]{:S(2)}, u32[]{:S(2)}) %collective-permute-start.11) | collective-permute-done | bytes 294944 | tf_op jit(solution)/shard_map/ppermute | solution.py:484
  50.4 0.1 collective-permute-start.14
  50.5 1.5 %collective-permute-start.13 = (f32[64,512]{1,0:T(8,128)S(1)}, f32[64,512]{1,0:T(8,128)S(1)}, u32[]{:S(2)}, u32[]{:S(2)}) collective-permute-start(f32[64,512]{1,0:T(8,128)S(1)} %slice.6), channel_id=1, source_target_pairs={{0,32},{32,64},{64,96},{96,128},{128,160},{160,192},{192,224},{224... | collective-permute-start | bytes 393224 | tf_op jit(solution)/shard_map/ppermute | solution.py:468
  51.9 0.6 collective-permute-start.17
  52.6 2.1 %collective-permute-done.14.refs_8_ = f32[64,512]{1,0:T(8,128)S(1)} collective-permute-done((f32[64,512]{1,0:T(8,128)S(1)}, f32[64,512]{1,0:T(8,128)S(1)}, u32[]{:S(2)}, u32[]{:S(2)}) %collective-permute-start.14) | collective-permute-done | bytes 131104 | tf_op jit(solution)/shard_map/ppermute | solution.py:468
  54.7 1.5 %collective-permute-done.13.refs_7_ = f32[64,512]{1,0:T(8,128)S(1)} collective-permute-done((f32[64,512]{1,0:T(8,128)S(1)}, f32[64,512]{1,0:T(8,128)S(1)}, u32[]{:S(2)}, u32[]{:S(2)}) %collective-permute-start.13) | collective-permute-done | bytes 131104 | tf_op jit(solution)/shard_map/ppermute | solution.py:468
  56.2 0.7 pick.5
  56.9 0.1 collective-permute-start.19
  56.9 2.7 %collective-permute-start.20 = (f32[144,512]{1,0:T(8,128)S(1)}, f32[144,512]{1,0:T(8,128)S(1)}, u32[]{:S(2)}, u32[]{:S(2)}) collective-permute-start(f32[144,512]{1,0:T(8,128)S(1)} %get-tuple-element.85), channel_id=1, source_target_pairs={{0,16},{8,24},{16,0},{24,8},{1,17},{9,25},{17,1},{25,9},{2,18},{10... | collective-permute-start | bytes 884744 | tf_op jit(solution)/shard_map/ppermute | solution.py:484
  59.6 0.1 collective-permute-start.21
  59.7 6.9 %collective-permute-start.15 = (f32[128,512]{1,0:T(8,128)S(1)}, f32[128,512]{1,0:T(8,128)S(1)}, u32[]{:S(2)}, u32[]{:S(2)}) collective-permute-start(f32[128,512]{1,0:T(8,128)S(1)} %collective-permute-done.9.e_in), channel_id=1, source_target_pairs={{0,1},{1,0},{2,3},{3,2},{4,5},{5,4},{6,7},{7,6},{8,9},{9,8},{10,11... | collective-permute-start | bytes 786440 | tf_op jit(solution)/shard_map/ppermute | solution.py:471
  66.6 0.6 collective-permute-start.18
  67.2 7.8 %collective-permute-done.18.refs_7_ = f32[96,512]{1,0:T(8,128)S(1)} collective-permute-done((f32[96,512]{1,0:T(8,128)S(1)}, f32[96,512]{1,0:T(8,128)S(1)}, u32[]{:S(2)}, u32[]{:S(2)}) %collective-permute-start.18) | collective-permute-done | bytes 196640 | tf_op jit(solution)/shard_map/ppermute | solution.py:484
  75.0 2.0 %send.1 = f32[768,512]{1,0:T(8,128)} custom-call(s32[48]{0:T(128)S(1)} %copy-done.4, f32[144,512]{1,0:T(8,128)S(1)} %get-tuple-element.88.refs_0_, f32[144,512]{1,0:T(8,128)S(1)} %collective-permute-done.10.refs_1_, f32[144,512]{1,0:T(8,128)S(1)} %collective-permute-done.11.refs_2_, f32[144,512]{1,0:T(8,128)S(1)} %collective-permute-done.12.refs_3_, ...), custom_call_target="tpu_custom_call" | custom-call | bytes 6291456 | tf_op jit(solution)/shard_map/send/pallas_call | solution.py:436
  77.0 11.6 %all-to-all-start = ((f32[8,96,512]{2,1,0:T(8,128)}), f32[8,96,512]{2,1,0:T(8,128)}, u32[]{:S(2)}, u32[]{:S(2)}) async-start(f32[8,96,512]{2,1,0:T(8,128)} %bitcast.10), calls=%async_computation | async-start | bytes 3145728 | tf_op jit(solution)/shard_map/all_to_all | solution.py:505
  88.6 0.7 copy.14.local_ref
  89.3 14.8 %near.1 = (f32[128,512]{1,0:T(8,128)}, bf16[2,4,256,512]{3,2,1,0:T(8,128)(2,1)}, bf16[2,4,128,512]{3,2,1,0:T(8,128)(2,1)}, bf16[2,512,512]{2,1,0:T(8,128)(2,1)}, f32[4,256,128]{2,1,0:T(8,128)}) custom-call(s32[5]{0:T(128)} %stack.23.pos.refs_0_, s32[8,3]{1,0:T(8,128)} %copy.14.local_ref, s32[8]{0:T(128)} %virt_ref.1, s32[256]{0:T(256)} %count_ref.3, ...), custom_call_target="tpu_custom_call" | custom-call | flops 6000000000 | bytes 16777216 | tf_op jit(solution)/shard_map/near/pallas_call | solution.py:239
  104.1 0.0 copy-start.5
  104.1 0.0 copy-start.7
  104.1 4.5 %prep.1 = (bf16[2,512,1024]{2,1,0:T(8,128)(2,1)}, bf16[2,1024,512]{2,1,0:T(8,128)(2,1)}) custom-call(f32[8,512,512]{2,1,0:T(8,128)} %bitcast.22), custom_call_target="tpu_custom_call" | custom-call | flops 10000000 | bytes 8388608 | tf_op jit(solution)/shard_map/prep/pallas_call | solution.py:268
  108.6 0.8 all-to-all-done
  109.5 0.0 copy-start.6
  109.5 12.8 %far.1 = f32[512,128]{1,0:T(8,128)S(1)} custom-call(s32[5]{0:T(128)S(1)} %copy-done.2, s32[8,6]{1,0:T(8,128)S(1)} %copy-done.5, s32[256]{0:T(256)S(1)} %copy-done.7, f32[768,512]{1,0:T(8,128)} %bitcast.11.xe_ref, bf16[2,4,256,512]{3,2,1,0:T(8,128)(2,1)} %get-tuple-element.104.q_hbm, f32[4,256,128]{2,1,0:T(8,128)S(1)} %copy-done.10, ...), custom_call_target="tpu_custom_call" | custom-call | flops 6000000000 | bytes 16777216 | tf_op jit(solution)/shard_map/far/pallas_call | solution.py:349
  122.3 10.3 %all_to_all.22 = f32[8,64,128]{2,1,0:T(8,128)S(1)} all-to-all(f32[8,64,128]{2,1,0:T(8,128)S(1)} %bitcast.16), channel_id=1, replica_groups=mesh['z'=8,'x'=4,'y'=4,'c'=2] {'y','c'}, dimensions={0} | all-to-all | bytes 524288 | tf_op jit(solution)/shard_map/all_to_all | solution.py:513
  132.6 2.1 %place.1 = f32[64,1024]{1,0:T(8,128)} custom-call(s32[5]{0:T(128)S(1)} %copy-done.2, f32[512,128]{1,0:T(8,128)S(1)} %bitcast.17, s32[8,128]{1,0:T(8,128)S(1)} %bitcast.20), custom_call_target="tpu_custom_call" | custom-call | flops 400000000 | bytes 1048576 | tf_op jit(solution)/shard_map/place/pallas_call | solution.py:379
  (48 shorter events, 0.1 us)
Async XLA Ops:
  6.5 82.7 %all-gather.2.cloned.1.call-start = ((), (), s32[]{:S(2)}) async-start(), calls=%async_computation.2 | async-start | bytes 9437184 | tf_op jit(solution)/shard_map/all_gather | solution.py:478
  10.7 17.6 %copy-start.14 = (f32[128,512]{1,0:T(8,128)S(1)}, f32[128,512]{1,0:T(8,128)}, u32[]{:S(2)}) copy-start(f32[128,512]{1,0:T(8,128)} %get-tuple-element.75) | copy-start | bytes 786436
  10.7 20.7 %copy-start = (f32[128,512]{1,0:T(8,128)S(1)}, f32[128,512]{1,0:T(8,128)}, u32[]{:S(2)}) copy-start(f32[128,512]{1,0:T(8,128)} %get-tuple-element.60.refs_5_) | copy-start | bytes 786436
  10.7 20.7 %copy-start.1 = (s32[5]{0:T(128)S(1)}, s32[5]{0:T(128)}, u32[]{:S(2)}) copy-start(s32[5]{0:T(128)} %stack.23.pos.refs_0_) | copy-start | bytes 64
  10.7 20.7 %copy-start.3 = (s32[96]{0:T(128)S(1)}, s32[96]{0:T(128)}, u32[]{:S(2)}) copy-start(s32[96]{0:T(128)} %get-tuple-element.65.refs_1_) | copy-start | bytes 1156
  10.7 13.6 %collective-permute-start.1 = (f32[128,512]{1,0:T(8,128)}, f32[128,512]{1,0:T(8,128)S(1)}, u32[]{:S(2)}, u32[]{:S(2)}) collective-permute-start(f32[128,512]{1,0:T(8,128)} %get-tuple-element.60.refs_5_), channel_id=1, source_target_pairs={{0,224},{32,0},{64,32},{96,64},{128,96},{160,128},{192,160},{224,1... | collective-permute-start | bytes 786440 | tf_op jit(solution)/shard_map/ppermute | solution.py:468
  17.2 8.3 %collective-permute-start = (f32[128,512]{1,0:T(8,128)}, f32[128,512]{1,0:T(8,128)S(1)}, u32[]{:S(2)}, u32[]{:S(2)}) collective-permute-start(f32[128,512]{1,0:T(8,128)} %get-tuple-element.60.refs_5_), channel_id=1, source_target_pairs={{0,32},{32,64},{64,96},{96,128},{128,160},{160,192},{192,224},{224... | collective-permute-start | bytes 786440 | tf_op jit(solution)/shard_map/ppermute | solution.py:468
  17.2 7.1 %collective-permute-start.4 = (s32[96]{0:T(128)}, s32[96]{0:T(128)S(1)}, u32[]{:S(2)}, u32[]{:S(2)}) collective-permute-start(s32[96]{0:T(128)} %get-tuple-element.65.refs_1_), channel_id=1, source_target_pairs={{0,8},{8,16},{16,24},{24,0},{1,9},{9,17},{17,25},{25,1},{2,10},{10... | collective-permute-start | bytes 1160 | tf_op jit(solution)/shard_map/ppermute | solution.py:475
  18.4 5.9 %collective-permute-start.3 = (s32[96]{0:T(128)}, s32[96]{0:T(128)S(1)}, u32[]{:S(2)}, u32[]{:S(2)}) collective-permute-start(s32[96]{0:T(128)} %get-tuple-element.65.refs_1_), channel_id=1, source_target_pairs={{0,16},{8,24},{16,0},{24,8},{1,17},{9,25},{17,1},{25,9},{2,18},{10... | collective-permute-start | bytes 1160 | tf_op jit(solution)/shard_map/ppermute | solution.py:475
  20.9 3.5 %collective-permute-start.2 = (s32[96]{0:T(128)}, s32[96]{0:T(128)S(1)}, u32[]{:S(2)}, u32[]{:S(2)}) collective-permute-start(s32[96]{0:T(128)} %get-tuple-element.65.refs_1_), channel_id=1, source_target_pairs={{0,24},{8,0},{16,8},{24,16},{1,25},{9,1},{17,9},{25,17},{2,26},{10... | collective-permute-start | bytes 1160 | tf_op jit(solution)/shard_map/ppermute | solution.py:475
  24.3 50.6 %copy-start.4 = (s32[48]{0:T(128)S(1)}, s32[48]{0:T(128)}, u32[]{:S(2)}) copy-start(s32[48]{0:T(128)} %get-tuple-element.59.row) | copy-start | bytes 580
  25.5 9.2 %collective-permute-start.5 = (f32[128,512]{1,0:T(8,128)S(1)}, f32[128,512]{1,0:T(8,128)S(1)}, u32[]{:S(2)}, u32[]{:S(2)}) collective-permute-start(f32[128,512]{1,0:T(8,128)S(1)} %collective-permute-done.refs_7_), channel_id=1, source_target_pairs={{0,32},{32,64},{64,96},{96,128},{128,160},{160,192},{192,224},{224... | collective-permute-start | bytes 786440 | tf_op jit(solution)/shard_map/ppermute | solution.py:468
  25.6 11.1 %collective-permute-start.6 = (f32[128,512]{1,0:T(8,128)S(1)}, f32[128,512]{1,0:T(8,128)S(1)}, u32[]{:S(2)}, u32[]{:S(2)}) collective-permute-start(f32[128,512]{1,0:T(8,128)S(1)} %collective-permute-done.1.refs_6_), channel_id=1, source_target_pairs={{0,224},{32,0},{64,32},{96,64},{128,96},{160,128},{192,160},{224,1... | collective-permute-start | bytes 786440 | tf_op jit(solution)/shard_map/ppermute | solution.py:468
  28.3 8.4 %collective-permute-start.9 = (f32[128,512]{1,0:T(8,128)S(1)}, f32[128,512]{1,0:T(8,128)S(1)}, u32[]{:S(2)}, u32[]{:S(2)}) collective-permute-start(f32[128,512]{1,0:T(8,128)S(1)} %copy-done.14), channel_id=1, source_target_pairs={{0,8},{1,9},{8,16},{9,17},{16,24},{17,25},{24,32},{25,33},{32,40},... | collective-permute-start | bytes 786440 | tf_op jit(solution)/shard_map/ppermute | solution.py:487
  32.1 9.5 %collective-permute-start.10 = (f32[144,512]{1,0:T(8,128)S(1)}, f32[144,512]{1,0:T(8,128)S(1)}, u32[]{:S(2)}, u32[]{:S(2)}) collective-permute-start(f32[144,512]{1,0:T(8,128)S(1)} %get-tuple-element.70), channel_id=1, source_target_pairs={{0,8},{8,16},{16,24},{24,0},{1,9},{9,17},{17,25},{25,1},{2,10},{10... | collective-permute-start | bytes 884744 | tf_op jit(solution)/shard_map/ppermute | solution.py:484
  33.4 17.0 %collective-permute-start.11 = (f32[144,512]{1,0:T(8,128)S(1)}, f32[144,512]{1,0:T(8,128)S(1)}, u32[]{:S(2)}, u32[]{:S(2)}) collective-permute-start(f32[144,512]{1,0:T(8,128)S(1)} %get-tuple-element.71), channel_id=1, source_target_pairs={{0,16},{8,24},{16,0},{24,8},{1,17},{9,25},{17,1},{25,9},{2,18},{10... | collective-permute-start | bytes 884744 | tf_op jit(solution)/shard_map/ppermute | solution.py:484
  34.7 15.6 %collective-permute-start.12 = (f32[144,512]{1,0:T(8,128)S(1)}, f32[144,512]{1,0:T(8,128)S(1)}, u32[]{:S(2)}, u32[]{:S(2)}) collective-permute-start(f32[144,512]{1,0:T(8,128)S(1)} %get-tuple-element.72), channel_id=1, source_target_pairs={{0,24},{8,0},{16,8},{24,16},{1,25},{9,1},{17,9},{25,17},{2,26},{10... | collective-permute-start | bytes 884744 | tf_op jit(solution)/shard_map/ppermute | solution.py:484
  36.7 13.7 %collective-permute-start.7 = (f32[128,512]{1,0:T(8,128)S(1)}, f32[128,512]{1,0:T(8,128)S(1)}, u32[]{:S(2)}, u32[]{:S(2)}) collective-permute-start(f32[128,512]{1,0:T(8,128)S(1)} %collective-permute-done.5.refs_6_), channel_id=1, source_target_pairs={{0,32},{32,64},{64,96},{96,128},{128,160},{160,192},{192,224},{224... | collective-permute-start | bytes 786440 | tf_op jit(solution)/shard_map/ppermute | solution.py:468
  36.7 40.3 %copy-start.13 = (f32[128,512]{1,0:T(8,128)}, f32[128,512]{1,0:T(8,128)S(1)}, u32[]{:S(2)}) copy-start(f32[128,512]{1,0:T(8,128)S(1)} %collective-permute-done.9.e_in) | copy-start | bytes 786436
  36.7 13.6 %collective-permute-start.8 = (f32[128,512]{1,0:T(8,128)S(1)}, f32[128,512]{1,0:T(8,128)S(1)}, u32[]{:S(2)}, u32[]{:S(2)}) collective-permute-start(f32[128,512]{1,0:T(8,128)S(1)} %collective-permute-done.6.refs_5_), channel_id=1, source_target_pairs={{0,224},{32,0},{64,32},{96,64},{128,96},{160,128},{192,160},{224,1... | collective-permute-start | bytes 786440 | tf_op jit(solution)/shard_map/ppermute | solution.py:468
  41.6 18.1 %collective-permute-start.16 = (f32[96,512]{1,0:T(8,128)S(1)}, f32[96,512]{1,0:T(8,128)S(1)}, u32[]{:S(2)}, u32[]{:S(2)}) collective-permute-start(f32[96,512]{1,0:T(8,128)S(1)} %get-tuple-element.77), channel_id=1, source_target_pairs={{0,8},{8,16},{16,24},{24,0},{1,9},{9,17},{17,25},{25,1},{2,10},{10... | collective-permute-start | bytes 589832 | tf_op jit(solution)/shard_map/ppermute | solution.py:484
  50.4 4.3 %collective-permute-start.14 = (f32[64,512]{1,0:T(8,128)S(1)}, f32[64,512]{1,0:T(8,128)S(1)}, u32[]{:S(2)}, u32[]{:S(2)}) collective-permute-start(f32[64,512]{1,0:T(8,128)S(1)} %slice.7), channel_id=1, source_target_pairs={{0,224},{32,0},{64,32},{96,64},{128,96},{160,128},{192,160},{224,1... | collective-permute-start | bytes 393224 | tf_op jit(solution)/shard_map/ppermute | solution.py:468
  50.5 5.7 %collective-permute-start.13 = (f32[64,512]{1,0:T(8,128)S(1)}, f32[64,512]{1,0:T(8,128)S(1)}, u32[]{:S(2)}, u32[]{:S(2)}) collective-permute-start(f32[64,512]{1,0:T(8,128)S(1)} %slice.6), channel_id=1, source_target_pairs={{0,32},{32,64},{64,96},{96,128},{128,160},{160,192},{192,224},{224... | collective-permute-start | bytes 393224 | tf_op jit(solution)/shard_map/ppermute | solution.py:468
  51.9 14.7 %collective-permute-start.17 = (f32[96,512]{1,0:T(8,128)S(1)}, f32[96,512]{1,0:T(8,128)S(1)}, u32[]{:S(2)}, u32[]{:S(2)}) collective-permute-start(f32[96,512]{1,0:T(8,128)S(1)} %get-tuple-element.78), channel_id=1, source_target_pairs={{0,16},{8,24},{16,0},{24,8},{1,17},{9,25},{17,1},{25,9},{2,18},{10... | collective-permute-start | bytes 589832 | tf_op jit(solution)/shard_map/ppermute | solution.py:484
  56.9 18.1 %collective-permute-start.19 = (f32[144,512]{1,0:T(8,128)S(1)}, f32[144,512]{1,0:T(8,128)S(1)}, u32[]{:S(2)}, u32[]{:S(2)}) collective-permute-start(f32[144,512]{1,0:T(8,128)S(1)} %get-tuple-element.84), channel_id=1, source_target_pairs={{0,8},{8,16},{16,24},{24,0},{1,9},{9,17},{17,25},{25,1},{2,10},{10... | collective-permute-start | bytes 884744 | tf_op jit(solution)/shard_map/ppermute | solution.py:484
  56.9 18.0 %collective-permute-start.20 = (f32[144,512]{1,0:T(8,128)S(1)}, f32[144,512]{1,0:T(8,128)S(1)}, u32[]{:S(2)}, u32[]{:S(2)}) collective-permute-start(f32[144,512]{1,0:T(8,128)S(1)} %get-tuple-element.85), channel_id=1, source_target_pairs={{0,16},{8,24},{16,0},{24,8},{1,17},{9,25},{17,1},{25,9},{2,18},{10... | collective-permute-start | bytes 884744 | tf_op jit(solution)/shard_map/ppermute | solution.py:484
  59.6 15.3 %collective-permute-start.21 = (f32[144,512]{1,0:T(8,128)S(1)}, f32[144,512]{1,0:T(8,128)S(1)}, u32[]{:S(2)}, u32[]{:S(2)}) collective-permute-start(f32[144,512]{1,0:T(8,128)S(1)} %get-tuple-element.86), channel_id=1, source_target_pairs={{0,24},{8,0},{16,8},{24,16},{1,25},{9,1},{17,9},{25,17},{2,26},{10... | collective-permute-start | bytes 884744 | tf_op jit(solution)/shard_map/ppermute | solution.py:484
  59.7 15.2 %collective-permute-start.15 = (f32[128,512]{1,0:T(8,128)S(1)}, f32[128,512]{1,0:T(8,128)S(1)}, u32[]{:S(2)}, u32[]{:S(2)}) collective-permute-start(f32[128,512]{1,0:T(8,128)S(1)} %collective-permute-done.9.e_in), channel_id=1, source_target_pairs={{0,1},{1,0},{2,3},{3,2},{4,5},{5,4},{6,7},{7,6},{8,9},{9,8},{10,11... | collective-permute-start | bytes 786440 | tf_op jit(solution)/shard_map/ppermute | solution.py:471
  66.6 8.3 %collective-permute-start.18 = (f32[96,512]{1,0:T(8,128)S(1)}, f32[96,512]{1,0:T(8,128)S(1)}, u32[]{:S(2)}, u32[]{:S(2)}) collective-permute-start(f32[96,512]{1,0:T(8,128)S(1)} %get-tuple-element.79), channel_id=1, source_target_pairs={{0,24},{8,0},{16,8},{24,16},{1,25},{9,1},{17,9},{25,17},{2,26},{10... | collective-permute-start | bytes 589832 | tf_op jit(solution)/shard_map/ppermute | solution.py:484
  74.9 2.1 %copy-start.15 = (f32[128,512]{1,0:T(8,128)}, f32[128,512]{1,0:T(8,128)S(1)}, u32[]{:S(2)}) copy-start(f32[128,512]{1,0:T(8,128)S(1)} %collective-permute-done.15.e_other) | copy-start | bytes 786436
  77.0 11.6 %copy-start.12 = (s32[8,3]{0,1:T(4,128)S(1)}, s32[8,3]{0,1:T(4,128)}, u32[]{:S(2)}) copy-start(s32[8,3]{0,1:T(4,128)} %param.16) | copy-start | bytes 292
  77.0 32.4 %all-to-all-start = ((f32[8,96,512]{2,1,0:T(8,128)}), f32[8,96,512]{2,1,0:T(8,128)}, u32[]{:S(2)}, u32[]{:S(2)}) async-start(f32[8,96,512]{2,1,0:T(8,128)} %bitcast.10), calls=%async_computation | async-start | bytes 3145728 | tf_op jit(solution)/shard_map/all_to_all | solution.py:505
  104.0 5.4 %copy-start.2 = (s32[5]{0:T(128)S(1)}, s32[5]{0:T(128)}, u32[]{:S(2)}) copy-start(s32[5]{0:T(128)} %stack.23.pos.refs_0_) | copy-start | bytes 64
  104.1 5.4 %copy-start.5 = (s32[8,6]{1,0:T(8,128)S(1)}, s32[8,6]{1,0:T(8,128)}, u32[]{:S(2)}) copy-start(s32[8,6]{1,0:T(8,128)} %exp_ref.3) | copy-start | bytes 580
  104.1 5.3 %copy-start.7 = (s32[256]{0:T(256)S(1)}, s32[256]{0:T(256)}, u32[]{:S(2)}) copy-start(s32[256]{0:T(256)} %count_ref.3) | copy-start | bytes 3076
  104.1 5.3 %copy-start.8 = (bf16[2,4,128,512]{3,2,1,0:T(8,128)(2,1)S(1)}, bf16[2,4,128,512]{3,2,1,0:T(8,128)(2,1)}, u32[]{:S(2)}) copy-start(bf16[2,4,128,512]{3,2,1,0:T(8,128)(2,1)} %get-tuple-element.107.v_hbm) | copy-start | bytes 3145732
  104.1 5.3 %copy-start.9 = (bf16[2,512,512]{2,1,0:T(8,128)(2,1)S(1)}, bf16[2,512,512]{2,1,0:T(8,128)(2,1)}, u32[]{:S(2)}) copy-start(bf16[2,512,512]{2,1,0:T(8,128)(2,1)} %get-tuple-element.109.o_hbm) | copy-start | bytes 3145732
  104.1 5.3 %copy-start.10 = (f32[4,256,128]{2,1,0:T(8,128)S(1)}, f32[4,256,128]{2,1,0:T(8,128)}, u32[]{:S(2)}) copy-start(f32[4,256,128]{2,1,0:T(8,128)} %get-tuple-element.106.s_hbm) | copy-start | bytes 1572868
  104.1 5.3 %copy-start.11 = (f32[128,512]{1,0:T(8,128)S(1)}, f32[128,512]{1,0:T(8,128)}, u32[]{:S(2)}) copy-start(f32[128,512]{1,0:T(8,128)} %get-tuple-element.108.x_hbm) | copy-start | bytes 786436
  109.5 23.2 %copy-start.6 = (s32[1024]{0:T(1024)S(1)}, s32[1024]{0:T(1024)}, u32[]{:S(2)}) copy-start(s32[1024]{0:T(1024)} %param.14) | copy-start | bytes 12292
Sparse Core Ops, SparseCore 0:
  25.6 51.3 all-gather.1

commit v6 on v5

--- a/solution.py
+++ b/solution.py
@@ -498,8 +498,9 @@
     up, down, e_in, *_ = tie((up, down, e_in, *one, *two))
     held[4] = both_z(up[:half], down[half:])
     three = pick(GROUPS[2])
-    (e_other,) = swap(tie((e_in, *three))[0])
-    e_other, *arrived = tie((e_other, *one, *exchange(two), *exchange(three)))
+    two, three = exchange(two), exchange(three)
+    (e_other,) = swap(tie((e_in, *two))[0])
+    e_other, *arrived = tie((e_other, *one, *two, *three))
 
     sending = send_call(row, arrived)
     xe = lax.all_to_all(sending, ("y", "c"), 0, 0, tiled=True)

time: 142 us -> 144 us (1.014)
  starting transfers between devices: 51.6 us -> 59.5 us
  waiting for transfers between devices: 20.5 us -> 14.7 us
    ppermute x9, waiting for transfers between devices: 15 us -> 7.21 us  [exchange(): lax.ppermute(blocks[k], 'x', ring(NX, k))]
    all_to_all x1, starting transfers between devices: 11.6 us -> 16.7 us  [shards(): xe = lax.all_to_all(sending, ('y', 'c'), 0, 0, tiled=True)]
    ppermute x9, starting transfers between devices: 10.2 us -> 12.2 us  [exchange(): lax.ppermute(blocks[k], 'x', ring(NX, k))]
  transfers between devices with their start and end apart: 24 -> 24, of which waited for: 6 -> 6; matrix products, arithmetic and copies ran while one was open for 0% -> 0% of each run, Pallas kernels for 17% -> 16%
where the time goes in v6:
time: 144 us
  starting transfers between devices  59.5 us (41%)
  Pallas kernels  44 us (31%)
  waiting for transfers between devices  14.7 us (10%)
  between operations  13.7 us (10%)
  blocking collectives  10.3 us (7%)
    all_to_all x1, starting transfers between devices, shards(): xe = lax.all_to_all(sending, ('y', 'c'), 0, 0, tiled=True)  16.7 us
    pallas_call x1, Pallas kernels, near_call(): pl.pallas_call(near_kernel, out_shape=shapes, in_specs=[sspec()] * len(sc...  14.8 us
    ppermute x4, starting transfers between devices, both_z(): lax.ppermute(b, 'z', ring(NZ, -1))  13.5 us
    pallas_call x1, Pallas kernels, far_call(): pl.pallas_call(far_kernel, out_shape=sds(D, CL), in_specs=[sspec()] * len...  12.8 us
    ppermute x9, starting transfers between devices, exchange(): lax.ppermute(blocks[k], 'x', ring(NX, k))  12.2 us
    all_to_all x1, blocking collectives, shards(): received = lax.all_to_all(result, ('y', 'c'), 0, 0, tiled=True)  10.3 us
    ppermute x1, starting transfers between devices, swap(): return [lax.ppermute(t, 'c', SWAP) for t in arrays]  7.66 us
    ppermute x9, waiting for transfers between devices, exchange(): lax.ppermute(blocks[k], 'x', ring(NX, k))  7.21 us
  transfers between devices with their start and end apart: 24, of which 6 were waited for; matrix products, arithmetic and copies ran while one was open for 0% of the time, Pallas kernels for 16%

profile of v6, /device:TPU:1, one launch (start us, length us, event | category | flops | bytes accessed | tf_op | source)
XLA Modules:
  0.0 143.6 jit_solution(18227608281022993553)
XLA Ops:
  6.5 0.6 stack.23.pos.refs_0_
  7.1 3.6 %first.1 = (f32[128,512]{1,0:T(8,128)}, f32[128,512]{1,0:T(8,128)}, s32[96]{0:T(128)}, s32[48]{0:T(128)}) custom-call(s32[5]{0:T(128)} %stack.23.pos.refs_0_, s32[8,6]{1,0:T(8,128)} %exp_ref.3, s32[8,128]{1,0:T(8,128)} %bitcast.18, f32[1024,512]{1,0:T(8,128)} %nodes_ref.1), custom_call_target="tpu_custom_call" | custom-call | flops 1000000000 | bytes 3145728 | tf_op jit(solution)/shard_map/first/pallas_call | solution.py:134
  10.7 0.0 copy-start
  10.7 6.5 %collective-permute-start.1 = (f32[128,512]{1,0:T(8,128)}, f32[128,512]{1,0:T(8,128)S(1)}, u32[]{:S(2)}, u32[]{:S(2)}) collective-permute-start(f32[128,512]{1,0:T(8,128)} %get-tuple-element.60.refs_5_), channel_id=1, source_target_pairs={{0,224},{32,0},{64,32},{96,64},{128,96},{160,128},{192,160},{224,1... | collective-permute-start | bytes 786440 | tf_op jit(solution)/shard_map/ppermute | solution.py:468
  17.2 0.0 collective-permute-start
  17.2 1.2 collective-permute-start.4
  18.4 2.4 %collective-permute-start.3 = (s32[96]{0:T(128)}, s32[96]{0:T(128)S(1)}, u32[]{:S(2)}, u32[]{:S(2)}) collective-permute-start(s32[96]{0:T(128)} %get-tuple-element.65.refs_1_), channel_id=1, source_target_pairs={{0,16},{8,24},{16,0},{24,8},{1,17},{9,25},{17,1},{25,9},{2,18},{10... | collective-permute-start | bytes 1160 | tf_op jit(solution)/shard_map/ppermute | solution.py:475
  20.9 1.2 collective-permute-start.2
  22.0 2.3 %pack.1 = f32[512,512]{1,0:T(8,128)} custom-call(f32[64,512]{1,0:T(8,128)} %bitcast.23, f32[64,512]{1,0:T(8,128)} %bitcast.24, f32[64,512]{1,0:T(8,128)} %bitcast.25, f32[64,512]{1,0:T(8,128)} %bitcast.26, f32[512,128]{1,0:T(8,128)} %up.1, f32[128,512]{1,0:T(8,128)} %down.1), custom_call_target="tpu_custom_call" | custom-call | flops 1000 | bytes 2097152 | tf_op jit(solution)/shard_map/pack/pallas_call | solution.py:160
  24.4 1.1 collective-permute-done.refs_7_
  25.5 0.0 all-gather.2.cloned.1.call-update
  25.5 0.1 collective-permute-start.5
  25.6 2.7 %collective-permute-start.6 = (f32[128,512]{1,0:T(8,128)S(1)}, f32[128,512]{1,0:T(8,128)S(1)}, u32[]{:S(2)}, u32[]{:S(2)}) collective-permute-start(f32[128,512]{1,0:T(8,128)S(1)} %collective-permute-done.1.refs_6_), channel_id=1, source_target_pairs={{0,224},{32,0},{64,32},{96,64},{128,96},{160,128},{192,160},{224,1... | collective-permute-start | bytes 786440 | tf_op jit(solution)/shard_map/ppermute | solution.py:468
  28.3 3.1 %collective-permute-start.9 = (f32[128,512]{1,0:T(8,128)S(1)}, f32[128,512]{1,0:T(8,128)S(1)}, u32[]{:S(2)}, u32[]{:S(2)}) collective-permute-start(f32[128,512]{1,0:T(8,128)S(1)} %copy-done.14), channel_id=1, source_target_pairs={{0,8},{1,9},{8,16},{9,17},{16,24},{17,25},{24,32},{25,33},{32,40},... | collective-permute-start | bytes 786440 | tf_op jit(solution)/shard_map/ppermute | solution.py:487
  31.4 0.7 pick.3
  32.1 1.3 collective-permute-start.10
  33.4 1.3 collective-permute-start.11
  34.7 2.0 %collective-permute-start.12 = (f32[144,512]{1,0:T(8,128)S(1)}, f32[144,512]{1,0:T(8,128)S(1)}, u32[]{:S(2)}, u32[]{:S(2)}) collective-permute-start(f32[144,512]{1,0:T(8,128)S(1)} %get-tuple-element.72), channel_id=1, source_target_pairs={{0,24},{8,0},{16,8},{24,16},{1,25},{9,1},{17,9},{25,17},{2,26},{10... | collective-permute-start | bytes 884744 | tf_op jit(solution)/shard_map/ppermute | solution.py:484
  36.7 0.0 copy-start.13
  36.7 4.3 %collective-permute-start.8 = (f32[128,512]{1,0:T(8,128)S(1)}, f32[128,512]{1,0:T(8,128)S(1)}, u32[]{:S(2)}, u32[]{:S(2)}) collective-permute-start(f32[128,512]{1,0:T(8,128)S(1)} %collective-permute-done.6.refs_5_), channel_id=1, source_target_pairs={{0,224},{32,0},{64,32},{96,64},{128,96},{160,128},{192,160},{224,1... | collective-permute-start | bytes 786440 | tf_op jit(solution)/shard_map/ppermute | solution.py:468
  41.0 0.6 pick.4
  41.6 1.5 %collective-permute-start.13 = (f32[96,512]{1,0:T(8,128)S(1)}, f32[96,512]{1,0:T(8,128)S(1)}, u32[]{:S(2)}, u32[]{:S(2)}) collective-permute-start(f32[96,512]{1,0:T(8,128)S(1)} %get-tuple-element.77), channel_id=1, source_target_pairs={{0,8},{8,16},{16,24},{24,0},{1,9},{9,17},{17,25},{25,1},{2,10},{10... | collective-permute-start | bytes 589832 | tf_op jit(solution)/shard_map/ppermute | solution.py:484
  43.2 7.2 %collective-permute-done.11.refs_2_ = f32[144,512]{1,0:T(8,128)S(1)} collective-permute-done((f32[144,512]{1,0:T(8,128)S(1)}, f32[144,512]{1,0:T(8,128)S(1)}, u32[]{:S(2)}, u32[]{:S(2)}) %collective-permute-start.11) | collective-permute-done | bytes 294944 | tf_op jit(solution)/shard_map/ppermute | solution.py:484
  50.3 0.6 collective-permute-start.14
  51.0 1.2 collective-permute-start.15
  52.2 0.1 collective-permute-start.18
  52.3 1.5 %collective-permute-start.17 = (f32[64,512]{1,0:T(8,128)S(1)}, f32[64,512]{1,0:T(8,128)S(1)}, u32[]{:S(2)}, u32[]{:S(2)}) collective-permute-start(f32[64,512]{1,0:T(8,128)S(1)} %slice.6), channel_id=1, source_target_pairs={{0,32},{32,64},{64,96},{96,128},{128,160},{160,192},{192,224},{224... | collective-permute-start | bytes 393224 | tf_op jit(solution)/shard_map/ppermute | solution.py:468
  53.8 2.8 %collective-permute-done.18.refs_8_ = f32[64,512]{1,0:T(8,128)S(1)} collective-permute-done((f32[64,512]{1,0:T(8,128)S(1)}, f32[64,512]{1,0:T(8,128)S(1)}, u32[]{:S(2)}, u32[]{:S(2)}) %collective-permute-start.18) | collective-permute-done | bytes 131104 | tf_op jit(solution)/shard_map/ppermute | solution.py:468
  56.5 1.4 collective-permute-done.17.refs_7_
  57.9 0.7 pick.5
  58.6 0.5 collective-permute-start.19
  59.1 2.1 %collective-permute-start.20 = (f32[144,512]{1,0:T(8,128)S(1)}, f32[144,512]{1,0:T(8,128)S(1)}, u32[]{:S(2)}, u32[]{:S(2)}) collective-permute-start(f32[144,512]{1,0:T(8,128)S(1)} %get-tuple-element.86), channel_id=1, source_target_pairs={{0,16},{8,24},{16,0},{24,8},{1,17},{9,25},{17,1},{25,9},{2,18},{10... | collective-permute-start | bytes 884744 | tf_op jit(solution)/shard_map/ppermute | solution.py:484
  61.2 1.7 %collective-permute-start.21 = (f32[144,512]{1,0:T(8,128)S(1)}, f32[144,512]{1,0:T(8,128)S(1)}, u32[]{:S(2)}, u32[]{:S(2)}) collective-permute-start(f32[144,512]{1,0:T(8,128)S(1)} %get-tuple-element.87), channel_id=1, source_target_pairs={{0,24},{8,0},{16,8},{24,16},{1,25},{9,1},{17,9},{25,17},{2,26},{10... | collective-permute-start | bytes 884744 | tf_op jit(solution)/shard_map/ppermute | solution.py:484
  62.9 7.7 %collective-permute-start.16 = (f32[128,512]{1,0:T(8,128)S(1)}, f32[128,512]{1,0:T(8,128)S(1)}, u32[]{:S(2)}, u32[]{:S(2)}) collective-permute-start(f32[128,512]{1,0:T(8,128)S(1)} %collective-permute-done.9.e_in), channel_id=1, source_target_pairs={{0,1},{1,0},{2,3},{3,2},{4,5},{5,4},{6,7},{7,6},{8,9},{9,8},{10,11... | collective-permute-start | bytes 786440 | tf_op jit(solution)/shard_map/ppermute | solution.py:471
  70.5 1.4 collective-permute-done.16.e_other
  71.9 0.0 collective-permute-done.20.refs_10_
  71.9 2.0 %send.1 = f32[768,512]{1,0:T(8,128)} custom-call(s32[48]{0:T(128)S(1)} %copy-done.4, f32[144,512]{1,0:T(8,128)S(1)} %get-tuple-element.88.refs_0_, f32[144,512]{1,0:T(8,128)S(1)} %collective-permute-done.10.refs_1_, f32[144,512]{1,0:T(8,128)S(1)} %collective-permute-done.11.refs_2_, f32[144,512]{1,0:T(8,128)S(1)} %collective-permute-done.12.refs_3_, ...), custom_call_target="tpu_custom_call" | custom-call | bytes 6291456 | tf_op jit(solution)/shard_map/send/pallas_call | solution.py:436
  74.0 16.7 %all-to-all-start = ((f32[8,96,512]{2,1,0:T(8,128)}), f32[8,96,512]{2,1,0:T(8,128)}, u32[]{:S(2)}, u32[]{:S(2)}) async-start(f32[8,96,512]{2,1,0:T(8,128)} %bitcast.10), calls=%async_computation | async-start | bytes 3145728 | tf_op jit(solution)/shard_map/all_to_all | solution.py:506
  90.6 0.7 copy.14.local_ref
  91.3 14.8 %near.1 = (f32[128,512]{1,0:T(8,128)}, bf16[2,4,256,512]{3,2,1,0:T(8,128)(2,1)}, bf16[2,4,128,512]{3,2,1,0:T(8,128)(2,1)}, bf16[2,512,512]{2,1,0:T(8,128)(2,1)}, f32[4,256,128]{2,1,0:T(8,128)}) custom-call(s32[5]{0:T(128)} %stack.23.pos.refs_0_, s32[8,3]{1,0:T(8,128)} %copy.14.local_ref, s32[8]{0:T(128)} %virt_ref.1, s32[256]{0:T(256)} %count_ref.3, ...), custom_call_target="tpu_custom_call" | custom-call | flops 6000000000 | bytes 16777216 | tf_op jit(solution)/shard_map/near/pallas_call | solution.py:239
  106.1 0.0 copy-start.5
  106.1 0.0 copy-start.7
  106.2 4.5 %prep.1 = (bf16[2,512,1024]{2,1,0:T(8,128)(2,1)}, bf16[2,1024,512]{2,1,0:T(8,128)(2,1)}) custom-call(f32[8,512,512]{2,1,0:T(8,128)} %bitcast.22), custom_call_target="tpu_custom_call" | custom-call | flops 10000000 | bytes 8388608 | tf_op jit(solution)/shard_map/prep/pallas_call | solution.py:268
  110.6 0.8 all-to-all-done
  111.5 0.0 copy-start.6
  111.5 12.8 %far.1 = f32[512,128]{1,0:T(8,128)S(1)} custom-call(s32[5]{0:T(128)S(1)} %copy-done.2, s32[8,6]{1,0:T(8,128)S(1)} %copy-done.5, s32[256]{0:T(256)S(1)} %copy-done.7, f32[768,512]{1,0:T(8,128)} %bitcast.11.xe_ref, bf16[2,4,256,512]{3,2,1,0:T(8,128)(2,1)} %get-tuple-element.104.q_hbm, f32[4,256,128]{2,1,0:T(8,128)S(1)} %copy-done.10, ...), custom_call_target="tpu_custom_call" | custom-call | flops 6000000000 | bytes 16777216 | tf_op jit(solution)/shard_map/far/pallas_call | solution.py:349
  124.3 10.3 %all_to_all.22 = f32[8,64,128]{2,1,0:T(8,128)S(1)} all-to-all(f32[8,64,128]{2,1,0:T(8,128)S(1)} %bitcast.16), channel_id=1, replica_groups=mesh['z'=8,'x'=4,'y'=4,'c'=2] {'y','c'}, dimensions={0} | all-to-all | bytes 524288 | tf_op jit(solution)/shard_map/all_to_all | solution.py:514
  134.7 2.1 %place.1 = f32[64,1024]{1,0:T(8,128)} custom-call(s32[5]{0:T(128)S(1)} %copy-done.2, f32[512,128]{1,0:T(8,128)S(1)} %bitcast.17, s32[8,128]{1,0:T(8,128)S(1)} %bitcast.20), custom_call_target="tpu_custom_call" | custom-call | flops 400000000 | bytes 1048576 | tf_op jit(solution)/shard_map/place/pallas_call | solution.py:379
  (48 shorter events, 0.1 us)
Async XLA Ops:
  6.5 84.8 %all-gather.2.cloned.1.call-start = ((), (), s32[]{:S(2)}) async-start(), calls=%async_computation.2 | async-start | bytes 9437184 | tf_op jit(solution)/shard_map/all_gather | solution.py:478
  10.7 17.6 %copy-start.14 = (f32[128,512]{1,0:T(8,128)S(1)}, f32[128,512]{1,0:T(8,128)}, u32[]{:S(2)}) copy-start(f32[128,512]{1,0:T(8,128)} %get-tuple-element.75) | copy-start | bytes 786436
  10.7 20.7 %copy-start = (f32[128,512]{1,0:T(8,128)S(1)}, f32[128,512]{1,0:T(8,128)}, u32[]{:S(2)}) copy-start(f32[128,512]{1,0:T(8,128)} %get-tuple-element.60.refs_5_) | copy-start | bytes 786436
  10.7 20.7 %copy-start.1 = (s32[5]{0:T(128)S(1)}, s32[5]{0:T(128)}, u32[]{:S(2)}) copy-start(s32[5]{0:T(128)} %stack.23.pos.refs_0_) | copy-start | bytes 64
  10.7 20.7 %copy-start.3 = (s32[96]{0:T(128)S(1)}, s32[96]{0:T(128)}, u32[]{:S(2)}) copy-start(s32[96]{0:T(128)} %get-tuple-element.65.refs_1_) | copy-start | bytes 1156
  10.7 13.6 %collective-permute-start.1 = (f32[128,512]{1,0:T(8,128)}, f32[128,512]{1,0:T(8,128)S(1)}, u32[]{:S(2)}, u32[]{:S(2)}) collective-permute-start(f32[128,512]{1,0:T(8,128)} %get-tuple-element.60.refs_5_), channel_id=1, source_target_pairs={{0,224},{32,0},{64,32},{96,64},{128,96},{160,128},{192,160},{224,1... | collective-permute-start | bytes 786440 | tf_op jit(solution)/shard_map/ppermute | solution.py:468
  17.2 8.3 %collective-permute-start = (f32[128,512]{1,0:T(8,128)}, f32[128,512]{1,0:T(8,128)S(1)}, u32[]{:S(2)}, u32[]{:S(2)}) collective-permute-start(f32[128,512]{1,0:T(8,128)} %get-tuple-element.60.refs_5_), channel_id=1, source_target_pairs={{0,32},{32,64},{64,96},{96,128},{128,160},{160,192},{192,224},{224... | collective-permute-start | bytes 786440 | tf_op jit(solution)/shard_map/ppermute | solution.py:468
  17.2 7.1 %collective-permute-start.4 = (s32[96]{0:T(128)}, s32[96]{0:T(128)S(1)}, u32[]{:S(2)}, u32[]{:S(2)}) collective-permute-start(s32[96]{0:T(128)} %get-tuple-element.65.refs_1_), channel_id=1, source_target_pairs={{0,8},{8,16},{16,24},{24,0},{1,9},{9,17},{17,25},{25,1},{2,10},{10... | collective-permute-start | bytes 1160 | tf_op jit(solution)/shard_map/ppermute | solution.py:475
  18.4 5.9 %collective-permute-start.3 = (s32[96]{0:T(128)}, s32[96]{0:T(128)S(1)}, u32[]{:S(2)}, u32[]{:S(2)}) collective-permute-start(s32[96]{0:T(128)} %get-tuple-element.65.refs_1_), channel_id=1, source_target_pairs={{0,16},{8,24},{16,0},{24,8},{1,17},{9,25},{17,1},{25,9},{2,18},{10... | collective-permute-start | bytes 1160 | tf_op jit(solution)/shard_map/ppermute | solution.py:475
  20.9 3.5 %collective-permute-start.2 = (s32[96]{0:T(128)}, s32[96]{0:T(128)S(1)}, u32[]{:S(2)}, u32[]{:S(2)}) collective-permute-start(s32[96]{0:T(128)} %get-tuple-element.65.refs_1_), channel_id=1, source_target_pairs={{0,24},{8,0},{16,8},{24,16},{1,25},{9,1},{17,9},{25,17},{2,26},{10... | collective-permute-start | bytes 1160 | tf_op jit(solution)/shard_map/ppermute | solution.py:475
  24.3 47.6 %copy-start.4 = (s32[48]{0:T(128)S(1)}, s32[48]{0:T(128)}, u32[]{:S(2)}) copy-start(s32[48]{0:T(128)} %get-tuple-element.59.row) | copy-start | bytes 580
  25.5 9.2 %collective-permute-start.5 = (f32[128,512]{1,0:T(8,128)S(1)}, f32[128,512]{1,0:T(8,128)S(1)}, u32[]{:S(2)}, u32[]{:S(2)}) collective-permute-start(f32[128,512]{1,0:T(8,128)S(1)} %collective-permute-done.refs_7_), channel_id=1, source_target_pairs={{0,32},{32,64},{64,96},{96,128},{128,160},{160,192},{192,224},{224... | collective-permute-start | bytes 786440 | tf_op jit(solution)/shard_map/ppermute | solution.py:468
  25.6 11.1 %collective-permute-start.6 = (f32[128,512]{1,0:T(8,128)S(1)}, f32[128,512]{1,0:T(8,128)S(1)}, u32[]{:S(2)}, u32[]{:S(2)}) collective-permute-start(f32[128,512]{1,0:T(8,128)S(1)} %collective-permute-done.1.refs_6_), channel_id=1, source_target_pairs={{0,224},{32,0},{64,32},{96,64},{128,96},{160,128},{192,160},{224,1... | collective-permute-start | bytes 786440 | tf_op jit(solution)/shard_map/ppermute | solution.py:468
  28.3 8.4 %collective-permute-start.9 = (f32[128,512]{1,0:T(8,128)S(1)}, f32[128,512]{1,0:T(8,128)S(1)}, u32[]{:S(2)}, u32[]{:S(2)}) collective-permute-start(f32[128,512]{1,0:T(8,128)S(1)} %copy-done.14), channel_id=1, source_target_pairs={{0,8},{1,9},{8,16},{9,17},{16,24},{17,25},{24,32},{25,33},{32,40},... | collective-permute-start | bytes 786440 | tf_op jit(solution)/shard_map/ppermute | solution.py:487
  32.1 9.5 %collective-permute-start.10 = (f32[144,512]{1,0:T(8,128)S(1)}, f32[144,512]{1,0:T(8,128)S(1)}, u32[]{:S(2)}, u32[]{:S(2)}) collective-permute-start(f32[144,512]{1,0:T(8,128)S(1)} %get-tuple-element.70), channel_id=1, source_target_pairs={{0,8},{8,16},{16,24},{24,0},{1,9},{9,17},{17,25},{25,1},{2,10},{10... | collective-permute-start | bytes 884744 | tf_op jit(solution)/shard_map/ppermute | solution.py:484
  33.4 17.0 %collective-permute-start.11 = (f32[144,512]{1,0:T(8,128)S(1)}, f32[144,512]{1,0:T(8,128)S(1)}, u32[]{:S(2)}, u32[]{:S(2)}) collective-permute-start(f32[144,512]{1,0:T(8,128)S(1)} %get-tuple-element.71), channel_id=1, source_target_pairs={{0,16},{8,24},{16,0},{24,8},{1,17},{9,25},{17,1},{25,9},{2,18},{10... | collective-permute-start | bytes 884744 | tf_op jit(solution)/shard_map/ppermute | solution.py:484
  34.7 16.3 %collective-permute-start.12 = (f32[144,512]{1,0:T(8,128)S(1)}, f32[144,512]{1,0:T(8,128)S(1)}, u32[]{:S(2)}, u32[]{:S(2)}) collective-permute-start(f32[144,512]{1,0:T(8,128)S(1)} %get-tuple-element.72), channel_id=1, source_target_pairs={{0,24},{8,0},{16,8},{24,16},{1,25},{9,1},{17,9},{25,17},{2,26},{10... | collective-permute-start | bytes 884744 | tf_op jit(solution)/shard_map/ppermute | solution.py:484
  36.7 15.5 %collective-permute-start.7 = (f32[128,512]{1,0:T(8,128)S(1)}, f32[128,512]{1,0:T(8,128)S(1)}, u32[]{:S(2)}, u32[]{:S(2)}) collective-permute-start(f32[128,512]{1,0:T(8,128)S(1)} %collective-permute-done.5.refs_6_), channel_id=1, source_target_pairs={{0,32},{32,64},{64,96},{96,128},{128,160},{160,192},{192,224},{224... | collective-permute-start | bytes 786440 | tf_op jit(solution)/shard_map/ppermute | solution.py:468
  36.7 37.3 %copy-start.13 = (f32[128,512]{1,0:T(8,128)}, f32[128,512]{1,0:T(8,128)S(1)}, u32[]{:S(2)}) copy-start(f32[128,512]{1,0:T(8,128)S(1)} %collective-permute-done.9.e_in) | copy-start | bytes 786436
  36.7 15.5 %collective-permute-start.8 = (f32[128,512]{1,0:T(8,128)S(1)}, f32[128,512]{1,0:T(8,128)S(1)}, u32[]{:S(2)}, u32[]{:S(2)}) collective-permute-start(f32[128,512]{1,0:T(8,128)S(1)} %collective-permute-done.6.refs_5_), channel_id=1, source_target_pairs={{0,224},{32,0},{64,32},{96,64},{128,96},{160,128},{192,160},{224,1... | collective-permute-start | bytes 786440 | tf_op jit(solution)/shard_map/ppermute | solution.py:468
  41.6 19.6 %collective-permute-start.13 = (f32[96,512]{1,0:T(8,128)S(1)}, f32[96,512]{1,0:T(8,128)S(1)}, u32[]{:S(2)}, u32[]{:S(2)}) collective-permute-start(f32[96,512]{1,0:T(8,128)S(1)} %get-tuple-element.77), channel_id=1, source_target_pairs={{0,8},{8,16},{16,24},{24,0},{1,9},{9,17},{17,25},{25,1},{2,10},{10... | collective-permute-start | bytes 589832 | tf_op jit(solution)/shard_map/ppermute | solution.py:484
  50.3 12.5 %collective-permute-start.14 = (f32[96,512]{1,0:T(8,128)S(1)}, f32[96,512]{1,0:T(8,128)S(1)}, u32[]{:S(2)}, u32[]{:S(2)}) collective-permute-start(f32[96,512]{1,0:T(8,128)S(1)} %get-tuple-element.78), channel_id=1, source_target_pairs={{0,16},{8,24},{16,0},{24,8},{1,17},{9,25},{17,1},{25,9},{2,18},{10... | collective-permute-start | bytes 589832 | tf_op jit(solution)/shard_map/ppermute | solution.py:484
  51.0 11.9 %collective-permute-start.15 = (f32[96,512]{1,0:T(8,128)S(1)}, f32[96,512]{1,0:T(8,128)S(1)}, u32[]{:S(2)}, u32[]{:S(2)}) collective-permute-start(f32[96,512]{1,0:T(8,128)S(1)} %get-tuple-element.79), channel_id=1, source_target_pairs={{0,24},{8,0},{16,8},{24,16},{1,25},{9,1},{17,9},{25,17},{2,26},{10... | collective-permute-start | bytes 589832 | tf_op jit(solution)/shard_map/ppermute | solution.py:484
  52.2 4.3 %collective-permute-start.18 = (f32[64,512]{1,0:T(8,128)S(1)}, f32[64,512]{1,0:T(8,128)S(1)}, u32[]{:S(2)}, u32[]{:S(2)}) collective-permute-start(f32[64,512]{1,0:T(8,128)S(1)} %slice.7), channel_id=1, source_target_pairs={{0,224},{32,0},{64,32},{96,64},{128,96},{160,128},{192,160},{224,1... | collective-permute-start | bytes 393224 | tf_op jit(solution)/shard_map/ppermute | solution.py:468
  52.3 5.6 %collective-permute-start.17 = (f32[64,512]{1,0:T(8,128)S(1)}, f32[64,512]{1,0:T(8,128)S(1)}, u32[]{:S(2)}, u32[]{:S(2)}) collective-permute-start(f32[64,512]{1,0:T(8,128)S(1)} %slice.6), channel_id=1, source_target_pairs={{0,32},{32,64},{64,96},{96,128},{128,160},{160,192},{192,224},{224... | collective-permute-start | bytes 393224 | tf_op jit(solution)/shard_map/ppermute | solution.py:468
  58.6 13.3 %collective-permute-start.19 = (f32[144,512]{1,0:T(8,128)S(1)}, f32[144,512]{1,0:T(8,128)S(1)}, u32[]{:S(2)}, u32[]{:S(2)}) collective-permute-start(f32[144,512]{1,0:T(8,128)S(1)} %get-tuple-element.85), channel_id=1, source_target_pairs={{0,8},{8,16},{16,24},{24,0},{1,9},{9,17},{17,25},{25,1},{2,10},{10... | collective-permute-start | bytes 884744 | tf_op jit(solution)/shard_map/ppermute | solution.py:484
  59.1 12.8 %collective-permute-start.20 = (f32[144,512]{1,0:T(8,128)S(1)}, f32[144,512]{1,0:T(8,128)S(1)}, u32[]{:S(2)}, u32[]{:S(2)}) collective-permute-start(f32[144,512]{1,0:T(8,128)S(1)} %get-tuple-element.86), channel_id=1, source_target_pairs={{0,16},{8,24},{16,0},{24,8},{1,17},{9,25},{17,1},{25,9},{2,18},{10... | collective-permute-start | bytes 884744 | tf_op jit(solution)/shard_map/ppermute | solution.py:484
  61.2 10.7 %collective-permute-start.21 = (f32[144,512]{1,0:T(8,128)S(1)}, f32[144,512]{1,0:T(8,128)S(1)}, u32[]{:S(2)}, u32[]{:S(2)}) collective-permute-start(f32[144,512]{1,0:T(8,128)S(1)} %get-tuple-element.87), channel_id=1, source_target_pairs={{0,24},{8,0},{16,8},{24,16},{1,25},{9,1},{17,9},{25,17},{2,26},{10... | collective-permute-start | bytes 884744 | tf_op jit(solution)/shard_map/ppermute | solution.py:484
  62.9 9.0 %collective-permute-start.16 = (f32[128,512]{1,0:T(8,128)S(1)}, f32[128,512]{1,0:T(8,128)S(1)}, u32[]{:S(2)}, u32[]{:S(2)}) collective-permute-start(f32[128,512]{1,0:T(8,128)S(1)} %collective-permute-done.9.e_in), channel_id=1, source_target_pairs={{0,1},{1,0},{2,3},{3,2},{4,5},{5,4},{6,7},{7,6},{8,9},{9,8},{10,11... | collective-permute-start | bytes 786440 | tf_op jit(solution)/shard_map/ppermute | solution.py:471
  71.9 2.1 %copy-start.15 = (f32[128,512]{1,0:T(8,128)}, f32[128,512]{1,0:T(8,128)S(1)}, u32[]{:S(2)}) copy-start(f32[128,512]{1,0:T(8,128)S(1)} %collective-permute-done.16.e_other) | copy-start | bytes 786436
  74.0 16.7 %copy-start.12 = (s32[8,3]{0,1:T(4,128)S(1)}, s32[8,3]{0,1:T(4,128)}, u32[]{:S(2)}) copy-start(s32[8,3]{0,1:T(4,128)} %param.16) | copy-start | bytes 292
  74.0 37.5 %all-to-all-start = ((f32[8,96,512]{2,1,0:T(8,128)}), f32[8,96,512]{2,1,0:T(8,128)}, u32[]{:S(2)}, u32[]{:S(2)}) async-start(f32[8,96,512]{2,1,0:T(8,128)} %bitcast.10), calls=%async_computation | async-start | bytes 3145728 | tf_op jit(solution)/shard_map/all_to_all | solution.py:506
  106.1 5.4 %copy-start.2 = (s32[5]{0:T(128)S(1)}, s32[5]{0:T(128)}, u32[]{:S(2)}) copy-start(s32[5]{0:T(128)} %stack.23.pos.refs_0_) | copy-start | bytes 64
  106.1 5.4 %copy-start.5 = (s32[8,6]{1,0:T(8,128)S(1)}, s32[8,6]{1,0:T(8,128)}, u32[]{:S(2)}) copy-start(s32[8,6]{1,0:T(8,128)} %exp_ref.3) | copy-start | bytes 580
  106.1 5.3 %copy-start.7 = (s32[256]{0:T(256)S(1)}, s32[256]{0:T(256)}, u32[]{:S(2)}) copy-start(s32[256]{0:T(256)} %count_ref.3) | copy-start | bytes 3076
  106.1 5.3 %copy-start.8 = (bf16[2,4,128,512]{3,2,1,0:T(8,128)(2,1)S(1)}, bf16[2,4,128,512]{3,2,1,0:T(8,128)(2,1)}, u32[]{:S(2)}) copy-start(bf16[2,4,128,512]{3,2,1,0:T(8,128)(2,1)} %get-tuple-element.107.v_hbm) | copy-start | bytes 3145732
  106.1 5.3 %copy-start.9 = (bf16[2,512,512]{2,1,0:T(8,128)(2,1)S(1)}, bf16[2,512,512]{2,1,0:T(8,128)(2,1)}, u32[]{:S(2)}) copy-start(bf16[2,512,512]{2,1,0:T(8,128)(2,1)} %get-tuple-element.109.o_hbm) | copy-start | bytes 3145732
  106.1 5.3 %copy-start.10 = (f32[4,256,128]{2,1,0:T(8,128)S(1)}, f32[4,256,128]{2,1,0:T(8,128)}, u32[]{:S(2)}) copy-start(f32[4,256,128]{2,1,0:T(8,128)} %get-tuple-element.106.s_hbm) | copy-start | bytes 1572868
  106.1 5.3 %copy-start.11 = (f32[128,512]{1,0:T(8,128)S(1)}, f32[128,512]{1,0:T(8,128)}, u32[]{:S(2)}) copy-start(f32[128,512]{1,0:T(8,128)} %get-tuple-element.108.x_hbm) | copy-start | bytes 786436
  111.5 23.2 %copy-start.6 = (s32[1024]{0:T(1024)S(1)}, s32[1024]{0:T(1024)}, u32[]{:S(2)}) copy-start(s32[1024]{0:T(1024)} %param.14) | copy-start | bytes 12292
Sparse Core Ops, SparseCore 0:
  25.6 51.3 all-gather.1

commit v7 on v5

--- a/solution.py
+++ b/solution.py
@@ -484,13 +484,13 @@
         return [blocks[0]] + [lax.ppermute(blocks[k], "x", ring(NX, k)) for k in (1, 2, 3)]
 
     one = pick(GROUPS[0])
+    up, down = both_z(up, down)
+    held[6], held[2] = (up,), (down,)
+    up, down, edge, *_ = tie((up, down, edge, *one))
     e_in = lax.ppermute(edge, ("z", "x", "y", "c"), [
         (i * CD + h, (i + s) * CD + h)
         for s, hs in ((1, (0, 1)), (-1, (6, 7)))
         for i in range(NZ * NX) if 0 <= i + s < NZ * NX for h in hs])
-    up, down = both_z(up, down)
-    held[6], held[2] = (up,), (down,)
-    up, down, *_ = tie((up, down, *one))
     one = exchange(one)
     two = pick(GROUPS[1])
     up, down = both_z(up, down)

time: 142 us -> 139 us (0.979)
  starting transfers between devices: 51.6 us -> 47.6 us
    ppermute x4, starting transfers between devices: 13.5 us -> 18.6 us  [both_z(): lax.ppermute(b, 'z', ring(NZ, -1))]
    all_to_all x1, starting transfers between devices: 11.6 us -> 7.83 us  [shards(): xe = lax.all_to_all(sending, ('y', 'c'), 0, 0, tiled=True)]
    ppermute x4, waiting for transfers between devices: 2.6 us -> 5.21 us  [both_z(): lax.ppermute(a, 'z', ring(NZ, 1))]
    ppermute x1, starting transfers between devices: 6.91 us -> 4.51 us  [swap(): return [lax.ppermute(t, 'c', SWAP) for t in arrays]]
    ppermute x9, waiting for transfers between devices: 15 us -> 13.3 us  [exchange(): lax.ppermute(blocks[k], 'x', ring(NX, k))]
    ppermute x4, starting transfers between devices: 1.54 us -> 0.01 us  [both_z(): lax.ppermute(a, 'z', ring(NZ, 1))]
    ppermute x9, starting transfers between devices: 10.2 us -> 8.69 us  [exchange(): lax.ppermute(blocks[k], 'x', ring(NX, k))]
  transfers between devices with their start and end apart: 24 -> 24, of which waited for: 6 -> 8; matrix products, arithmetic and copies ran while one was open for 0% -> 0% of each run, Pallas kernels for 17% -> 17%
where the time goes in v7:
time: 139 us; the launch traced here: 138 us
  starting transfers between devices  47.6 us (34%)
  Pallas kernels  44 us (32%)
  waiting for transfers between devices  21.3 us (15%)
  between operations  13.7 us (10%)
  blocking collectives  10.3 us (7%)
    ppermute x4, starting transfers between devices, both_z(): lax.ppermute(b, 'z', ring(NZ, -1))  18.6 us
    pallas_call x1, Pallas kernels, near_call(): pl.pallas_call(near_kernel, out_shape=shapes, in_specs=[sspec()] * len(sc...  14.8 us
    ppermute x9, waiting for transfers between devices, exchange(): lax.ppermute(blocks[k], 'x', ring(NX, k))  13.3 us
    pallas_call x1, Pallas kernels, far_call(): pl.pallas_call(far_kernel, out_shape=sds(D, CL), in_specs=[sspec()] * len...  12.8 us
    all_to_all x1, blocking collectives, shards(): received = lax.all_to_all(result, ('y', 'c'), 0, 0, tiled=True)  10.3 us
    ppermute x9, starting transfers between devices, exchange(): lax.ppermute(blocks[k], 'x', ring(NX, k))  8.69 us
    all_to_all x1, starting transfers between devices, shards(): xe = lax.all_to_all(sending, ('y', 'c'), 0, 0, tiled=True)  7.83 us
    ppermute x4, waiting for transfers between devices, both_z(): lax.ppermute(a, 'z', ring(NZ, 1))  5.21 us
  transfers between devices with their start and end apart: 24, of which 8 were waited for; matrix products, arithmetic and copies ran while one was open for 0% of the time, Pallas kernels for 17%

profile of v7, /device:TPU:1, one launch (start us, length us, event | category | flops | bytes accessed | tf_op | source)
XLA Modules:
  0.0 138.3 jit_solution(13728954804820582500)
XLA Ops:
  6.5 0.6 stack.23.pos.refs_0_
  7.1 3.6 %first.1 = (f32[128,512]{1,0:T(8,128)}, f32[128,512]{1,0:T(8,128)}, s32[96]{0:T(128)}, s32[48]{0:T(128)}) custom-call(s32[5]{0:T(128)} %stack.23.pos.refs_0_, s32[8,6]{1,0:T(8,128)} %exp_ref.3, s32[8,128]{1,0:T(8,128)} %bitcast.18, f32[1024,512]{1,0:T(8,128)} %nodes_ref.1), custom_call_target="tpu_custom_call" | custom-call | flops 1000000000 | bytes 3145728 | tf_op jit(solution)/shard_map/first/pallas_call | solution.py:134
  10.7 0.0 copy-start
  10.7 6.5 %collective-permute-start.1 = (f32[128,512]{1,0:T(8,128)}, f32[128,512]{1,0:T(8,128)S(1)}, u32[]{:S(2)}, u32[]{:S(2)}) collective-permute-start(f32[128,512]{1,0:T(8,128)} %get-tuple-element.61.refs_5_), channel_id=1, source_target_pairs={{0,224},{32,0},{64,32},{96,64},{128,96},{160,128},{192,160},{224,1... | collective-permute-start | bytes 786440 | tf_op jit(solution)/shard_map/ppermute | solution.py:468
  17.2 1.2 collective-permute-start.4
  18.4 2.4 %collective-permute-start.3 = (s32[96]{0:T(128)}, s32[96]{0:T(128)S(1)}, u32[]{:S(2)}, u32[]{:S(2)}) collective-permute-start(s32[96]{0:T(128)} %get-tuple-element.67.refs_1_), channel_id=1, source_target_pairs={{0,16},{8,24},{16,0},{24,8},{1,17},{9,25},{17,1},{25,9},{2,18},{10... | collective-permute-start | bytes 1160 | tf_op jit(solution)/shard_map/ppermute | solution.py:475
  20.9 1.2 collective-permute-start.2
  22.0 2.3 %pack.1 = f32[512,512]{1,0:T(8,128)} custom-call(f32[64,512]{1,0:T(8,128)} %bitcast.23, f32[64,512]{1,0:T(8,128)} %bitcast.24, f32[64,512]{1,0:T(8,128)} %bitcast.25, f32[64,512]{1,0:T(8,128)} %bitcast.26, f32[512,128]{1,0:T(8,128)} %up.1, f32[128,512]{1,0:T(8,128)} %down.1), custom_call_target="tpu_custom_call" | custom-call | flops 1000 | bytes 2097152 | tf_op jit(solution)/shard_map/pack/pallas_call | solution.py:160
  24.3 0.0 collective-permute-done.3.refs_3_
  24.3 0.0 collective-permute-done.2.refs_2_
  24.4 1.1 collective-permute-done.refs_7_
  25.5 0.0 all-gather.2.cloned.1.call-update
  25.5 0.7 pick.3
  26.2 1.3 collective-permute-start.10
  27.5 2.7 %collective-permute-start.6 = (f32[128,512]{1,0:T(8,128)S(1)}, f32[128,512]{1,0:T(8,128)S(1)}, u32[]{:S(2)}, u32[]{:S(2)}) collective-permute-start(f32[128,512]{1,0:T(8,128)S(1)} %collective-permute-done.1.refs_6_), channel_id=1, source_target_pairs={{0,224},{32,0},{64,32},{96,64},{128,96},{160,128},{192,160},{224,1... | collective-permute-start | bytes 786440 | tf_op jit(solution)/shard_map/ppermute | solution.py:468
  30.2 2.4 %collective-permute-start.11 = (f32[144,512]{1,0:T(8,128)S(1)}, f32[144,512]{1,0:T(8,128)S(1)}, u32[]{:S(2)}, u32[]{:S(2)}) collective-permute-start(f32[144,512]{1,0:T(8,128)S(1)} %get-tuple-element.73), channel_id=1, source_target_pairs={{0,16},{8,24},{16,0},{24,8},{1,17},{9,25},{17,1},{25,9},{2,18},{10... | collective-permute-start | bytes 884744 | tf_op jit(solution)/shard_map/ppermute | solution.py:484
  32.6 1.2 collective-permute-start.12
  33.8 0.6 collective-permute-done.5.refs_6_
  34.4 2.7 %collective-permute-start.8 = (f32[128,512]{1,0:T(8,128)S(1)}, f32[128,512]{1,0:T(8,128)S(1)}, u32[]{:S(2)}, u32[]{:S(2)}) collective-permute-start(f32[128,512]{1,0:T(8,128)S(1)} %collective-permute-done.6.refs_5_), channel_id=1, source_target_pairs={{0,224},{32,0},{64,32},{96,64},{128,96},{160,128},{192,160},{224,1... | collective-permute-start | bytes 786440 | tf_op jit(solution)/shard_map/ppermute | solution.py:468
  37.1 3.1 %collective-permute-start.9 = (f32[128,512]{1,0:T(8,128)S(1)}, f32[128,512]{1,0:T(8,128)S(1)}, u32[]{:S(2)}, u32[]{:S(2)}) collective-permute-start(f32[128,512]{1,0:T(8,128)S(1)} %copy-done.14), channel_id=1, source_target_pairs={{0,8},{1,9},{8,16},{9,17},{16,24},{17,25},{24,32},{25,33},{32,40},... | collective-permute-start | bytes 786440 | tf_op jit(solution)/shard_map/ppermute | solution.py:490
  40.2 0.6 pick.4
  40.8 0.6 collective-permute-done.11.refs_2_
  41.4 0.4 collective-permute-start.16
  41.8 2.1 %collective-permute-done.12.refs_3_ = f32[144,512]{1,0:T(8,128)S(1)} collective-permute-done((f32[144,512]{1,0:T(8,128)S(1)}, f32[144,512]{1,0:T(8,128)S(1)}, u32[]{:S(2)}, u32[]{:S(2)}) %collective-permute-start.12) | collective-permute-done | bytes 294944 | tf_op jit(solution)/shard_map/ppermute | solution.py:484
  43.9 0.0 copy-start.13
  44.0 6.8 %collective-permute-start.14 = (f32[64,512]{1,0:T(8,128)S(1)}, f32[64,512]{1,0:T(8,128)S(1)}, u32[]{:S(2)}, u32[]{:S(2)}) collective-permute-start(f32[64,512]{1,0:T(8,128)S(1)} %slice.7), channel_id=1, source_target_pairs={{0,224},{32,0},{64,32},{96,64},{128,96},{160,128},{192,160},{224,1... | collective-permute-start | bytes 393224 | tf_op jit(solution)/shard_map/ppermute | solution.py:468
  50.8 0.0 collective-permute-start.13
  50.8 1.9 %collective-permute-done.14.refs_8_ = f32[64,512]{1,0:T(8,128)S(1)} collective-permute-done((f32[64,512]{1,0:T(8,128)S(1)}, f32[64,512]{1,0:T(8,128)S(1)}, u32[]{:S(2)}, u32[]{:S(2)}) %collective-permute-start.14) | collective-permute-done | bytes 131104 | tf_op jit(solution)/shard_map/ppermute | solution.py:468
  52.7 3.5 %collective-permute-done.13.refs_7_ = f32[64,512]{1,0:T(8,128)S(1)} collective-permute-done((f32[64,512]{1,0:T(8,128)S(1)}, f32[64,512]{1,0:T(8,128)S(1)}, u32[]{:S(2)}, u32[]{:S(2)}) %collective-permute-start.13) | collective-permute-done | bytes 131104 | tf_op jit(solution)/shard_map/ppermute | solution.py:468
  56.2 0.7 pick.5
  56.9 0.1 collective-permute-start.19
  57.0 0.1 collective-permute-start.20
  57.1 2.6 %collective-permute-start.21 = (f32[144,512]{1,0:T(8,128)S(1)}, f32[144,512]{1,0:T(8,128)S(1)}, u32[]{:S(2)}, u32[]{:S(2)}) collective-permute-start(f32[144,512]{1,0:T(8,128)S(1)} %get-tuple-element.88), channel_id=1, source_target_pairs={{0,24},{8,0},{16,8},{24,16},{1,25},{9,1},{17,9},{25,17},{2,26},{10... | collective-permute-start | bytes 884744 | tf_op jit(solution)/shard_map/ppermute | solution.py:484
  59.7 4.5 %collective-permute-start.15 = (f32[128,512]{1,0:T(8,128)S(1)}, f32[128,512]{1,0:T(8,128)S(1)}, u32[]{:S(2)}, u32[]{:S(2)}) collective-permute-start(f32[128,512]{1,0:T(8,128)S(1)} %collective-permute-done.9.e_in), channel_id=1, source_target_pairs={{0,1},{1,0},{2,3},{3,2},{4,5},{5,4},{6,7},{7,6},{8,9},{9,8},{10,11... | collective-permute-start | bytes 786440 | tf_op jit(solution)/shard_map/ppermute | solution.py:471
  64.2 0.7 collective-permute-start.18
  64.9 10.6 %collective-permute-done.18.refs_7_ = f32[96,512]{1,0:T(8,128)S(1)} collective-permute-done((f32[96,512]{1,0:T(8,128)S(1)}, f32[96,512]{1,0:T(8,128)S(1)}, u32[]{:S(2)}, u32[]{:S(2)}) %collective-permute-start.18) | collective-permute-done | bytes 196640 | tf_op jit(solution)/shard_map/ppermute | solution.py:484
  75.5 2.0 %send.1 = f32[768,512]{1,0:T(8,128)} custom-call(s32[48]{0:T(128)S(1)} %copy-done.4, f32[144,512]{1,0:T(8,128)S(1)} %get-tuple-element.90.refs_0_, f32[144,512]{1,0:T(8,128)S(1)} %collective-permute-done.10.refs_1_, f32[144,512]{1,0:T(8,128)S(1)} %collective-permute-done.11.refs_2_, f32[144,512]{1,0:T(8,128)S(1)} %collective-permute-done.12.refs_3_, ...), custom_call_target="tpu_custom_call" | custom-call | bytes 6291456 | tf_op jit(solution)/shard_map/send/pallas_call | solution.py:436
  77.5 7.8 %all-to-all-start = ((f32[8,96,512]{2,1,0:T(8,128)}), f32[8,96,512]{2,1,0:T(8,128)}, u32[]{:S(2)}, u32[]{:S(2)}) async-start(f32[8,96,512]{2,1,0:T(8,128)} %bitcast.10), calls=%async_computation | async-start | bytes 3145728 | tf_op jit(solution)/shard_map/all_to_all | solution.py:505
  85.3 0.7 copy.14.local_ref
  86.0 14.8 %near.1 = (f32[128,512]{1,0:T(8,128)}, bf16[2,4,256,512]{3,2,1,0:T(8,128)(2,1)}, bf16[2,4,128,512]{3,2,1,0:T(8,128)(2,1)}, bf16[2,512,512]{2,1,0:T(8,128)(2,1)}, f32[4,256,128]{2,1,0:T(8,128)}) custom-call(s32[5]{0:T(128)} %stack.23.pos.refs_0_, s32[8,3]{1,0:T(8,128)} %copy.14.local_ref, s32[8]{0:T(128)} %virt_ref.1, s32[256]{0:T(256)} %count_ref.3, ...), custom_call_target="tpu_custom_call" | custom-call | flops 6000000000 | bytes 16777216 | tf_op jit(solution)/shard_map/near/pallas_call | solution.py:239
  100.8 0.0 copy-start.5
  100.8 0.0 copy-start.7
  100.9 4.5 %prep.1 = (bf16[2,512,1024]{2,1,0:T(8,128)(2,1)}, bf16[2,1024,512]{2,1,0:T(8,128)(2,1)}) custom-call(f32[8,512,512]{2,1,0:T(8,128)} %bitcast.22), custom_call_target="tpu_custom_call" | custom-call | flops 10000000 | bytes 8388608 | tf_op jit(solution)/shard_map/prep/pallas_call | solution.py:268
  105.3 0.8 all-to-all-done
  106.2 0.0 copy-start.6
  106.2 12.8 %far.1 = f32[512,128]{1,0:T(8,128)S(1)} custom-call(s32[5]{0:T(128)S(1)} %copy-done.2, s32[8,6]{1,0:T(8,128)S(1)} %copy-done.5, s32[256]{0:T(256)S(1)} %copy-done.7, f32[768,512]{1,0:T(8,128)} %bitcast.11.xe_ref, bf16[2,4,256,512]{3,2,1,0:T(8,128)(2,1)} %get-tuple-element.106.q_hbm, f32[4,256,128]{2,1,0:T(8,128)S(1)} %copy-done.10, ...), custom_call_target="tpu_custom_call" | custom-call | flops 6000000000 | bytes 16777216 | tf_op jit(solution)/shard_map/far/pallas_call | solution.py:349
  119.0 10.3 %all_to_all.22 = f32[8,64,128]{2,1,0:T(8,128)S(1)} all-to-all(f32[8,64,128]{2,1,0:T(8,128)S(1)} %bitcast.16), channel_id=1, replica_groups=mesh['z'=8,'x'=4,'y'=4,'c'=2] {'y','c'}, dimensions={0} | all-to-all | bytes 524288 | tf_op jit(solution)/shard_map/all_to_all | solution.py:513
  129.3 2.1 %place.1 = f32[64,1024]{1,0:T(8,128)} custom-call(s32[5]{0:T(128)S(1)} %copy-done.2, f32[512,128]{1,0:T(8,128)S(1)} %bitcast.17, s32[8,128]{1,0:T(8,128)S(1)} %bitcast.20), custom_call_target="tpu_custom_call" | custom-call | flops 400000000 | bytes 1048576 | tf_op jit(solution)/shard_map/place/pallas_call | solution.py:379
  (48 shorter events, 0.1 us)
Async XLA Ops:
  6.5 79.5 %all-gather.2.cloned.1.call-start = ((), (), s32[]{:S(2)}) async-start(), calls=%async_computation.2 | async-start | bytes 9437184 | tf_op jit(solution)/shard_map/all_gather | solution.py:478
  10.7 14.8 %copy-start = (f32[128,512]{1,0:T(8,128)S(1)}, f32[128,512]{1,0:T(8,128)}, u32[]{:S(2)}) copy-start(f32[128,512]{1,0:T(8,128)} %get-tuple-element.61.refs_5_) | copy-start | bytes 786436
  10.7 14.8 %copy-start.1 = (s32[5]{0:T(128)S(1)}, s32[5]{0:T(128)}, u32[]{:S(2)}) copy-start(s32[5]{0:T(128)} %stack.23.pos.refs_0_) | copy-start | bytes 64
  10.7 14.8 %copy-start.3 = (s32[96]{0:T(128)S(1)}, s32[96]{0:T(128)}, u32[]{:S(2)}) copy-start(s32[96]{0:T(128)} %get-tuple-element.67.refs_1_) | copy-start | bytes 1156
  10.7 26.4 %copy-start.14 = (f32[128,512]{1,0:T(8,128)S(1)}, f32[128,512]{1,0:T(8,128)}, u32[]{:S(2)}) copy-start(f32[128,512]{1,0:T(8,128)} %get-tuple-element.77) | copy-start | bytes 786436
  10.7 13.6 %collective-permute-start.1 = (f32[128,512]{1,0:T(8,128)}, f32[128,512]{1,0:T(8,128)S(1)}, u32[]{:S(2)}, u32[]{:S(2)}) collective-permute-start(f32[128,512]{1,0:T(8,128)} %get-tuple-element.61.refs_5_), channel_id=1, source_target_pairs={{0,224},{32,0},{64,32},{96,64},{128,96},{160,128},{192,160},{224,1... | collective-permute-start | bytes 786440 | tf_op jit(solution)/shard_map/ppermute | solution.py:468
  17.2 8.3 %collective-permute-start = (f32[128,512]{1,0:T(8,128)}, f32[128,512]{1,0:T(8,128)S(1)}, u32[]{:S(2)}, u32[]{:S(2)}) collective-permute-start(f32[128,512]{1,0:T(8,128)} %get-tuple-element.61.refs_5_), channel_id=1, source_target_pairs={{0,32},{32,64},{64,96},{96,128},{128,160},{160,192},{192,224},{224... | collective-permute-start | bytes 786440 | tf_op jit(solution)/shard_map/ppermute | solution.py:468
  17.2 7.1 %collective-permute-start.4 = (s32[96]{0:T(128)}, s32[96]{0:T(128)S(1)}, u32[]{:S(2)}, u32[]{:S(2)}) collective-permute-start(s32[96]{0:T(128)} %get-tuple-element.67.refs_1_), channel_id=1, source_target_pairs={{0,8},{8,16},{16,24},{24,0},{1,9},{9,17},{17,25},{25,1},{2,10},{10... | collective-permute-start | bytes 1160 | tf_op jit(solution)/shard_map/ppermute | solution.py:475
  18.4 5.9 %collective-permute-start.3 = (s32[96]{0:T(128)}, s32[96]{0:T(128)S(1)}, u32[]{:S(2)}, u32[]{:S(2)}) collective-permute-start(s32[96]{0:T(128)} %get-tuple-element.67.refs_1_), channel_id=1, source_target_pairs={{0,16},{8,24},{16,0},{24,8},{1,17},{9,25},{17,1},{25,9},{2,18},{10... | collective-permute-start | bytes 1160 | tf_op jit(solution)/shard_map/ppermute | solution.py:475
  20.9 3.5 %collective-permute-start.2 = (s32[96]{0:T(128)}, s32[96]{0:T(128)S(1)}, u32[]{:S(2)}, u32[]{:S(2)}) collective-permute-start(s32[96]{0:T(128)} %get-tuple-element.67.refs_1_), channel_id=1, source_target_pairs={{0,24},{8,0},{16,8},{24,16},{1,25},{9,1},{17,9},{25,17},{2,26},{10... | collective-permute-start | bytes 1160 | tf_op jit(solution)/shard_map/ppermute | solution.py:475
  24.3 51.1 %copy-start.4 = (s32[48]{0:T(128)S(1)}, s32[48]{0:T(128)}, u32[]{:S(2)}) copy-start(s32[48]{0:T(128)} %get-tuple-element.60.row) | copy-start | bytes 580
  26.2 10.9 %collective-permute-start.10 = (f32[144,512]{1,0:T(8,128)S(1)}, f32[144,512]{1,0:T(8,128)S(1)}, u32[]{:S(2)}, u32[]{:S(2)}) collective-permute-start(f32[144,512]{1,0:T(8,128)S(1)} %get-tuple-element.72), channel_id=1, source_target_pairs={{0,8},{8,16},{16,24},{24,0},{1,9},{9,17},{17,25},{25,1},{2,10},{10... | collective-permute-start | bytes 884744 | tf_op jit(solution)/shard_map/ppermute | solution.py:484
  27.5 6.9 %collective-permute-start.5 = (f32[128,512]{1,0:T(8,128)S(1)}, f32[128,512]{1,0:T(8,128)S(1)}, u32[]{:S(2)}, u32[]{:S(2)}) collective-permute-start(f32[128,512]{1,0:T(8,128)S(1)} %collective-permute-done.refs_7_), channel_id=1, source_target_pairs={{0,32},{32,64},{64,96},{96,128},{128,160},{160,192},{192,224},{224... | collective-permute-start | bytes 786440 | tf_op jit(solution)/shard_map/ppermute | solution.py:468
  27.5 6.9 %collective-permute-start.6 = (f32[128,512]{1,0:T(8,128)S(1)}, f32[128,512]{1,0:T(8,128)S(1)}, u32[]{:S(2)}, u32[]{:S(2)}) collective-permute-start(f32[128,512]{1,0:T(8,128)S(1)} %collective-permute-done.1.refs_6_), channel_id=1, source_target_pairs={{0,224},{32,0},{64,32},{96,64},{128,96},{160,128},{192,160},{224,1... | collective-permute-start | bytes 786440 | tf_op jit(solution)/shard_map/ppermute | solution.py:468
  30.2 11.2 %collective-permute-start.11 = (f32[144,512]{1,0:T(8,128)S(1)}, f32[144,512]{1,0:T(8,128)S(1)}, u32[]{:S(2)}, u32[]{:S(2)}) collective-permute-start(f32[144,512]{1,0:T(8,128)S(1)} %get-tuple-element.73), channel_id=1, source_target_pairs={{0,16},{8,24},{16,0},{24,8},{1,17},{9,25},{17,1},{25,9},{2,18},{10... | collective-permute-start | bytes 884744 | tf_op jit(solution)/shard_map/ppermute | solution.py:484
  32.6 11.3 %collective-permute-start.12 = (f32[144,512]{1,0:T(8,128)S(1)}, f32[144,512]{1,0:T(8,128)S(1)}, u32[]{:S(2)}, u32[]{:S(2)}) collective-permute-start(f32[144,512]{1,0:T(8,128)S(1)} %get-tuple-element.74), channel_id=1, source_target_pairs={{0,24},{8,0},{16,8},{24,16},{1,25},{9,1},{17,9},{25,17},{2,26},{10... | collective-permute-start | bytes 884744 | tf_op jit(solution)/shard_map/ppermute | solution.py:484
  34.4 9.5 %collective-permute-start.7 = (f32[128,512]{1,0:T(8,128)S(1)}, f32[128,512]{1,0:T(8,128)S(1)}, u32[]{:S(2)}, u32[]{:S(2)}) collective-permute-start(f32[128,512]{1,0:T(8,128)S(1)} %collective-permute-done.5.refs_6_), channel_id=1, source_target_pairs={{0,32},{32,64},{64,96},{96,128},{128,160},{160,192},{192,224},{224... | collective-permute-start | bytes 786440 | tf_op jit(solution)/shard_map/ppermute | solution.py:468
  34.4 9.5 %collective-permute-start.8 = (f32[128,512]{1,0:T(8,128)S(1)}, f32[128,512]{1,0:T(8,128)S(1)}, u32[]{:S(2)}, u32[]{:S(2)}) collective-permute-start(f32[128,512]{1,0:T(8,128)S(1)} %collective-permute-done.6.refs_5_), channel_id=1, source_target_pairs={{0,224},{32,0},{64,32},{96,64},{128,96},{160,128},{192,160},{224,1... | collective-permute-start | bytes 786440 | tf_op jit(solution)/shard_map/ppermute | solution.py:468
  37.1 6.8 %collective-permute-start.9 = (f32[128,512]{1,0:T(8,128)S(1)}, f32[128,512]{1,0:T(8,128)S(1)}, u32[]{:S(2)}, u32[]{:S(2)}) collective-permute-start(f32[128,512]{1,0:T(8,128)S(1)} %copy-done.14), channel_id=1, source_target_pairs={{0,8},{1,9},{8,16},{9,17},{16,24},{17,25},{24,32},{25,33},{32,40},... | collective-permute-start | bytes 786440 | tf_op jit(solution)/shard_map/ppermute | solution.py:490
  41.4 18.2 %collective-permute-start.16 = (f32[96,512]{1,0:T(8,128)S(1)}, f32[96,512]{1,0:T(8,128)S(1)}, u32[]{:S(2)}, u32[]{:S(2)}) collective-permute-start(f32[96,512]{1,0:T(8,128)S(1)} %get-tuple-element.79), channel_id=1, source_target_pairs={{0,8},{8,16},{16,24},{24,0},{1,9},{9,17},{17,25},{25,1},{2,10},{10... | collective-permute-start | bytes 589832 | tf_op jit(solution)/shard_map/ppermute | solution.py:484
  43.9 33.6 %copy-start.13 = (f32[128,512]{1,0:T(8,128)}, f32[128,512]{1,0:T(8,128)S(1)}, u32[]{:S(2)}) copy-start(f32[128,512]{1,0:T(8,128)S(1)} %collective-permute-done.9.e_in) | copy-start | bytes 786436
  44.0 8.8 %collective-permute-start.14 = (f32[64,512]{1,0:T(8,128)S(1)}, f32[64,512]{1,0:T(8,128)S(1)}, u32[]{:S(2)}, u32[]{:S(2)}) collective-permute-start(f32[64,512]{1,0:T(8,128)S(1)} %slice.7), channel_id=1, source_target_pairs={{0,224},{32,0},{64,32},{96,64},{128,96},{160,128},{192,160},{224,1... | collective-permute-start | bytes 393224 | tf_op jit(solution)/shard_map/ppermute | solution.py:468
  50.8 5.4 %collective-permute-start.13 = (f32[64,512]{1,0:T(8,128)S(1)}, f32[64,512]{1,0:T(8,128)S(1)}, u32[]{:S(2)}, u32[]{:S(2)}) collective-permute-start(f32[64,512]{1,0:T(8,128)S(1)} %slice.6), channel_id=1, source_target_pairs={{0,32},{32,64},{64,96},{96,128},{128,160},{160,192},{192,224},{224... | collective-permute-start | bytes 393224 | tf_op jit(solution)/shard_map/ppermute | solution.py:468
  50.8 13.4 %collective-permute-start.17 = (f32[96,512]{1,0:T(8,128)S(1)}, f32[96,512]{1,0:T(8,128)S(1)}, u32[]{:S(2)}, u32[]{:S(2)}) collective-permute-start(f32[96,512]{1,0:T(8,128)S(1)} %get-tuple-element.80), channel_id=1, source_target_pairs={{0,16},{8,24},{16,0},{24,8},{1,17},{9,25},{17,1},{25,9},{2,18},{10... | collective-permute-start | bytes 589832 | tf_op jit(solution)/shard_map/ppermute | solution.py:484
  56.9 18.5 %collective-permute-start.19 = (f32[144,512]{1,0:T(8,128)S(1)}, f32[144,512]{1,0:T(8,128)S(1)}, u32[]{:S(2)}, u32[]{:S(2)}) collective-permute-start(f32[144,512]{1,0:T(8,128)S(1)} %get-tuple-element.86), channel_id=1, source_target_pairs={{0,8},{8,16},{16,24},{24,0},{1,9},{9,17},{17,25},{25,1},{2,10},{10... | collective-permute-start | bytes 884744 | tf_op jit(solution)/shard_map/ppermute | solution.py:484
  57.0 18.4 %collective-permute-start.20 = (f32[144,512]{1,0:T(8,128)S(1)}, f32[144,512]{1,0:T(8,128)S(1)}, u32[]{:S(2)}, u32[]{:S(2)}) collective-permute-start(f32[144,512]{1,0:T(8,128)S(1)} %get-tuple-element.87), channel_id=1, source_target_pairs={{0,16},{8,24},{16,0},{24,8},{1,17},{9,25},{17,1},{25,9},{2,18},{10... | collective-permute-start | bytes 884744 | tf_op jit(solution)/shard_map/ppermute | solution.py:484
  57.1 18.3 %collective-permute-start.21 = (f32[144,512]{1,0:T(8,128)S(1)}, f32[144,512]{1,0:T(8,128)S(1)}, u32[]{:S(2)}, u32[]{:S(2)}) collective-permute-start(f32[144,512]{1,0:T(8,128)S(1)} %get-tuple-element.88), channel_id=1, source_target_pairs={{0,24},{8,0},{16,8},{24,16},{1,25},{9,1},{17,9},{25,17},{2,26},{10... | collective-permute-start | bytes 884744 | tf_op jit(solution)/shard_map/ppermute | solution.py:484
  59.7 15.8 %collective-permute-start.15 = (f32[128,512]{1,0:T(8,128)S(1)}, f32[128,512]{1,0:T(8,128)S(1)}, u32[]{:S(2)}, u32[]{:S(2)}) collective-permute-start(f32[128,512]{1,0:T(8,128)S(1)} %collective-permute-done.9.e_in), channel_id=1, source_target_pairs={{0,1},{1,0},{2,3},{3,2},{4,5},{5,4},{6,7},{7,6},{8,9},{9,8},{10,11... | collective-permute-start | bytes 786440 | tf_op jit(solution)/shard_map/ppermute | solution.py:471
  64.2 11.2 %collective-permute-start.18 = (f32[96,512]{1,0:T(8,128)S(1)}, f32[96,512]{1,0:T(8,128)S(1)}, u32[]{:S(2)}, u32[]{:S(2)}) collective-permute-start(f32[96,512]{1,0:T(8,128)S(1)} %get-tuple-element.81), channel_id=1, source_target_pairs={{0,24},{8,0},{16,8},{24,16},{1,25},{9,1},{17,9},{25,17},{2,26},{10... | collective-permute-start | bytes 589832 | tf_op jit(solution)/shard_map/ppermute | solution.py:484
  75.4 2.1 %copy-start.15 = (f32[128,512]{1,0:T(8,128)}, f32[128,512]{1,0:T(8,128)S(1)}, u32[]{:S(2)}) copy-start(f32[128,512]{1,0:T(8,128)S(1)} %collective-permute-done.15.e_other) | copy-start | bytes 786436
  77.5 7.8 %copy-start.12 = (s32[8,3]{0,1:T(4,128)S(1)}, s32[8,3]{0,1:T(4,128)}, u32[]{:S(2)}) copy-start(s32[8,3]{0,1:T(4,128)} %param.16) | copy-start | bytes 292
  77.5 28.6 %all-to-all-start = ((f32[8,96,512]{2,1,0:T(8,128)}), f32[8,96,512]{2,1,0:T(8,128)}, u32[]{:S(2)}, u32[]{:S(2)}) async-start(f32[8,96,512]{2,1,0:T(8,128)} %bitcast.10), calls=%async_computation | async-start | bytes 3145728 | tf_op jit(solution)/shard_map/all_to_all | solution.py:505
  100.8 5.4 %copy-start.2 = (s32[5]{0:T(128)S(1)}, s32[5]{0:T(128)}, u32[]{:S(2)}) copy-start(s32[5]{0:T(128)} %stack.23.pos.refs_0_) | copy-start | bytes 64
  100.8 5.4 %copy-start.5 = (s32[8,6]{1,0:T(8,128)S(1)}, s32[8,6]{1,0:T(8,128)}, u32[]{:S(2)}) copy-start(s32[8,6]{1,0:T(8,128)} %exp_ref.3) | copy-start | bytes 580
  100.8 5.3 %copy-start.7 = (s32[256]{0:T(256)S(1)}, s32[256]{0:T(256)}, u32[]{:S(2)}) copy-start(s32[256]{0:T(256)} %count_ref.3) | copy-start | bytes 3076
  100.8 5.3 %copy-start.8 = (bf16[2,4,128,512]{3,2,1,0:T(8,128)(2,1)S(1)}, bf16[2,4,128,512]{3,2,1,0:T(8,128)(2,1)}, u32[]{:S(2)}) copy-start(bf16[2,4,128,512]{3,2,1,0:T(8,128)(2,1)} %get-tuple-element.109.v_hbm) | copy-start | bytes 3145732
  100.8 5.3 %copy-start.9 = (bf16[2,512,512]{2,1,0:T(8,128)(2,1)S(1)}, bf16[2,512,512]{2,1,0:T(8,128)(2,1)}, u32[]{:S(2)}) copy-start(bf16[2,512,512]{2,1,0:T(8,128)(2,1)} %get-tuple-element.111.o_hbm) | copy-start | bytes 3145732
  100.8 5.3 %copy-start.10 = (f32[4,256,128]{2,1,0:T(8,128)S(1)}, f32[4,256,128]{2,1,0:T(8,128)}, u32[]{:S(2)}) copy-start(f32[4,256,128]{2,1,0:T(8,128)} %get-tuple-element.108.s_hbm) | copy-start | bytes 1572868
  100.8 5.3 %copy-start.11 = (f32[128,512]{1,0:T(8,128)S(1)}, f32[128,512]{1,0:T(8,128)}, u32[]{:S(2)}) copy-start(f32[128,512]{1,0:T(8,128)} %get-tuple-element.110.x_hbm) | copy-start | bytes 786436
  106.2 23.1 %copy-start.6 = (s32[1024]{0:T(1024)S(1)}, s32[1024]{0:T(1024)}, u32[]{:S(2)}) copy-start(s32[1024]{0:T(1024)} %param.14) | copy-start | bytes 12292
Sparse Core Ops, SparseCore 0:
  25.6 51.3 all-gather.1
